TPU v7x, 256 devices: a whole 4x4x8 slice. The times are simulated.
256 devices in a mesh: dp: 8 (over x_hi, y), tm: 4 (over x_lo, core), height: 8 (over z).
Axes of the slice: x: 4 (x_hi: 2, x_lo: 2; x = x_hi * 2 + x_lo), y: 4, z: 8, core: 2. Of those that a mesh axis runs over, the one named last changes fastest.
Arguments:
- queries: bfloat16 [8, 16, 32, 8, 2560], P('dp', 'tm', 'height'), may hold values from -9 to 9
- keys: bfloat16 [8, 16, 32, 8, 2560], P('dp', 'tm', 'height'), may hold values from -9 to 9
- values: bfloat16 [8, 16, 32, 8, 2560], P('dp', 'tm', 'height'), may hold values from -6 to 6
- projection: bfloat16 [2560, 2560], P('dp'), may hold values from -0.125 to 0.125
- d_outputs: bfloat16 [8, 16, 32, 8, 2560], P('dp', 'tm', 'height'), may hold values from -6 to 6
Outputs:
- outputs: bfloat16 [8, 16, 32, 8, 2560], P('dp', 'tm', 'height')
- d_queries: bfloat16 [8, 16, 32, 8, 2560], P('dp', 'tm', 'height')
- d_keys: bfloat16 [8, 16, 32, 8, 2560], P('dp', 'tm', 'height')
- d_values: bfloat16 [8, 16, 32, 8, 2560], P('dp', 'tm', 'height')
All inputs are finite; a program needn't handle non-finite values.
Results may differ from a plain program's by a relative error of at most 0.01.
Values may be sent and summed in bfloat16 or wider, within the bound.
No kernel may reach another device: no remote copies, remote signals or barrier semaphores. Data moves between devices by JAX's collectives and lax.ppermute only.
A program may use at most 128 MiB of HBM per device.

v0:
```python
import math

import jax
import jax.numpy as jnp
from jax import lax
from jax.sharding import PartitionSpec as P

HEADS = 20
HDIM = 128
TWIDE = 4
TILES_W = 2


head_groups = 4


def extended_2(cells, sides, width):
    for axis, dim in sides:
        count = lax.axis_size(axis)
        ends = count - 1
        head = lax.slice_in_dim(cells, 0, width, axis=dim)
        tail = lax.slice_in_dim(cells, cells.shape[dim] - width, cells.shape[dim], axis=dim)
        cells = jnp.concatenate(
            [
                lax.ppermute(tail, axis, [(i, (i + 1) % count) for i in range(ends)]),
                cells,
                lax.ppermute(head, axis, [((i + 1) % count, i) for i in range(ends)]),
            ],
            axis=dim,
        )
    return cells


def window_mask(
    frame_block, row_block, frame_blocks, row_blocks, tiles_across, tile_len, tile_cols
):
    grid_shape = (2, 2, tiles_across, 4, 4, tiles_across)
    query_frame = lax.broadcasted_iota(jnp.int32, grid_shape, 0)
    query_row = lax.broadcasted_iota(jnp.int32, grid_shape, 1)
    query_column = lax.broadcasted_iota(jnp.int32, grid_shape, 2)
    key_frame = lax.broadcasted_iota(jnp.int32, grid_shape, 3)
    key_row = lax.broadcasted_iota(jnp.int32, grid_shape, 4)
    key_column = lax.broadcasted_iota(jnp.int32, grid_shape, 5)
    frame_step = key_frame - query_frame - 1
    row_step = key_row - query_row - 1
    column_step = key_column - query_column
    frame_tile = 2 * frame_block + key_frame - 1
    row_tile = 2 * row_block + key_row - 1
    inside = (jnp.abs(frame_step) <= 1) & (jnp.abs(row_step) <= 1) & (jnp.abs(column_step) <= 1)
    inside = inside & (frame_tile >= 0) & (frame_tile < 2 * frame_blocks)
    inside = inside & (row_tile >= 0) & (row_tile < 2 * row_blocks)
    spread = inside[:, None, :, None, :, None, :, None, :, None, :, None]
    spread = jnp.broadcast_to(
        spread,
        (
            2,
            tile_len,
            2,
            tile_len,
            tiles_across,
            tile_cols,
            4,
            tile_len,
            4,
            tile_len,
            tiles_across,
            tile_cols,
        ),
    )
    query_count = 4 * tile_len * tile_len * tiles_across * tile_cols
    return spread.reshape(query_count, 4 * query_count)


def split_heads(matrix, group_index, group_width, head_count):
    piece = lax.dynamic_slice_in_dim(matrix, group_index * group_width, group_width, 1)
    return piece.reshape(matrix.shape[0], head_count, group_width // head_count)


def join_groups(stacked):
    return jnp.transpose(stacked, (1, 0, 2)).reshape(
        stacked.shape[1], stacked.shape[0] * stacked.shape[2]
    )


def body(queries, keys, values, projection, d_outputs):
    full_weight = lax.all_gather(projection, "dp", axis=0, tiled=True)
    tile_len = queries.shape[1] // 2
    key_value = jnp.stack((keys[0], values[0]))
    extended = extended_2(key_value, (("tm", 1), ("height", 2)), tile_len)
    query_count = queries.shape[1] * queries.shape[2] * queries.shape[3]
    model_dim = queries.shape[4]
    key_count = 4 * query_count
    query_flat = queries.reshape(query_count, model_dim)
    key_flat = extended[0].reshape(key_count, model_dim)
    value_flat = extended[1].reshape(key_count, model_dim)
    window = window_mask(
        lax.axis_index("tm"),
        lax.axis_index("height"),
        lax.axis_size("tm"),
        lax.axis_size("height"),
        TILES_W,
        tile_len,
        TWIDE,
    )
    group_width = model_dim // head_groups
    group_heads = HEADS // head_groups
    scaling = 1.0 / math.sqrt(HDIM)

    def forward_group(group_index):
        query_heads = split_heads(query_flat, group_index, group_width, group_heads)
        key_heads = split_heads(key_flat, group_index, group_width, group_heads)
        value_heads = split_heads(value_flat, group_index, group_width, group_heads)
        scores = (
            jnp.einsum("qhd,khd->hqk", query_heads, key_heads, preferred_element_type=jnp.float32)
            * scaling
        )
        masked = jnp.where(window[None], scores, -jnp.inf)
        largest = jnp.max(masked, axis=2, keepdims=True)
        weights = jnp.exp(masked - largest)
        soft_weights = (weights / jnp.sum(weights, axis=2, keepdims=True)).astype(jnp.bfloat16)
        attended = jnp.einsum(
            "hqk,khd->qhd", soft_weights, value_heads, preferred_element_type=jnp.float32
        )
        return (attended.reshape(query_count, group_width).astype(jnp.bfloat16), soft_weights)

    group_ids = jnp.arange(head_groups, dtype=jnp.int32)
    attended_groups, weight_groups = lax.map(forward_group, group_ids)
    attended = join_groups(attended_groups)
    outputs = jnp.dot(attended, full_weight, preferred_element_type=jnp.float32).astype(
        jnp.bfloat16
    )
    cotangent = d_outputs.reshape(query_count, d_outputs.shape[4])
    grad_attended = lax.dot_general(
        cotangent, full_weight, (((1,), (1,)), ((), ())), preferred_element_type=jnp.float32
    ).astype(jnp.bfloat16)

    def backward_group(group_items):
        group_index, soft_weights = group_items
        query_heads = split_heads(query_flat, group_index, group_width, group_heads)
        key_heads = split_heads(key_flat, group_index, group_width, group_heads)
        value_heads = split_heads(value_flat, group_index, group_width, group_heads)
        grad_heads = split_heads(grad_attended, group_index, group_width, group_heads)
        weights_wide = soft_weights.astype(jnp.float32)
        grad_weights = jnp.einsum(
            "qhd,khd->hqk", grad_heads, value_heads, preferred_element_type=jnp.float32
        )
        row_dot = jnp.sum(weights_wide * grad_weights, axis=2, keepdims=True)
        grad_scores = (weights_wide * (grad_weights - row_dot) * scaling).astype(jnp.bfloat16)
        grad_query = jnp.einsum(
            "hqk,khd->qhd", grad_scores, key_heads, preferred_element_type=jnp.float32
        )
        grad_key = jnp.einsum(
            "hqk,qhd->khd", grad_scores, query_heads, preferred_element_type=jnp.float32
        )
        grad_value = jnp.einsum(
            "hqk,qhd->khd", soft_weights, grad_heads, preferred_element_type=jnp.float32
        )
        return (
            grad_query.reshape(query_count, group_width).astype(jnp.bfloat16),
            grad_key.reshape(key_count, group_width),
            grad_value.reshape(key_count, group_width),
        )

    query_groups, key_groups, value_groups = lax.map(backward_group, (group_ids, weight_groups))
    key_grads = join_groups(key_groups).reshape(extended.shape[1:])
    value_grads = join_groups(value_groups).reshape(extended.shape[1:])
    grads_ext = jnp.stack((key_grads, value_grads))
    low_rim = grads_ext[:, :tile_len].astype(jnp.bfloat16)
    high_rim = grads_ext[:, 3 * tile_len :].astype(jnp.bfloat16)
    outgoing = jnp.concatenate((low_rim, high_rim), axis=1)
    arrived = extended_2(outgoing, (("tm", 1),), tile_len)
    incoming = jnp.concatenate((arrived[:, :tile_len], arrived[:, 3 * tile_len :]), axis=1)
    middle = grads_ext[:, tile_len : 3 * tile_len]
    own_rims = jnp.concatenate(
        (middle[:, :, :tile_len], middle[:, :, 3 * tile_len :]), axis=2
    ).astype(jnp.bfloat16)
    corner_rims = jnp.concatenate(
        (incoming[:, :, :tile_len], incoming[:, :, 3 * tile_len :]), axis=2
    )
    row_parcel = jnp.stack((own_rims, corner_rims))
    row_arrived = extended_2(row_parcel, (("height", 3),), tile_len)
    from_rows = jnp.concatenate(
        (row_arrived[:, :, :, :tile_len], row_arrived[:, :, :, 3 * tile_len :]), axis=3
    )
    summed = middle[:, :, tile_len : 3 * tile_len] + incoming[:, :, tile_len : 3 * tile_len].astype(
        jnp.float32
    )
    summed = summed + from_rows[0].astype(jnp.float32) + from_rows[1].astype(jnp.float32)
    summed = summed.astype(jnp.bfloat16)
    d_queries = join_groups(query_groups).reshape(queries.shape)
    return (
        outputs.reshape(d_outputs.shape),
        d_queries,
        summed[0].reshape(keys.shape),
        summed[1].reshape(values.shape),
    )


def solution(mesh):
    in_specs = (
        P("dp", "tm", "height", None, None),
        P("dp", "tm", "height", None, None),
        P("dp", "tm", "height", None, None),
        P("dp", None),
        P("dp", "tm", "height", None, None),
    )
    out_specs = (
        P("dp", "tm", "height", None, None),
        P("dp", "tm", "height", None, None),
        P("dp", "tm", "height", None, None),
        P("dp", "tm", "height", None, None),
    )
    return jax.shard_map(body, mesh=mesh, in_specs=in_specs, out_specs=out_specs, check_vma=False)
```

profile of v0, /device:TPU:1, one launch (start us, length us, event | category | flops | bytes accessed | tf_op | source)
XLA Modules:
  0.0 336.3 jit_solution(16390311716919025579)
XLA Ops:
  9.2 4.5 %collective-permute-start = (bf16[2,2,4,8,2560]{4,3,2,1,0:T(8,128)(2,1)S(1)}, bf16[2,2,4,8,2560]{4,3,2,1,0:T(8,128)(2,1)S(1)}, u32[]{:S(2)}, u32[]{:S(2)}) collective-permute-start(bf16[2,2,4,8,2560]{4,3,2,1,0:T(8,128)(2,1)S(1)} %get-tuple-element.227), channel_id=1, source_target_pairs={{0,8},{8,16},{16,24},{1,9},{9,17},{17,25},{2,10},{10,18},{18,26},{... | collective-permute-start | bytes 1966088 | tf_op jit(solution)/shard_map/ppermute | solution.py:25
  15.7 5.6 %collective-permute-done = bf16[2,2,4,8,2560]{4,3,2,1,0:T(8,128)(2,1)S(1)} collective-permute-done((bf16[2,2,4,8,2560]{4,3,2,1,0:T(8,128)(2,1)S(1)}, bf16[2,2,4,8,2560]{4,3,2,1,0:T(8,128)(2,1)S(1)}, u32[]{:S(2)}, u32[]{:S(2)}) %collective-permute-start) | collective-permute-done | bytes 655392 | tf_op jit(solution)/shard_map/ppermute | solution.py:25
  21.2 4.4 %collective-permute-done.1 = bf16[2,2,4,8,2560]{4,3,2,1,0:T(8,128)(2,1)S(1)} collective-permute-done((bf16[2,2,4,8,2560]{4,3,2,1,0:T(8,128)(2,1)S(1)}, bf16[2,2,4,8,2560]{4,3,2,1,0:T(8,128)(2,1)S(1)}, u32[]{:S(2)}, u32[]{:S(2)}) %collective-permute-start.1) | collective-permute-done | bytes 655392 | tf_op jit(solution)/shard_map/ppermute | solution.py:27
  27.7 5.0 %collective-permute-start.2 = (bf16[2,8,2,8,2560]{4,3,2,1,0:T(8,128)(2,1)}, bf16[2,8,2,8,2560]{4,3,2,1,0:T(8,128)(2,1)}, u32[]{:S(2)}, u32[]{:S(2)}) collective-permute-start(bf16[2,8,2,8,2560]{4,3,2,1,0:T(8,128)(2,1)} %get-tuple-element.223), channel_id=1, source_target_pairs={{0,1},{1,2},{2,3},{3,4},{4,5},{5,6},{6,7},{8,9},{9,10},{10,11},{11... | collective-permute-start | bytes 3932168 | tf_op jit(solution)/shard_map/ppermute | solution.py:25
  36.3 16.4 %collective-permute-done.2 = bf16[2,8,2,8,2560]{4,3,2,1,0:T(8,128)(2,1)} collective-permute-done((bf16[2,8,2,8,2560]{4,3,2,1,0:T(8,128)(2,1)}, bf16[2,8,2,8,2560]{4,3,2,1,0:T(8,128)(2,1)}, u32[]{:S(2)}, u32[]{:S(2)}) %collective-permute-start.2) | collective-permute-done | bytes 1310752 | tf_op jit(solution)/shard_map/ppermute | solution.py:25
  52.7 5.4 %collective-permute-done.3 = bf16[2,8,2,8,2560]{4,3,2,1,0:T(8,128)(2,1)} collective-permute-done((bf16[2,8,2,8,2560]{4,3,2,1,0:T(8,128)(2,1)}, bf16[2,8,2,8,2560]{4,3,2,1,0:T(8,128)(2,1)}, u32[]{:S(2)}, u32[]{:S(2)}) %collective-permute-start.3) | collective-permute-done | bytes 1310752 | tf_op jit(solution)/shard_map/ppermute | solution.py:27
  70.9 95.7 %while.28 = (s32[]{:T(128)}, bf16[4,128,640]{1,2,0:T(8,128)(2,1)}, bf16[4,5,128,512]{3,2,1,0:T(8,128)(2,1)}, s32[4]{0:T(128)S(1)}, bf16[512,2560]{0,1:T(8,128)(2...) while((s32[]{:T(128)}, bf16[4,128,640]{1,2,0:T(8,128)(2,1)}, ...), condition=%wide.region_3.4_spmd.clone, body=%wide.region_0.3_spmd.clone.sunk | while | flops 170476032 | bytes 9772999 | solution.py:127
  74.9 5.4 %broadcast_in_dim.70 = pred[2,2,2,2,2,4,4,2,4,2,2,4]{11,10,9,8,7,6,5,4,3,2,1,0:T(4,128)(4,1)} broadcast(pred[2,2,2,4,4,2]{5,4,3,2,1,0:T(4,128)(4,1)S(1)} %get-tuple-element.386), dimensions={0,2,4,6,8,10} | broadcast | bytes 65792 | tf_op jit(solution)/shard_map/broadcast_in_dim | solution.py:53
  80.3 12.1 %broadcast_in_dim.71 = pred[128,512]{1,0:T(8,128)(4,1)S(1)} reshape(pred[2,2,2,2,2,4,4,2,4,2,2,4]{11,10,9,8,7,6,5,4,3,2,1,0:T(4,128)(4,1)} %broadcast_in_dim.70) | data formatting | bytes 131072 | tf_op jit(solution)/shard_map/while/body/eval_jaxpr/jit(_where)/broadcast_in_dim | solution.py:117
  98.7 5.4 %broadcast_in_dim.70 = pred[2,2,2,2,2,4,4,2,4,2,2,4]{11,10,9,8,7,6,5,4,3,2,1,0:T(4,128)(4,1)} broadcast(pred[2,2,2,4,4,2]{5,4,3,2,1,0:T(4,128)(4,1)S(1)} %get-tuple-element.386), dimensions={0,2,4,6,8,10} | broadcast | bytes 65792 | tf_op jit(solution)/shard_map/broadcast_in_dim | solution.py:53
  104.1 12.1 %broadcast_in_dim.71 = pred[128,512]{1,0:T(8,128)(4,1)S(1)} reshape(pred[2,2,2,2,2,4,4,2,4,2,2,4]{11,10,9,8,7,6,5,4,3,2,1,0:T(4,128)(4,1)} %broadcast_in_dim.70) | data formatting | bytes 131072 | tf_op jit(solution)/shard_map/while/body/eval_jaxpr/jit(_where)/broadcast_in_dim | solution.py:117
  122.6 5.4 %broadcast_in_dim.70 = pred[2,2,2,2,2,4,4,2,4,2,2,4]{11,10,9,8,7,6,5,4,3,2,1,0:T(4,128)(4,1)} broadcast(pred[2,2,2,4,4,2]{5,4,3,2,1,0:T(4,128)(4,1)S(1)} %get-tuple-element.386), dimensions={0,2,4,6,8,10} | broadcast | bytes 65792 | tf_op jit(solution)/shard_map/broadcast_in_dim | solution.py:53
  127.9 12.1 %broadcast_in_dim.71 = pred[128,512]{1,0:T(8,128)(4,1)S(1)} reshape(pred[2,2,2,2,2,4,4,2,4,2,2,4]{11,10,9,8,7,6,5,4,3,2,1,0:T(4,128)(4,1)} %broadcast_in_dim.70) | data formatting | bytes 131072 | tf_op jit(solution)/shard_map/while/body/eval_jaxpr/jit(_where)/broadcast_in_dim | solution.py:117
  146.4 5.4 %broadcast_in_dim.70 = pred[2,2,2,2,2,4,4,2,4,2,2,4]{11,10,9,8,7,6,5,4,3,2,1,0:T(4,128)(4,1)} broadcast(pred[2,2,2,4,4,2]{5,4,3,2,1,0:T(4,128)(4,1)S(1)} %get-tuple-element.386), dimensions={0,2,4,6,8,10} | broadcast | bytes 65792 | tf_op jit(solution)/shard_map/broadcast_in_dim | solution.py:53
  151.8 12.1 %broadcast_in_dim.71 = pred[128,512]{1,0:T(8,128)(4,1)S(1)} reshape(pred[2,2,2,2,2,4,4,2,4,2,2,4]{11,10,9,8,7,6,5,4,3,2,1,0:T(4,128)(4,1)} %broadcast_in_dim.70) | data formatting | bytes 131072 | tf_op jit(solution)/shard_map/while/body/eval_jaxpr/jit(_where)/broadcast_in_dim | solution.py:117
  167.9 9.8 %convolution_convert_fusion.2 = bf16[128,2560]{1,0:T(8,128)(2,1)} fusion(bf16[128,2560]{1,0:T(8,128)(2,1)S(1)} %bitcast.136, bf16[2560,2560]{1,0:T(8,128)(2,1)} %all-gather.2.cloned.1.call-done), kind=kOutput, calls=%fused_computation.49 | convolution fusion | flops 1678049280 | bytes 14417920 | tf_op jit(solution)/shard_map/dot_general | solution.py:133
  178.6 54.4 %while.27 = (s32[]{:T(128)}, bf16[4,128,640]{1,2,0:T(8,128)(2,1)}, f32[4,512,640]{1,2,0:T(8,128)}, f32[4,512,640]{1,2,0:T(8,128)}, s32[4]{0:T(128)S(1)}, /*index...) while((s32[]{:T(128)}, bf16[4,128,640]{1,2,0:T(8,128)(2,1)}, ...), condition=%wide.region_6.7_spmd, body=%wide.region_4.6_spmd.sunk | while | flops 340216064 | bytes 23595236 | solution.py:164
  233.0 7.2 %copy.43 = f32[512,4,640]{2,1,0:T(4,128)} copy(f32[512,4,640]{0,2,1:T(8,128)} %bitcast.148) | data formatting | bytes 10485760 | tf_op jit(solution)/shard_map/transpose | solution.py:80
  240.3 7.4 %stack_reshape_reshape.7 = f32[1,8,8,8,2560]{4,3,2,1,0:T(8,128)} reshape(f32[512,4,640]{2,1,0:T(4,128)} %copy.43) | data formatting | bytes 10485760 | tf_op jit(solution)/shard_map/stack;reshape;reshape | solution.py:167
  247.7 7.2 %copy.42 = f32[512,4,640]{2,1,0:T(4,128)} copy(f32[512,4,640]{0,2,1:T(8,128)} %bitcast.149) | data formatting | bytes 10485760 | tf_op jit(solution)/shard_map/transpose | solution.py:80
  254.9 7.4 %stack_reshape_reshape.6 = f32[1,8,8,8,2560]{4,3,2,1,0:T(8,128)} reshape(f32[512,4,640]{2,1,0:T(4,128)} %copy.42) | data formatting | bytes 10485760 | tf_op jit(solution)/shard_map/stack;reshape;reshape | solution.py:167
  282.7 11.2 %collective-permute-done.4 = bf16[2,2,8,8,2560]{4,3,2,1,0:T(8,128)(2,1)S(1)} collective-permute-done((bf16[2,2,8,8,2560]{4,3,2,1,0:T(8,128)(2,1)S(1)}, bf16[2,2,8,8,2560]{4,3,2,1,0:T(8,128)(2,1)S(1)}, u32[]{:S(2)}, u32[]{:S(2)}) %collective-permute-start.4) | collective-permute-done | bytes 1310752 | tf_op jit(solution)/shard_map/ppermute | solution.py:25
  294.0 4.7 %collective-permute-done.5 = bf16[2,2,8,8,2560]{4,3,2,1,0:T(8,128)(2,1)S(1)} collective-permute-done((bf16[2,2,8,8,2560]{4,3,2,1,0:T(8,128)(2,1)S(1)}, bf16[2,2,8,8,2560]{4,3,2,1,0:T(8,128)(2,1)S(1)}, u32[]{:S(2)}, u32[]{:S(2)}) %collective-permute-start.5) | collective-permute-done | bytes 1310752 | tf_op jit(solution)/shard_map/ppermute | solution.py:27
  311.0 7.5 %convolution_convert_fusion.3 = bf16[128,2560]{1,0:T(8,128)(2,1)} fusion(bf16[128,2560]{0,1:T(8,128)(2,1)S(1)} %bitcast.153, bf16[2560,2560]{1,0:T(8,128)(2,1)} %all-gather.2.cloned.1.call-done), kind=kOutput, calls=%fused_computation.50 | convolution fusion | flops 1678049280 | bytes 14417920 | tf_op jit(solution)/shard_map/dot_general | solution.py:129
  (134 shorter events, 142.9 us)
Async XLA Ops:
  7.2 160.7 %copy-start = (bf16[1,4,4,8,2560]{4,3,2,1,0:T(8,128)(2,1)S(1)}, bf16[1,4,4,8,2560]{4,3,2,1,0:T(8,128)(2,1)}, u32[]{:S(2)}) copy-start(bf16[1,4,4,8,2560]{4,3,2,1,0:T(8,128)(2,1)} %param.13) | copy-start | bytes 1966084
  7.2 1.9 copy-start.4
  7.2 160.7 %all-gather.2.cloned.1.call-start = ((), (), s32[]{:S(2)}) async-start(), calls=%async_computation | async-start | bytes 14745600 | tf_op jit(solution)/shard_map/all_gather | solution.py:86
  9.2 12.0 %collective-permute-start = (bf16[2,2,4,8,2560]{4,3,2,1,0:T(8,128)(2,1)S(1)}, bf16[2,2,4,8,2560]{4,3,2,1,0:T(8,128)(2,1)S(1)}, u32[]{:S(2)}, u32[]{:S(2)}) collective-permute-start(bf16[2,2,4,8,2560]{4,3,2,1,0:T(8,128)(2,1)S(1)} %get-tuple-element.227), channel_id=1, source_target_pairs={{0,8},{8,16},{16,24},{1,9},{9,17},{17,25},{2,10},{10,18},{18,26},{... | collective-permute-start | bytes 1966088 | tf_op jit(solution)/shard_map/ppermute | solution.py:25
  13.7 11.9 %collective-permute-start.1 = (bf16[2,2,4,8,2560]{4,3,2,1,0:T(8,128)(2,1)S(1)}, bf16[2,2,4,8,2560]{4,3,2,1,0:T(8,128)(2,1)S(1)}, u32[]{:S(2)}, u32[]{:S(2)}) collective-permute-start(bf16[2,2,4,8,2560]{4,3,2,1,0:T(8,128)(2,1)S(1)} %get-tuple-element.228), channel_id=1, source_target_pairs={{8,0},{16,8},{24,16},{9,1},{17,9},{25,17},{10,2},{18,10},{26,18},{... | collective-permute-start | bytes 1966088 | tf_op jit(solution)/shard_map/ppermute | solution.py:27
  27.7 25.0 %collective-permute-start.2 = (bf16[2,8,2,8,2560]{4,3,2,1,0:T(8,128)(2,1)}, bf16[2,8,2,8,2560]{4,3,2,1,0:T(8,128)(2,1)}, u32[]{:S(2)}, u32[]{:S(2)}) collective-permute-start(bf16[2,8,2,8,2560]{4,3,2,1,0:T(8,128)(2,1)} %get-tuple-element.223), channel_id=1, source_target_pairs={{0,1},{1,2},{2,3},{3,4},{4,5},{5,6},{6,7},{8,9},{9,10},{10,11},{11... | collective-permute-start | bytes 3932168 | tf_op jit(solution)/shard_map/ppermute | solution.py:25
  32.7 25.4 %collective-permute-start.3 = (bf16[2,8,2,8,2560]{4,3,2,1,0:T(8,128)(2,1)}, bf16[2,8,2,8,2560]{4,3,2,1,0:T(8,128)(2,1)}, u32[]{:S(2)}, u32[]{:S(2)}) collective-permute-start(bf16[2,8,2,8,2560]{4,3,2,1,0:T(8,128)(2,1)} %get-tuple-element.224), channel_id=1, source_target_pairs={{1,0},{2,1},{3,2},{4,3},{5,4},{6,5},{7,6},{9,8},{10,9},{11,10},{12... | collective-permute-start | bytes 3932168 | tf_op jit(solution)/shard_map/ppermute | solution.py:27
  268.5 5.5 %copy-start.2 = (f32[2,8,8,8,2560]{4,3,2,1,0:T(8,128)}, f32[2,8,8,8,2560]{4,3,2,1,0:T(8,128)S(1)}, u32[]{:S(2)}) copy-start(f32[2,8,8,8,2560]{4,3,2,1,0:T(8,128)S(1)} %constant_dynamic-update-slice_fusion.6) | copy-start | bytes 31457284
  275.9 18.0 %collective-permute-start.4 = (bf16[2,2,8,8,2560]{4,3,2,1,0:T(8,128)(2,1)S(1)}, bf16[2,2,8,8,2560]{4,3,2,1,0:T(8,128)(2,1)S(1)}, u32[]{:S(2)}, u32[]{:S(2)}) collective-permute-start(bf16[2,2,8,8,2560]{4,3,2,1,0:T(8,128)(2,1)S(1)} %get-tuple-element.216), channel_id=1, source_target_pairs={{0,8},{8,16},{16,24},{1,9},{9,17},{17,25},{2,10},{10,18},{18,26},{... | collective-permute-start | bytes 3932168 | tf_op jit(solution)/shard_map/ppermute | solution.py:25
  279.3 19.3 %collective-permute-start.5 = (bf16[2,2,8,8,2560]{4,3,2,1,0:T(8,128)(2,1)S(1)}, bf16[2,2,8,8,2560]{4,3,2,1,0:T(8,128)(2,1)S(1)}, u32[]{:S(2)}, u32[]{:S(2)}) collective-permute-start(bf16[2,2,8,8,2560]{4,3,2,1,0:T(8,128)(2,1)S(1)} %get-tuple-element.215), channel_id=1, source_target_pairs={{8,0},{16,8},{24,16},{9,1},{17,9},{25,17},{10,2},{18,10},{26,18},{... | collective-permute-start | bytes 3932168 | tf_op jit(solution)/shard_map/ppermute | solution.py:27
  301.0 10.0 %copy-start.3 = (bf16[4,128,640]{1,2,0:T(8,128)(2,1)S(1)}, bf16[4,128,640]{1,2,0:T(8,128)(2,1)}, u32[]{:S(2)}) copy-start(bf16[4,128,640]{1,2,0:T(8,128)(2,1)} %get-tuple-element.101) | copy-start | bytes 1966084
  301.0 18.3 %collective-permute-start.6 = (bf16[2,2,4,2,8,2560]{5,4,3,2,1,0:T(8,128)(2,1)}, bf16[2,2,4,2,8,2560]{5,4,3,2,1,0:T(8,128)(2,1)}, u32[]{:S(2)}, u32[]{:S(2)}) collective-permute-start(bf16[2,2,4,2,8,2560]{5,4,3,2,1,0:T(8,128)(2,1)} %get-tuple-element.220), channel_id=1, source_target_pairs={{0,1},{1,2},{2,3},{3,4},{4,5},{5,6},{6,7},{8,9},{9,10},{10,11},{11... | collective-permute-start | bytes 3932168 | tf_op jit(solution)/shard_map/ppermute | solution.py:25
  305.4 19.1 %collective-permute-start.7 = (bf16[2,2,4,2,8,2560]{5,4,3,2,1,0:T(8,128)(2,1)}, bf16[2,2,4,2,8,2560]{5,4,3,2,1,0:T(8,128)(2,1)}, u32[]{:S(2)}, u32[]{:S(2)}) collective-permute-start(bf16[2,2,4,2,8,2560]{5,4,3,2,1,0:T(8,128)(2,1)} %get-tuple-element.219), channel_id=1, source_target_pairs={{1,0},{2,1},{3,2},{4,3},{5,4},{6,5},{7,6},{9,8},{10,9},{11,10},{12... | collective-permute-start | bytes 3932168 | tf_op jit(solution)/shard_map/ppermute | solution.py:27
  325.8 3.6 %copy-start.1 = (bf16[1,4,4,8,2560]{4,3,2,1,0:T(8,128)(2,1)S(1)}, bf16[1,4,4,8,2560]{4,3,2,1,0:T(8,128)(2,1)}, u32[]{:S(2)}) copy-start(bf16[1,4,4,8,2560]{4,3,2,1,0:T(8,128)(2,1)} %param.13) | copy-start | bytes 1966084
Sparse Core Ops, SparseCore 0:
  10.6 157.2 all-gather.1
where the time goes:
time: 340 us; the launch traced here: 336 us
  local copies, waits for them, and re-layouts  181 us (53%)
  waiting for transfers between devices  54.1 us (16%)
  matrix products  43.7 us (13%)
  starting transfers between devices  23.8 us (7%)
  between operations  14.3 us (4%)
  other arithmetic  13.8 us (4%)
  loops' own time  5.61 us (2%)
    broadcast_in_dim x4, local copies, waits for them, and re-layouts, forward_group(): masked = jnp.where(window[None], scores, -jnp.inf)  48.2 us
    ppermute x4, waiting for transfers between devices, extended_2(): lax.ppermute(tail, axis, [(i, (i + 1) % count) for i in range(ends)])  33.9 us
    dynamic_slice x28, local copies, waits for them, and re-layouts, split_heads(): lax.dynamic_slice_in_dim(matrix, group_index * group_width, group_width, 1)  26.9 us
    broadcast_in_dim x4, local copies, waits for them, and re-layouts, window_mask(): jnp.broadcast_to(spread, (2, tile_len, 2, tile_len, tiles_across, tile_co...  21.5 us
    ppermute x4, waiting for transfers between devices, extended_2(): lax.ppermute(head, axis, [((i + 1) % count, i) for i in range(ends)])  18.2 us
    another operation x3, local copies, waits for them, and re-layouts, body(): grads_ext = jnp.stack((key_grads, value_grads))  17.9 us
    ppermute x4, starting transfers between devices, extended_2(): lax.ppermute(tail, axis, [(i, (i + 1) % count) for i in range(ends)])  17.3 us
    unnamed x17, local copies, waits for them, and re-layouts  17 us
  transfers between devices with their start and end apart: 9, of which 9 were waited for; matrix products, arithmetic and copies ran while one was open for 38% of the time, Pallas kernels for 0%

commit v1 on v0

v1 whole, which is shorter than its diff:
```python
import functools
import math

import jax
import jax.numpy as jnp
from jax import lax
from jax.experimental import pallas as pl
from jax.experimental.pallas import tpu as pltpu
from jax.sharding import PartitionSpec as P

HDIM = 128
AXES = ("dp", "tm", "height")
NEG = -1e30
SCALE = 1.0 / math.sqrt(HDIM)
EXP2_SCALE = SCALE * math.log2(math.e)
F32 = jnp.float32
BF16 = jnp.bfloat16

HPS = 2
HEADS_HALF = 10
W_HALF = 1280
VMEM_LIMIT = 10 * 1024 * 1024


def make_perm(shape, fn):
    n_dp, n_tm, n_h = shape
    pairs = []
    for d in range(n_dp):
        for t in range(n_tm):
            for h in range(n_h):
                e, u, g = fn(d, t, h)
                if 0 <= u < n_tm and 0 <= g < n_h:
                    pairs.append(((d * n_tm + t) * n_h + h, (e * n_tm + u) * n_h + g))
    return pairs


def dot(a, b, ca, cb):
    return lax.dot_general(a, b, (((ca,), (cb,)), ((), ())), preferred_element_type=F32)


def in_vmem(shape, dtype):
    return pltpu.VMEM(shape, dtype)


def call(kernel, outs, ins, flops=0, moved=1_000_000, exps=0, scratch=(), aliases=None, hbm_in=0):
    vm = pl.BlockSpec(memory_space=pltpu.VMEM)
    hb = pl.BlockSpec(memory_space=pl.ANY)
    near = [pltpu.with_memory_space_constraint(x, pltpu.VMEM) for x in ins[: len(ins) - hbm_in]]
    far = list(ins[len(ins) - hbm_in :])
    out_specs = [hb if isinstance(o, jax.ShapeDtypeStruct) else vm for o in outs]
    return pl.pallas_call(
        kernel,
        out_shape=tuple(outs),
        in_specs=[vm] * len(near) + [hb] * len(far),
        out_specs=tuple(out_specs),
        scratch_shapes=list(scratch),
        input_output_aliases=aliases or {},
        compiler_params=pltpu.CompilerParams(vmem_limit_bytes=VMEM_LIMIT),
        cost_estimate=pl.CostEstimate(flops=flops, bytes_accessed=moved, transcendentals=exps),
    )(*near, *far)


def half_of(kind):
    mine = lax.axis_index("dp") // 4
    return mine if kind == "local" else 1 - mine


def window_bias(zb_ref, tb_ref):
    tm = lax.axis_index("tm")
    ht = lax.axis_index("height")
    t_lo = jnp.where(tm > 0, 1, 0)
    t_hi = jnp.where(tm < lax.axis_size("tm") - 1, 1, 0)
    z_lo = jnp.where(ht > 0, 1, 0)
    z_hi = jnp.where(ht < lax.axis_size("height") - 1, 1, 0)
    q = lax.broadcasted_iota(jnp.int32, (128, 128), 0)
    k = lax.broadcasted_iota(jnp.int32, (128, 128), 1)
    late = (q // 16) % 2
    side_ok = jnp.where(late == 0, z_lo, z_hi)
    z_side = jnp.where(k < 64, 0, 1)
    zb_ref[...] = jnp.where((z_side == late) & (side_ok > 0), 0.0, NEG).astype(F32)
    t_ok = jnp.where(q < 64, t_lo, t_hi)
    corner = jnp.where(k < 96, 0, 1)
    t_in = (k < 64) | ((corner == late) & (side_ok > 0))
    tb_ref[...] = jnp.where(t_in & (t_ok > 0), 0.0, NEG).astype(F32)


def key_values(k_ref, v_ref, zl_ref, zh_ref, tl_ref, cl_ref, th_ref, ch_ref, c):
    cat = lambda *a: jnp.concatenate(a, axis=0)
    k_oz = cat(k_ref[:, c], zl_ref[0, :, c], zh_ref[0, :, c])
    v_oz = cat(v_ref[:, c], zl_ref[1, :, c], zh_ref[1, :, c])
    k_tl = cat(tl_ref[0, :, c], cl_ref[0, :, c])
    v_tl = cat(tl_ref[1, :, c], cl_ref[1, :, c])
    k_th = cat(th_ref[0, :, c], ch_ref[0, :, c])
    v_th = cat(th_ref[1, :, c], ch_ref[1, :, c])
    return k_oz, v_oz, k_tl, v_tl, k_th, v_th


def lanes(head):
    return pl.ds(pl.multiple_of(head * HDIM, HDIM), HDIM)


def forward_kernel(kind, q_ref, k_ref, v_ref, *rest):
    halo, (att_ref, p_ref, zb_ref, tb_ref) = rest[:6], rest[6:]
    window_bias(zb_ref, tb_ref)
    first = half_of(kind) * HEADS_HALF

    def one(h):
        c = lanes(first + h)
        q = q_ref[:, c]
        k_oz, v_oz, k_tl, v_tl, k_th, v_th = key_values(k_ref, v_ref, *halo, c)
        s_oz = dot(q, k_oz, 1, 1)
        s_t = jnp.concatenate([dot(q[:64], k_tl, 1, 1), dot(q[64:], k_th, 1, 1)], axis=0)
        s_o = s_oz[:, :128]
        s_z = s_oz[:, 128:] + zb_ref[...]
        s_t = s_t + tb_ref[...]
        m = jnp.max(jnp.maximum(jnp.maximum(s_o, s_z), s_t), axis=1, keepdims=True)
        e_o = jnp.exp2((s_o - m) * EXP2_SCALE)
        e_z = jnp.exp2((s_z - m) * EXP2_SCALE)
        e_t = jnp.exp2((s_t - m) * EXP2_SCALE)
        inv = 1.0 / jnp.sum(e_o + e_z + e_t, axis=1, keepdims=True)
        p_oz = jnp.concatenate([e_o * inv, e_z * inv], axis=1).astype(BF16)
        p_t = (e_t * inv).astype(BF16)
        p_ref[h, :, :256] = p_oz
        p_ref[h, :, 256:] = p_t
        a_t = jnp.concatenate([dot(p_t[:64], v_tl, 1, 0), dot(p_t[64:], v_th, 1, 0)], axis=0)
        att_ref[:, lanes(h)] = (dot(p_oz, v_oz, 1, 0) + a_t).astype(BF16)

    def step(i, carry):
        for j in range(HPS):
            one(i * HPS + j)
        return carry

    lax.fori_loop(0, HEADS_HALF // HPS, step, 0)


def forward_half(kind, operands):
    return call(
        functools.partial(forward_kernel, kind),
        (in_vmem((128, W_HALF), BF16), in_vmem((HEADS_HALF, 128, 384), BF16)),
        operands, flops=2 * 2 * 10 * 128 * 384 * 128, moved=6_000_000, exps=10 * 128 * 384,
        scratch=(pltpu.VMEM((128, 128), F32), pltpu.VMEM((128, 128), F32)),
    )


def backward_kernel(kind, q_ref, k_ref, v_ref, *rest):
    halo, (p_ref, g_ref, dq_ref, own_ref, rim_ref, tlo_ref, thi_ref) = rest[:6], rest[6:]
    first = half_of(kind) * HEADS_HALF

    def one(h):
        c = lanes(first + h)
        o = lanes(h)
        q = q_ref[:, c]
        g = g_ref[:, o]
        k_oz, v_oz, k_tl, v_tl, k_th, v_th = key_values(k_ref, v_ref, *halo, c)
        p_oz = p_ref[h, :, :256]
        p_t = p_ref[h, :, 256:]
        dp_oz = dot(g, v_oz, 1, 1)
        dp_t = jnp.concatenate([dot(g[:64], v_tl, 1, 1), dot(g[64:], v_th, 1, 1)], axis=0)
        w_oz = p_oz.astype(F32)
        w_t = p_t.astype(F32)
        x_oz = w_oz * dp_oz
        row = jnp.sum(x_oz[:, :128] + x_oz[:, 128:] + w_t * dp_t, axis=1, keepdims=True)
        ds_oz = (w_oz * (dp_oz - row) * SCALE).astype(BF16)
        ds_t = (w_t * (dp_t - row) * SCALE).astype(BF16)
        dq_t = jnp.concatenate([dot(ds_t[:64], k_tl, 1, 0), dot(ds_t[64:], k_th, 1, 0)], axis=0)
        dq_ref[:, o] = (dot(ds_oz, k_oz, 1, 0) + dq_t).astype(BF16)
        dk_oz = dot(ds_oz, q, 0, 0)
        dv_oz = dot(p_oz, g, 0, 0)
        own_ref[0, :, o] = dk_oz[:128]
        own_ref[1, :, o] = dv_oz[:128]
        rim_ref[0, :, o] = dk_oz[128:]
        rim_ref[1, :, o] = dv_oz[128:]
        tlo_ref[0, :, o] = dot(ds_t[:64], q[:64], 0, 0).astype(BF16)
        tlo_ref[1, :, o] = dot(p_t[:64], g[:64], 0, 0).astype(BF16)
        thi_ref[0, :, o] = dot(ds_t[64:], q[64:], 0, 0).astype(BF16)
        thi_ref[1, :, o] = dot(p_t[64:], g[64:], 0, 0).astype(BF16)

    def step(i, carry):
        for j in range(HPS):
            one(i * HPS + j)
        return carry

    lax.fori_loop(0, HEADS_HALF // HPS, step, 0)


def backward_half(kind, operands, probs, grad):
    pair = (2, 128, W_HALF)
    return call(
        functools.partial(backward_kernel, kind),
        (in_vmem((128, W_HALF), BF16), in_vmem(pair, F32), in_vmem(pair, F32),
         in_vmem(pair, BF16), in_vmem(pair, BF16)),
        (*operands, probs, grad), flops=4 * 2 * 10 * 128 * 384 * 128, moved=12_000_000,
    )


def shard_rows(which):
    y = lax.axis_index("dp") % 4
    core = lax.axis_index("tm") % 2
    toward = jnp.where(core == 0, 3, 1)
    shard = {"own": y, "near": (y + toward) % 4, "far": (y + 4 - toward) % 4}.get(which, (y + 2) % 4)
    at = shard * 320
    if which == "c0":
        at = at + core * 160
    if which == "c1":
        at = at + (1 - core) * 160
    return at


def put_rows(dst_ref, src_ref, which):
    rows = src_ref.shape[0]
    at = shard_rows(which)

    def step(i, carry):
        r = pl.multiple_of(i * 32, 32)
        dst_ref[pl.ds(pl.multiple_of(at + r, 32), 32), :] = src_ref[pl.ds(r, 32), :]
        return carry

    lax.fori_loop(0, rows // 32, step, 0)


def gather_kernel(own_ref, near_ref, far_ref, w_ref):
    put_rows(w_ref, own_ref, "own")
    put_rows(w_ref, near_ref, "near")
    put_rows(w_ref, far_ref, "far")


def gather_rows(own, near, far):
    return call(gather_kernel, (in_vmem((W_HALF, 2560), BF16),), (own, near, far), moved=10_000_000)[0]


def grad_proj_kernel(w_in, c0_ref, c1_ref, mine_ref, theirs_ref, w_ref, o_ref, t_ref):
    put_rows(w_ref, c0_ref, "c0")
    put_rows(w_ref, c1_ref, "c1")

    def step(n, carry):
        r = pl.ds(pl.multiple_of(n * 256, 256), 256)
        w = w_ref[r, :]
        o_ref[:, r] = dot(mine_ref[...], w, 1, 1).astype(BF16)
        t_ref[:, r] = dot(theirs_ref[...], w, 1, 1).astype(BF16)
        return carry

    lax.fori_loop(0, W_HALF // 256, step, 0)


def grad_proj(w, c0, c1, mine, theirs):
    return call(
        grad_proj_kernel,
        (in_vmem((W_HALF, 2560), BF16), in_vmem((128, W_HALF), BF16), in_vmem((128, W_HALF), BF16)),
        (w, c0, c1, mine, theirs), flops=2 * 256 * 1280 * 2560, moved=9_000_000, aliases={0: 0},
    )


def out_proj_kernel(w_ref, mine_ref, theirs_ref, o_ref, t_ref):
    def step(n, carry):
        r = pl.ds(pl.multiple_of(n * 256, 256), 256)
        w = w_ref[:, r]
        o_ref[:, r] = dot(mine_ref[...], w, 1, 0)
        t_ref[:, r] = dot(theirs_ref[...], w, 1, 0).astype(BF16)
        return carry

    lax.fori_loop(0, 2560 // 256, step, 0)


def out_proj(w, mine, theirs):
    return call(
        out_proj_kernel, (in_vmem((128, 2560), F32), in_vmem((128, 2560), BF16)),
        (w, mine, theirs), flops=2 * 256 * 1280 * 2560, moved=9_000_000,
    )


def rim_kernel(rim_ref, prev_ref, next_ref, lo_ref, hi_ref):
    for half, out in ((0, lo_ref), (1, hi_ref)):
        c = slice(64 + 32 * half, 96 + 32 * half)
        corner = jnp.concatenate([prev_ref[:, c], next_ref[:, c]], axis=1).astype(F32)
        out[...] = (rim_ref[:, 64 * half : 64 * half + 64] + corner).astype(BF16)


def rim_half(rim, from_prev, from_next):
    return call(
        rim_kernel, (in_vmem((2, 64, W_HALF), BF16),) * 2, (rim, from_prev, from_next),
        moved=4_000_000,
    )


def final_kernel(kind, own_ref, prev_ref, next_ref, lo_ref, hi_ref, d_ref, *rest):
    dk_ref, dv_ref, dq_ref, dk_tile, dv_tile, sems = rest[-6:]
    at = pl.ds(pl.multiple_of(half_of(kind) * W_HALF, W_HALF), W_HALF)
    copies = [pltpu.make_async_copy(d_ref, dq_ref.at[:, at], sems.at[2])]
    copies[0].start()
    for kv, tile, out in ((0, dk_tile, dk_ref), (1, dv_tile, dv_ref)):
        frames = jnp.concatenate([prev_ref[kv, :64], next_ref[kv, :64]], axis=0).astype(F32)
        total = own_ref[kv] + frames
        for f in range(4):
            low = total[f * 32 : f * 32 + 16] + lo_ref[kv, f * 16 : f * 16 + 16].astype(F32)
            high = total[f * 32 + 16 : f * 32 + 32] + hi_ref[kv, f * 16 : f * 16 + 16].astype(F32)
            tile[f * 32 : f * 32 + 16] = low.astype(BF16)
            tile[f * 32 + 16 : f * 32 + 32] = high.astype(BF16)
        copies.append(pltpu.make_async_copy(tile, out.at[:, at], sems.at[kv]))
        copies[-1].start()
    for cp in copies:
        cp.wait()


def final_half(kind, own, from_prev, from_next, from_lo, from_hi, d_q, *earlier):
    whole = jax.ShapeDtypeStruct((128, 2560), BF16)
    return call(
        functools.partial(final_kernel, kind), (whole,) * 3,
        (own, from_prev, from_next, from_lo, from_hi, d_q, *earlier), moved=6_000_000,
        scratch=(pltpu.VMEM((128, W_HALF), BF16), pltpu.VMEM((128, W_HALF), BF16), pltpu.SemaphoreType.DMA((3,))),
        aliases={6: 0, 7: 1, 8: 2} if earlier else {}, hbm_in=len(earlier),
    )


def prep_kernel(k_ref, v_ref, zlo_ref, zhi_ref, tlo_ref, thi_ref):
    for kv, src in ((0, k_ref), (1, v_ref)):
        for f in range(4):
            zlo_ref[kv, f * 16 : f * 16 + 16] = src[f * 32 : f * 32 + 16]
            zhi_ref[kv, f * 16 : f * 16 + 16] = src[f * 32 + 16 : f * 32 + 32]
        tlo_ref[kv] = src[:64]
        thi_ref[kv] = src[64:]


def prep(keys, values):
    return call(prep_kernel, (in_vmem((2, 64, 2560), BF16),) * 4, (keys, values), moved=4_000_000)


def corner_kernel(lo_ref, hi_ref, down_ref, up_ref):
    down_ref[:, :32] = lo_ref[:, :32]
    down_ref[:, 32:] = hi_ref[:, :32]
    up_ref[:, :32] = lo_ref[:, 32:]
    up_ref[:, 32:] = hi_ref[:, 32:]


def corners(z_lo, z_hi):
    return call(corner_kernel, (in_vmem((2, 64, 2560), BF16),) * 2, (z_lo, z_hi), moved=2_600_000)


def body(queries, keys, values, projection, d_outputs):
    shape = (lax.axis_size("dp"), lax.axis_size("tm"), lax.axis_size("height"))

    def send(x, fn):
        return lax.ppermute(x, AXES, make_perm(shape, fn))

    pair_chip = lambda d, t, h: (d ^ 4, t ^ 2, h)
    other_core = lambda d, t, h: (d, t ^ 1, h)
    ring_y = lambda d, t, h: ((d & 4) | ((d + (1 if t % 2 == 0 else 3)) & 3), t, h)
    up_z = lambda d, t, h: (d, t, h + 1)
    down_z = lambda d, t, h: (d, t, h - 1)
    up_t = lambda d, t, h: (d, t + 1, h)
    down_t = lambda d, t, h: (d, t - 1, h)

    tokens = queries.shape[1] * queries.shape[2] * queries.shape[3]
    flat = lambda a: a.reshape(tokens, a.shape[-1])
    q, k, v, d_out = flat(queries), flat(keys), flat(values), flat(d_outputs)

    w_near = send(projection, ring_y)
    their_d_out = send(d_out, pair_chip)
    z_lo_s, z_hi_s, t_lo_s, t_hi_s = prep(k, v)
    z_lo = send(z_hi_s, up_z)
    z_hi = send(z_lo_s, down_z)
    t_lo = send(t_hi_s, up_t)
    t_hi = send(t_lo_s, down_t)
    c_down, c_up = corners(z_lo, z_hi)
    c_lo = send(c_up, up_t)
    c_hi = send(c_down, down_t)
    w_far = send(w_near, other_core)
    core = lax.axis_index("tm") % 2
    w_c0 = send(lax.dynamic_slice_in_dim(w_near, core * 160, 160, 0), ring_y)
    w_c1 = send(w_c0, other_core)
    rows = gather_rows(projection, w_near, w_far)

    operands = (q, k, v, z_lo, z_hi, t_lo, c_lo, t_hi, c_hi)
    att_remote, p_remote = forward_half("remote", operands)
    their_att = send(att_remote, pair_chip)
    att_local, p_local = forward_half("local", operands)

    rows, g_local, g_theirs = grad_proj(rows, w_c0, w_c1, d_out, their_d_out)
    g_remote = send(g_theirs, pair_chip)

    dq_a, own_a, rim_a, tlo_a, thi_a = backward_half("local", operands, p_local, g_local)
    prev_a = send(thi_a, up_t)
    next_a = send(tlo_a, down_t)
    dq_b, own_b, rim_b, tlo_b, thi_b = backward_half("remote", operands, p_remote, g_remote)
    prev_b = send(thi_b, up_t)
    next_b = send(tlo_b, down_t)

    part, part_theirs = out_proj(rows, att_local, their_att)
    part_remote = send(part_theirs, pair_chip)

    rlo_a, rhi_a = rim_half(rim_a, prev_a, next_a)
    from_lo_a = send(rhi_a, up_z)
    from_hi_a = send(rlo_a, down_z)
    rlo_b, rhi_b = rim_half(rim_b, prev_b, next_b)
    from_lo_b = send(rhi_b, up_z)
    from_hi_b = send(rlo_b, down_z)

    outputs = (part + part_remote.astype(F32)).astype(BF16)
    done = final_half("local", own_a, prev_a, next_a, from_lo_a, from_hi_a, dq_a)
    dk, dv, dq = final_half("remote", own_b, prev_b, next_b, from_lo_b, from_hi_b, dq_b, *done)
    return (
        outputs.reshape(d_outputs.shape),
        dq.reshape(queries.shape),
        dk.reshape(keys.shape),
        dv.reshape(values.shape),
    )


def solution(mesh):
    spec = P("dp", "tm", "height", None, None)
    return jax.shard_map(
        body, mesh=mesh, in_specs=(spec, spec, spec, P("dp", None), spec),
        out_specs=(spec, spec, spec, spec), check_vma=False,
    )
```

time: 340 us -> 126 us (0.37)
  the two profiles are of different devices: /device:TPU:1 before, /device:TPU:104 now
where the time goes in v1:
time: 126 us
  starting transfers between devices  52.4 us (42%)
  waiting for transfers between devices  40.5 us (32%)
  Pallas kernels  31.1 us (25%)
    ppermute x22, starting transfers between devices, send(): return lax.ppermute(x, AXES, make_perm(shape, fn))  52.4 us
    ppermute x22, waiting for transfers between devices, send(): return lax.ppermute(x, AXES, make_perm(shape, fn))  40.5 us
    pallas_call x13, Pallas kernels, call(): pl.pallas_call(kernel, out_shape=tuple(outs), in_specs=[vm] * len(near) +...  31.1 us
  transfers between devices with their start and end apart: 22, of which 7 were waited for; matrix products, arithmetic and copies ran while one was open for 1% of the time, Pallas kernels for 24%

profile of v1, /device:TPU:104, one launch (start us, length us, event | category | flops | bytes accessed | tf_op | source)
XLA Modules:
  0.0 126.0 jit_solution(17613568547407333480)
XLA Ops:
  2.3 19.8 %collective-permute-done.near_ref = bf16[320,2560]{1,0:T(8,128)(2,1)S(1)} collective-permute-done((bf16[320,2560]{1,0:T(8,128)(2,1)}, bf16[320,2560]{1,0:T(8,128)(2,1)S(1)}, u32[]{:S(2)}, u32[]{:S(2)}) %collective-permute-start) | collective-permute-done | bytes 1638432 | tf_op jit(solution)/shard_map/ppermute | solution.py:342
  24.0 5.2 %collective-permute-start.5 = (bf16[2,64,2560]{2,1,0:T(8,128)(2,1)S(1)}, bf16[2,64,2560]{2,1,0:T(8,128)(2,1)S(1)}, u32[]{:S(2)}, u32[]{:S(2)}) collective-permute-start(bf16[2,64,2560]{2,1,0:T(8,128)(2,1)S(1)} %get-tuple-element.40), channel_id=1, source_target_pairs={{0,1},{1,2},{2,3},{3,4},{4,5},{5,6},{6,7},{8,9},{9,10},{10,11},{11... | collective-permute-start | bytes 1966088 | tf_op jit(solution)/shard_map/ppermute | solution.py:342
  29.1 1.9 %collective-permute-start.6 = (bf16[2,64,2560]{2,1,0:T(8,128)(2,1)S(1)}, bf16[2,64,2560]{2,1,0:T(8,128)(2,1)S(1)}, u32[]{:S(2)}, u32[]{:S(2)}) collective-permute-start(bf16[2,64,2560]{2,1,0:T(8,128)(2,1)S(1)} %get-tuple-element.41), channel_id=1, source_target_pairs={{1,0},{2,1},{3,2},{4,3},{5,4},{6,5},{7,6},{9,8},{10,9},{11,10},{12... | collective-permute-start | bytes 1966088 | tf_op jit(solution)/shard_map/ppermute | solution.py:342
  31.1 2.8 %collective-permute-start.4 = (bf16[128,2560]{1,0:T(8,128)(2,1)S(1)}, bf16[128,2560]{1,0:T(8,128)(2,1)S(1)}, u32[]{:S(2)}, u32[]{:S(2)}) collective-permute-start(bf16[128,2560]{1,0:T(8,128)(2,1)S(1)} %bitcast.22), channel_id=1, source_target_pairs={{0,144},{1,145},{2,146},{3,147},{4,148},{5,149},{6,150},{7,151},{8... | collective-permute-start | bytes 1966088 | tf_op jit(solution)/shard_map/ppermute | solution.py:342
  34.5 9.0 %collective-permute-done.5.lo_ref.rest_0_ = bf16[2,64,2560]{2,1,0:T(8,128)(2,1)S(1)} collective-permute-done((bf16[2,64,2560]{2,1,0:T(8,128)(2,1)S(1)}, bf16[2,64,2560]{2,1,0:T(8,128)(2,1)S(1)}, u32[]{:S(2)}, u32[]{:S(2)}) %collective-permute-start.5) | collective-permute-done | bytes 655392 | tf_op jit(solution)/shard_map/ppermute | solution.py:342
  45.0 3.9 %collective-permute-done.6.hi_ref.rest_1_ = bf16[2,64,2560]{2,1,0:T(8,128)(2,1)S(1)} collective-permute-done((bf16[2,64,2560]{2,1,0:T(8,128)(2,1)S(1)}, bf16[2,64,2560]{2,1,0:T(8,128)(2,1)S(1)}, u32[]{:S(2)}, u32[]{:S(2)}) %collective-permute-start.6) | collective-permute-done | bytes 655392 | tf_op jit(solution)/shard_map/ppermute | solution.py:342
  50.3 3.1 %collective-permute-start.8 = (bf16[2,64,2560]{2,1,0:T(8,128)(2,1)S(1)}, bf16[2,64,2560]{2,1,0:T(8,128)(2,1)S(1)}, u32[]{:S(2)}, u32[]{:S(2)}) collective-permute-start(bf16[2,64,2560]{2,1,0:T(8,128)(2,1)S(1)} %get-tuple-element.43), channel_id=1, source_target_pairs={{0,8},{1,9},{2,10},{3,11},{4,12},{5,13},{6,14},{7,15},{8,16},{9,17... | collective-permute-start | bytes 1966088 | tf_op jit(solution)/shard_map/ppermute | solution.py:342
  54.7 1.9 %shard_map.84.w_in = bf16[1280,2560]{1,0:T(8,128)(2,1)S(1)} custom-call(bf16[320,2560]{1,0:T(8,128)(2,1)S(1)} %copy-done.3, bf16[320,2560]{1,0:T(8,128)(2,1)S(1)} %collective-permute-done.near_ref, bf16[320,2560]{1,0:T(8,128)(2,1)} %collective-permute-done.1.far_ref), custom_call_target="tpu_custom_call" | custom-call | bytes 10000000 | tf_op jit(solution)/shard_map/pallas_call | solution.py:51
  56.6 5.0 %shard_map.85 = (bf16[1280,2560]{1,0:T(8,128)(2,1)S(1)}, bf16[128,1280]{1,0:T(8,128)(2,1)S(1)}, bf16[128,1280]{1,0:T(8,128)(2,1)S(1)}) custom-call(bf16[1280,2560]{1,0:T(8,128)(2,1)S(1)} %shard_map.84.w_in, bf16[160,2560]{1,0:T(8,128)(2,1)S(1)} %collective-permute-done.2.c0_ref, ...), custom_call_target="tpu_custom_call", output_to_operand_aliasing={{0}: (0, {})} | custom-call | flops 1677721600 | bytes 9000000 | tf_op jit(solution)/shard_map/pallas_call | solution.py:51
  61.6 4.7 %collective-permute-start.13 = (bf16[128,1280]{1,0:T(8,128)(2,1)S(1)}, bf16[128,1280]{1,0:T(8,128)(2,1)S(1)}, u32[]{:S(2)}, u32[]{:S(2)}) collective-permute-start(bf16[128,1280]{1,0:T(8,128)(2,1)S(1)} %get-tuple-element.51), channel_id=1, source_target_pairs={{0,144},{1,145},{2,146},{3,147},{4,148},{5,149},{6,150},{7,151},{8... | collective-permute-start | bytes 983048 | tf_op jit(solution)/shard_map/ppermute | solution.py:342
  66.3 4.4 %shard_map.89 = (bf16[128,1280]{1,0:T(8,128)(2,1)S(1)}, bf16[10,128,384]{2,1,0:T(8,128)(2,1)S(1)}) custom-call(bf16[128,2560]{1,0:T(8,128)(2,1)S(1)} %bitcast.18, bf16[128,2560]{1,0:T(8,128)(2,1)S(1)} %bitcast.9, bf16[128,2560]{1,0:T(8,128)(2,1)S(1)} %bitcast.14, bf16[2,64,2560]{2,1,0:T(8,128)(2,1)S(1)} %collective-permute-done.5.lo_ref.rest_0_, ...), custom_call_target="tpu_custom_call" | custom-call | flops 251658240 | bytes 6000000 | tf_op jit(solution)/shard_map/pallas_call | solution.py:51
  70.7 2.5 %collective-permute-start.11 = (bf16[128,1280]{1,0:T(8,128)(2,1)S(1)}, bf16[128,1280]{1,0:T(8,128)(2,1)S(1)}, u32[]{:S(2)}, u32[]{:S(2)}) collective-permute-start(bf16[128,1280]{1,0:T(8,128)(2,1)S(1)} %get-tuple-element.47), channel_id=1, source_target_pairs={{0,144},{1,145},{2,146},{3,147},{4,148},{5,149},{6,150},{7,151},{8... | collective-permute-start | bytes 983048 | tf_op jit(solution)/shard_map/ppermute | solution.py:342
  73.2 4.4 %shard_map.88 = (bf16[128,1280]{1,0:T(8,128)(2,1)S(1)}, bf16[10,128,384]{2,1,0:T(8,128)(2,1)S(1)}) custom-call(bf16[128,2560]{1,0:T(8,128)(2,1)S(1)} %bitcast.19, bf16[128,2560]{1,0:T(8,128)(2,1)S(1)} %bitcast.10, bf16[128,2560]{1,0:T(8,128)(2,1)S(1)} %bitcast.15, bf16[2,64,2560]{2,1,0:T(8,128)(2,1)S(1)} %collective-permute-done.5.lo_ref.rest_0_, ...), custom_call_target="tpu_custom_call" | custom-call | flops 251658240 | bytes 6000000 | tf_op jit(solution)/shard_map/pallas_call | solution.py:51
  77.6 4.8 %shard_map.93 = (bf16[128,1280]{1,0:T(8,128)(2,1)S(1)}, f32[2,128,1280]{2,1,0:T(8,128)S(1)}, f32[2,128,1280]{2,1,0:T(8,128)S(1)}, bf16[2,128,1280]{2,1,0:T(8,128)(2,1)S(1)}, bf16[2,128,1280]{2,1,0:T(8,128)(2,1)S(1)}) custom-call(bf16[128,2560]{1,0:T(8,128)(2,1)S(1)} %bitcast.20, bf16[128,2560]{1,0:T(8,128)(2,1)S(1)} %bitcast.11, ...), custom_call_target="tpu_custom_call" | custom-call | flops 503316480 | bytes 12000000 | tf_op jit(solution)/shard_map/pallas_call | solution.py:51
  85.0 4.8 %shard_map.91 = (bf16[128,1280]{1,0:T(8,128)(2,1)S(1)}, f32[2,128,1280]{2,1,0:T(8,128)S(1)}, f32[2,128,1280]{2,1,0:T(8,128)S(1)}, bf16[2,128,1280]{2,1,0:T(8,128)(2,1)S(1)}, bf16[2,128,1280]{2,1,0:T(8,128)(2,1)S(1)}) custom-call(bf16[128,2560]{1,0:T(8,128)(2,1)S(1)} %bitcast.21, bf16[128,2560]{1,0:T(8,128)(2,1)S(1)} %bitcast.12, ...), custom_call_target="tpu_custom_call" | custom-call | flops 503316480 | bytes 12000000 | tf_op jit(solution)/shard_map/pallas_call | solution.py:51
  89.8 3.1 %collective-permute-start.14 = (bf16[2,128,1280]{2,1,0:T(8,128)(2,1)S(1)}, bf16[2,128,1280]{2,1,0:T(8,128)(2,1)S(1)}, u32[]{:S(2)}, u32[]{:S(2)}) collective-permute-start(bf16[2,128,1280]{2,1,0:T(8,128)(2,1)S(1)} %get-tuple-element.53), channel_id=1, source_target_pairs={{0,8},{1,9},{2,10},{3,11},{4,12},{5,13},{6,14},{7,15},{8,16},{9,17... | collective-permute-start | bytes 1966088 | tf_op jit(solution)/shard_map/ppermute | solution.py:342
  94.2 3.5 %shard_map.90 = (f32[128,2560]{1,0:T(8,128)S(1)}, bf16[128,2560]{1,0:T(8,128)(2,1)S(1)}) custom-call(bf16[1280,2560]{1,0:T(8,128)(2,1)S(1)} %get-tuple-element.39.w_ref, bf16[128,1280]{1,0:T(8,128)(2,1)S(1)} %get-tuple-element.46.mine_ref, bf16[128,1280]{1,0:T(8,128)(2,1)S(1)} %collective-permute-done.11.theirs_ref), custom_call_target="tpu_custom_call" | custom-call | flops 1677721600 | bytes 9000000 | tf_op jit(solution)/shard_map/pallas_call | solution.py:51
  97.6 5.1 %collective-permute-start.12 = (bf16[128,2560]{1,0:T(8,128)(2,1)S(1)}, bf16[128,2560]{1,0:T(8,128)(2,1)S(1)}, u32[]{:S(2)}, u32[]{:S(2)}) collective-permute-start(bf16[128,2560]{1,0:T(8,128)(2,1)S(1)} %get-tuple-element.49), channel_id=1, source_target_pairs={{0,144},{1,145},{2,146},{3,147},{4,148},{5,149},{6,150},{7,151},{8... | collective-permute-start | bytes 1966088 | tf_op jit(solution)/shard_map/ppermute | solution.py:342
  102.8 3.9 %collective-permute-start.20 = (bf16[2,64,1280]{2,1,0:T(8,128)(2,1)S(1)}, bf16[2,64,1280]{2,1,0:T(8,128)(2,1)S(1)}, u32[]{:S(2)}, u32[]{:S(2)}) collective-permute-start(bf16[2,64,1280]{2,1,0:T(8,128)(2,1)S(1)} %get-tuple-element.65), channel_id=1, source_target_pairs={{0,1},{1,2},{2,3},{3,4},{4,5},{5,6},{6,7},{8,9},{9,10},{10,11},{11... | collective-permute-start | bytes 983048 | tf_op jit(solution)/shard_map/ppermute | solution.py:342
  106.8 1.9 %collective-permute-start.21 = (bf16[2,64,1280]{2,1,0:T(8,128)(2,1)S(1)}, bf16[2,64,1280]{2,1,0:T(8,128)(2,1)S(1)}, u32[]{:S(2)}, u32[]{:S(2)}) collective-permute-start(bf16[2,64,1280]{2,1,0:T(8,128)(2,1)S(1)} %get-tuple-element.66), channel_id=1, source_target_pairs={{1,0},{2,1},{3,2},{4,3},{5,4},{6,5},{7,6},{9,8},{10,9},{11,10},{12... | collective-permute-start | bytes 983048 | tf_op jit(solution)/shard_map/ppermute | solution.py:342
  108.8 5.1 %collective-permute-start.16 = (bf16[2,64,1280]{2,1,0:T(8,128)(2,1)S(1)}, bf16[2,64,1280]{2,1,0:T(8,128)(2,1)S(1)}, u32[]{:S(2)}, u32[]{:S(2)}) collective-permute-start(bf16[2,64,1280]{2,1,0:T(8,128)(2,1)S(1)} %get-tuple-element.56), channel_id=1, source_target_pairs={{0,1},{1,2},{2,3},{3,4},{4,5},{5,6},{6,7},{8,9},{9,10},{10,11},{11... | collective-permute-start | bytes 983048 | tf_op jit(solution)/shard_map/ppermute | solution.py:342
  114.0 1.9 %collective-permute-start.17 = (bf16[2,64,1280]{2,1,0:T(8,128)(2,1)S(1)}, bf16[2,64,1280]{2,1,0:T(8,128)(2,1)S(1)}, u32[]{:S(2)}, u32[]{:S(2)}) collective-permute-start(bf16[2,64,1280]{2,1,0:T(8,128)(2,1)S(1)} %get-tuple-element.57), channel_id=1, source_target_pairs={{1,0},{2,1},{3,2},{4,3},{5,4},{6,5},{7,6},{9,8},{10,9},{11,10},{12... | collective-permute-start | bytes 983048 | tf_op jit(solution)/shard_map/ppermute | solution.py:342
  115.9 2.2 %collective-permute-done.12 = bf16[128,2560]{1,0:T(8,128)(2,1)S(1)} collective-permute-done((bf16[128,2560]{1,0:T(8,128)(2,1)S(1)}, bf16[128,2560]{1,0:T(8,128)(2,1)S(1)}, u32[]{:S(2)}, u32[]{:S(2)}) %collective-permute-start.12) | collective-permute-done | bytes 655392 | tf_op jit(solution)/shard_map/ppermute | solution.py:342
  120.1 4.9 %collective-permute-done.17.hi_ref = bf16[2,64,1280]{2,1,0:T(8,128)(2,1)S(1)} collective-permute-done((bf16[2,64,1280]{2,1,0:T(8,128)(2,1)S(1)}, bf16[2,64,1280]{2,1,0:T(8,128)(2,1)S(1)}, u32[]{:S(2)}, u32[]{:S(2)}) %collective-permute-start.17) | collective-permute-done | bytes 327712 | tf_op jit(solution)/shard_map/ppermute | solution.py:342
  (45 shorter events, 15.4 us)
Async XLA Ops:
  0.6 23.1 %copy-start = (bf16[1,4,4,8,2560]{4,3,2,1,0:T(8,128)(2,1)S(1)}, bf16[1,4,4,8,2560]{4,3,2,1,0:T(8,128)(2,1)}, u32[]{:S(2)}) copy-start(bf16[1,4,4,8,2560]{4,3,2,1,0:T(8,128)(2,1)} %param.6) | copy-start | bytes 1966084
  0.7 21.4 %collective-permute-start = (bf16[320,2560]{1,0:T(8,128)(2,1)}, bf16[320,2560]{1,0:T(8,128)(2,1)S(1)}, u32[]{:S(2)}, u32[]{:S(2)}) collective-permute-start(bf16[320,2560]{1,0:T(8,128)(2,1)} %own_ref.1), channel_id=1, source_target_pairs={{0,32},{1,33},{2,34},{3,35},{4,36},{5,37},{6,38},{7,39},{8,104},{9... | collective-permute-start | bytes 4915208 | tf_op jit(solution)/shard_map/ppermute | solution.py:342
  22.1 31.3 %collective-permute-start.1 = (bf16[320,2560]{1,0:T(8,128)(2,1)S(1)}, bf16[320,2560]{1,0:T(8,128)(2,1)}, u32[]{:S(2)}, u32[]{:S(2)}) collective-permute-start(bf16[320,2560]{1,0:T(8,128)(2,1)S(1)} %collective-permute-done.near_ref), channel_id=1, source_target_pairs={{0,8},{1,9},{2,10},{3,11},{4,12},{5,13},{6,14},{7,15},{8,0},{9,1},... | collective-permute-start | bytes 4915208 | tf_op jit(solution)/shard_map/ppermute | solution.py:342
  22.1 12.4 %collective-permute-start.2 = (bf16[160,2560]{1,0:T(8,128)(2,1)S(1)}, bf16[160,2560]{1,0:T(8,128)(2,1)S(1)}, u32[]{:S(2)}, u32[]{:S(2)}) collective-permute-start(bf16[160,2560]{1,0:T(8,128)(2,1)S(1)} %constant_dynamic-slice_fusion), channel_id=1, source_target_pairs={{0,32},{1,33},{2,34},{3,35},{4,36},{5,37},{6,38},{7,39},{8,104},{9... | collective-permute-start | bytes 2457608 | tf_op jit(solution)/shard_map/ppermute | solution.py:342
  23.8 30.9 %copy-start.3 = (bf16[320,2560]{1,0:T(8,128)(2,1)S(1)}, bf16[320,2560]{1,0:T(8,128)(2,1)}, u32[]{:S(2)}) copy-start(bf16[320,2560]{1,0:T(8,128)(2,1)} %own_ref.1) | copy-start | bytes 4915204
  24.0 19.6 %collective-permute-start.5 = (bf16[2,64,2560]{2,1,0:T(8,128)(2,1)S(1)}, bf16[2,64,2560]{2,1,0:T(8,128)(2,1)S(1)}, u32[]{:S(2)}, u32[]{:S(2)}) collective-permute-start(bf16[2,64,2560]{2,1,0:T(8,128)(2,1)S(1)} %get-tuple-element.40), channel_id=1, source_target_pairs={{0,1},{1,2},{2,3},{3,4},{4,5},{5,6},{6,7},{8,9},{9,10},{10,11},{11... | collective-permute-start | bytes 1966088 | tf_op jit(solution)/shard_map/ppermute | solution.py:342
  29.1 19.8 %collective-permute-start.6 = (bf16[2,64,2560]{2,1,0:T(8,128)(2,1)S(1)}, bf16[2,64,2560]{2,1,0:T(8,128)(2,1)S(1)}, u32[]{:S(2)}, u32[]{:S(2)}) collective-permute-start(bf16[2,64,2560]{2,1,0:T(8,128)(2,1)S(1)} %get-tuple-element.41), channel_id=1, source_target_pairs={{1,0},{2,1},{3,2},{4,3},{5,4},{6,5},{7,6},{9,8},{10,9},{11,10},{12... | collective-permute-start | bytes 1966088 | tf_op jit(solution)/shard_map/ppermute | solution.py:342
  31.1 19.2 %collective-permute-start.4 = (bf16[128,2560]{1,0:T(8,128)(2,1)S(1)}, bf16[128,2560]{1,0:T(8,128)(2,1)S(1)}, u32[]{:S(2)}, u32[]{:S(2)}) collective-permute-start(bf16[128,2560]{1,0:T(8,128)(2,1)S(1)} %bitcast.22), channel_id=1, source_target_pairs={{0,144},{1,145},{2,146},{3,147},{4,148},{5,149},{6,150},{7,151},{8... | collective-permute-start | bytes 1966088 | tf_op jit(solution)/shard_map/ppermute | solution.py:342
  34.5 22.0 %collective-permute-start.3 = (bf16[160,2560]{1,0:T(8,128)(2,1)S(1)}, bf16[160,2560]{1,0:T(8,128)(2,1)S(1)}, u32[]{:S(2)}, u32[]{:S(2)}) collective-permute-start(bf16[160,2560]{1,0:T(8,128)(2,1)S(1)} %collective-permute-done.2.c0_ref), channel_id=1, source_target_pairs={{0,8},{1,9},{2,10},{3,11},{4,12},{5,13},{6,14},{7,15},{8,0},{9,1},... | collective-permute-start | bytes 2457608 | tf_op jit(solution)/shard_map/ppermute | solution.py:342
  43.6 22.7 %collective-permute-start.7 = (bf16[2,64,2560]{2,1,0:T(8,128)(2,1)S(1)}, bf16[2,64,2560]{2,1,0:T(8,128)(2,1)S(1)}, u32[]{:S(2)}, u32[]{:S(2)}) collective-permute-start(bf16[2,64,2560]{2,1,0:T(8,128)(2,1)S(1)} %get-tuple-element.42), channel_id=1, source_target_pairs={{0,8},{1,9},{2,10},{3,11},{4,12},{5,13},{6,14},{7,15},{8,16},{9,17... | collective-permute-start | bytes 1966088 | tf_op jit(solution)/shard_map/ppermute | solution.py:342
  48.9 17.3 %collective-permute-start.9 = (bf16[2,64,2560]{2,1,0:T(8,128)(2,1)S(1)}, bf16[2,64,2560]{2,1,0:T(8,128)(2,1)S(1)}, u32[]{:S(2)}, u32[]{:S(2)}) collective-permute-start(bf16[2,64,2560]{2,1,0:T(8,128)(2,1)S(1)} %get-tuple-element.44), channel_id=1, source_target_pairs={{8,0},{9,1},{10,2},{11,3},{12,4},{13,5},{14,6},{15,7},{16,8},{17,9... | collective-permute-start | bytes 1966088 | tf_op jit(solution)/shard_map/ppermute | solution.py:342
  50.3 15.9 %collective-permute-start.8 = (bf16[2,64,2560]{2,1,0:T(8,128)(2,1)S(1)}, bf16[2,64,2560]{2,1,0:T(8,128)(2,1)S(1)}, u32[]{:S(2)}, u32[]{:S(2)}) collective-permute-start(bf16[2,64,2560]{2,1,0:T(8,128)(2,1)S(1)} %get-tuple-element.43), channel_id=1, source_target_pairs={{0,8},{1,9},{2,10},{3,11},{4,12},{5,13},{6,14},{7,15},{8,16},{9,17... | collective-permute-start | bytes 1966088 | tf_op jit(solution)/shard_map/ppermute | solution.py:342
  53.4 12.9 %collective-permute-start.10 = (bf16[2,64,2560]{2,1,0:T(8,128)(2,1)S(1)}, bf16[2,64,2560]{2,1,0:T(8,128)(2,1)S(1)}, u32[]{:S(2)}, u32[]{:S(2)}) collective-permute-start(bf16[2,64,2560]{2,1,0:T(8,128)(2,1)S(1)} %get-tuple-element.45), channel_id=1, source_target_pairs={{8,0},{9,1},{10,2},{11,3},{12,4},{13,5},{14,6},{15,7},{16,8},{17,9... | collective-permute-start | bytes 1966088 | tf_op jit(solution)/shard_map/ppermute | solution.py:342
  61.6 23.4 %collective-permute-start.13 = (bf16[128,1280]{1,0:T(8,128)(2,1)S(1)}, bf16[128,1280]{1,0:T(8,128)(2,1)S(1)}, u32[]{:S(2)}, u32[]{:S(2)}) collective-permute-start(bf16[128,1280]{1,0:T(8,128)(2,1)S(1)} %get-tuple-element.51), channel_id=1, source_target_pairs={{0,144},{1,145},{2,146},{3,147},{4,148},{5,149},{6,150},{7,151},{8... | collective-permute-start | bytes 983048 | tf_op jit(solution)/shard_map/ppermute | solution.py:342
  70.7 23.5 %collective-permute-start.11 = (bf16[128,1280]{1,0:T(8,128)(2,1)S(1)}, bf16[128,1280]{1,0:T(8,128)(2,1)S(1)}, u32[]{:S(2)}, u32[]{:S(2)}) collective-permute-start(bf16[128,1280]{1,0:T(8,128)(2,1)S(1)} %get-tuple-element.47), channel_id=1, source_target_pairs={{0,144},{1,145},{2,146},{3,147},{4,148},{5,149},{6,150},{7,151},{8... | collective-permute-start | bytes 983048 | tf_op jit(solution)/shard_map/ppermute | solution.py:342
  82.3 20.3 %collective-permute-start.18 = (bf16[2,128,1280]{2,1,0:T(8,128)(2,1)S(1)}, bf16[2,128,1280]{2,1,0:T(8,128)(2,1)S(1)}, u32[]{:S(2)}, u32[]{:S(2)}) collective-permute-start(bf16[2,128,1280]{2,1,0:T(8,128)(2,1)S(1)} %get-tuple-element.62), channel_id=1, source_target_pairs={{0,8},{1,9},{2,10},{3,11},{4,12},{5,13},{6,14},{7,15},{8,16},{9,17... | collective-permute-start | bytes 1966088 | tf_op jit(solution)/shard_map/ppermute | solution.py:342
  83.7 19.0 %collective-permute-start.19 = (bf16[2,128,1280]{2,1,0:T(8,128)(2,1)S(1)}, bf16[2,128,1280]{2,1,0:T(8,128)(2,1)S(1)}, u32[]{:S(2)}, u32[]{:S(2)}) collective-permute-start(bf16[2,128,1280]{2,1,0:T(8,128)(2,1)S(1)} %get-tuple-element.63), channel_id=1, source_target_pairs={{8,0},{9,1},{10,2},{11,3},{12,4},{13,5},{14,6},{15,7},{16,8},{17,9... | collective-permute-start | bytes 1966088 | tf_op jit(solution)/shard_map/ppermute | solution.py:342
  89.8 18.9 %collective-permute-start.14 = (bf16[2,128,1280]{2,1,0:T(8,128)(2,1)S(1)}, bf16[2,128,1280]{2,1,0:T(8,128)(2,1)S(1)}, u32[]{:S(2)}, u32[]{:S(2)}) collective-permute-start(bf16[2,128,1280]{2,1,0:T(8,128)(2,1)S(1)} %get-tuple-element.53), channel_id=1, source_target_pairs={{0,8},{1,9},{2,10},{3,11},{4,12},{5,13},{6,14},{7,15},{8,16},{9,17... | collective-permute-start | bytes 1966088 | tf_op jit(solution)/shard_map/ppermute | solution.py:342
  92.8 15.9 %collective-permute-start.15 = (bf16[2,128,1280]{2,1,0:T(8,128)(2,1)S(1)}, bf16[2,128,1280]{2,1,0:T(8,128)(2,1)S(1)}, u32[]{:S(2)}, u32[]{:S(2)}) collective-permute-start(bf16[2,128,1280]{2,1,0:T(8,128)(2,1)S(1)} %get-tuple-element.54), channel_id=1, source_target_pairs={{8,0},{9,1},{10,2},{11,3},{12,4},{13,5},{14,6},{15,7},{16,8},{17,9... | collective-permute-start | bytes 1966088 | tf_op jit(solution)/shard_map/ppermute | solution.py:342
  97.6 20.5 %collective-permute-start.12 = (bf16[128,2560]{1,0:T(8,128)(2,1)S(1)}, bf16[128,2560]{1,0:T(8,128)(2,1)S(1)}, u32[]{:S(2)}, u32[]{:S(2)}) collective-permute-start(bf16[128,2560]{1,0:T(8,128)(2,1)S(1)} %get-tuple-element.49), channel_id=1, source_target_pairs={{0,144},{1,145},{2,146},{3,147},{4,148},{5,149},{6,150},{7,151},{8... | collective-permute-start | bytes 1966088 | tf_op jit(solution)/shard_map/ppermute | solution.py:342
  102.8 16.3 %collective-permute-start.20 = (bf16[2,64,1280]{2,1,0:T(8,128)(2,1)S(1)}, bf16[2,64,1280]{2,1,0:T(8,128)(2,1)S(1)}, u32[]{:S(2)}, u32[]{:S(2)}) collective-permute-start(bf16[2,64,1280]{2,1,0:T(8,128)(2,1)S(1)} %get-tuple-element.65), channel_id=1, source_target_pairs={{0,1},{1,2},{2,3},{3,4},{4,5},{5,6},{6,7},{8,9},{9,10},{10,11},{11... | collective-permute-start | bytes 983048 | tf_op jit(solution)/shard_map/ppermute | solution.py:342
  106.8 12.3 %collective-permute-start.21 = (bf16[2,64,1280]{2,1,0:T(8,128)(2,1)S(1)}, bf16[2,64,1280]{2,1,0:T(8,128)(2,1)S(1)}, u32[]{:S(2)}, u32[]{:S(2)}) collective-permute-start(bf16[2,64,1280]{2,1,0:T(8,128)(2,1)S(1)} %get-tuple-element.66), channel_id=1, source_target_pairs={{1,0},{2,1},{3,2},{4,3},{5,4},{6,5},{7,6},{9,8},{10,9},{11,10},{12... | collective-permute-start | bytes 983048 | tf_op jit(solution)/shard_map/ppermute | solution.py:342
  108.8 11.3 %collective-permute-start.16 = (bf16[2,64,1280]{2,1,0:T(8,128)(2,1)S(1)}, bf16[2,64,1280]{2,1,0:T(8,128)(2,1)S(1)}, u32[]{:S(2)}, u32[]{:S(2)}) collective-permute-start(bf16[2,64,1280]{2,1,0:T(8,128)(2,1)S(1)} %get-tuple-element.56), channel_id=1, source_target_pairs={{0,1},{1,2},{2,3},{3,4},{4,5},{5,6},{6,7},{8,9},{9,10},{10,11},{11... | collective-permute-start | bytes 983048 | tf_op jit(solution)/shard_map/ppermute | solution.py:342
  114.0 11.0 %collective-permute-start.17 = (bf16[2,64,1280]{2,1,0:T(8,128)(2,1)S(1)}, bf16[2,64,1280]{2,1,0:T(8,128)(2,1)S(1)}, u32[]{:S(2)}, u32[]{:S(2)}) collective-permute-start(bf16[2,64,1280]{2,1,0:T(8,128)(2,1)S(1)} %get-tuple-element.57), channel_id=1, source_target_pairs={{1,0},{2,1},{3,2},{4,3},{5,4},{6,5},{7,6},{9,8},{10,9},{11,10},{12... | collective-permute-start | bytes 983048 | tf_op jit(solution)/shard_map/ppermute | solution.py:342
  (3 other events, 41.8 us)

commit v2 on v1

--- a/solution.py
+++ b/solution.py
@@ -29,8 +29,7 @@
         for t in range(n_tm):
             for h in range(n_h):
                 e, u, g = fn(d, t, h)
-                if 0 <= u < n_tm and 0 <= g < n_h:
-                    pairs.append(((d * n_tm + t) * n_h + h, (e * n_tm + u) * n_h + g))
+                pairs.append(((d * n_tm + t) * n_h + h, (e * n_tm + u) * n_h + g % n_h))
     return pairs
 
 
@@ -46,12 +45,12 @@
     vm = pl.BlockSpec(memory_space=pltpu.VMEM)
     hb = pl.BlockSpec(memory_space=pl.ANY)
     near = [pltpu.with_memory_space_constraint(x, pltpu.VMEM) for x in ins[: len(ins) - hbm_in]]
-    far = list(ins[len(ins) - hbm_in :])
+    far = [pltpu.with_memory_space_constraint(x, pltpu.HBM) for x in ins[len(ins) - hbm_in :]]
     out_specs = [hb if isinstance(o, jax.ShapeDtypeStruct) else vm for o in outs]
     return pl.pallas_call(
         kernel,
         out_shape=tuple(outs),
-        in_specs=[vm] * len(near) + [hb] * len(far),
+        in_specs=[vm] * len(near) + [pl.BlockSpec(memory_space=pltpu.HBM)] * len(far),
         out_specs=tuple(out_specs),
         scratch_shapes=list(scratch),
         input_output_aliases=aliases or {},
@@ -65,11 +64,17 @@
     return mine if kind == "local" else 1 - mine
 
 
+def side_rows(side, count=64):
+    core = lax.axis_index("tm") % 2
+    at = core * count if side == "x" else (1 - core) * count
+    return pl.multiple_of(at, count)
+
+
 def window_bias(zb_ref, tb_ref):
     tm = lax.axis_index("tm")
     ht = lax.axis_index("height")
-    t_lo = jnp.where(tm > 0, 1, 0)
-    t_hi = jnp.where(tm < lax.axis_size("tm") - 1, 1, 0)
+    last = lax.axis_size("tm") - 1
+    x_ok = jnp.where((tm > 0) & (tm < last), 1, 0)
     z_lo = jnp.where(ht > 0, 1, 0)
     z_hi = jnp.where(ht < lax.axis_size("height") - 1, 1, 0)
     q = lax.broadcasted_iota(jnp.int32, (128, 128), 0)
@@ -78,21 +83,32 @@
     side_ok = jnp.where(late == 0, z_lo, z_hi)
     z_side = jnp.where(k < 64, 0, 1)
     zb_ref[...] = jnp.where((z_side == late) & (side_ok > 0), 0.0, NEG).astype(F32)
-    t_ok = jnp.where(q < 64, t_lo, t_hi)
+    t_ok = jnp.where(q < 64, x_ok, 1)
     corner = jnp.where(k < 96, 0, 1)
     t_in = (k < 64) | ((corner == late) & (side_ok > 0))
     tb_ref[...] = jnp.where(t_in & (t_ok > 0), 0.0, NEG).astype(F32)
 
 
-def key_values(k_ref, v_ref, zl_ref, zh_ref, tl_ref, cl_ref, th_ref, ch_ref, c):
+def key_values(k_ref, v_ref, zl_ref, zh_ref, tx_ref, cx_ref, tc_ref, cc_ref, c):
     cat = lambda *a: jnp.concatenate(a, axis=0)
     k_oz = cat(k_ref[:, c], zl_ref[0, :, c], zh_ref[0, :, c])
     v_oz = cat(v_ref[:, c], zl_ref[1, :, c], zh_ref[1, :, c])
-    k_tl = cat(tl_ref[0, :, c], cl_ref[0, :, c])
-    v_tl = cat(tl_ref[1, :, c], cl_ref[1, :, c])
-    k_th = cat(th_ref[0, :, c], ch_ref[0, :, c])
-    v_th = cat(th_ref[1, :, c], ch_ref[1, :, c])
-    return k_oz, v_oz, k_tl, v_tl, k_th, v_th
+    k_tx = cat(tx_ref[0, :, c], cx_ref[0, :, c])
+    v_tx = cat(tx_ref[1, :, c], cx_ref[1, :, c])
+    k_tc = cat(tc_ref[0, :, c], cc_ref[0, :, c])
+    v_tc = cat(tc_ref[1, :, c], cc_ref[1, :, c])
+    return k_oz, v_oz, k_tx, v_tx, k_tc, v_tc
+
+
+def both_sides(ref, c):
+    return jnp.concatenate(
+        [ref[pl.ds(side_rows("x"), 64), c], ref[pl.ds(side_rows("c"), 64), c]], axis=0
+    )
+
+
+def put_sides(ref, c, value):
+    ref[pl.ds(side_rows("x"), 64), c] = value[:64]
+    ref[pl.ds(side_rows("c"), 64), c] = value[64:]
 
 
 def lanes(head):
@@ -106,10 +122,10 @@
 
     def one(h):
         c = lanes(first + h)
-        q = q_ref[:, c]
-        k_oz, v_oz, k_tl, v_tl, k_th, v_th = key_values(k_ref, v_ref, *halo, c)
+        q = both_sides(q_ref, c)
+        k_oz, v_oz, k_tx, v_tx, k_tc, v_tc = key_values(k_ref, v_ref, *halo, c)
         s_oz = dot(q, k_oz, 1, 1)
-        s_t = jnp.concatenate([dot(q[:64], k_tl, 1, 1), dot(q[64:], k_th, 1, 1)], axis=0)
+        s_t = jnp.concatenate([dot(q[:64], k_tx, 1, 1), dot(q[64:], k_tc, 1, 1)], axis=0)
         s_o = s_oz[:, :128]
         s_z = s_oz[:, 128:] + zb_ref[...]
         s_t = s_t + tb_ref[...]
@@ -122,8 +138,8 @@
         p_t = (e_t * inv).astype(BF16)
         p_ref[h, :, :256] = p_oz
         p_ref[h, :, 256:] = p_t
-        a_t = jnp.concatenate([dot(p_t[:64], v_tl, 1, 0), dot(p_t[64:], v_th, 1, 0)], axis=0)
-        att_ref[:, lanes(h)] = (dot(p_oz, v_oz, 1, 0) + a_t).astype(BF16)
+        a_t = jnp.concatenate([dot(p_t[:64], v_tx, 1, 0), dot(p_t[64:], v_tc, 1, 0)], axis=0)
+        put_sides(att_ref, lanes(h), (dot(p_oz, v_oz, 1, 0) + a_t).astype(BF16))
 
     def step(i, carry):
         for j in range(HPS):
@@ -143,37 +159,37 @@
 
 
 def backward_kernel(kind, q_ref, k_ref, v_ref, *rest):
-    halo, (p_ref, g_ref, dq_ref, own_ref, rim_ref, tlo_ref, thi_ref) = rest[:6], rest[6:]
+    halo, (p_ref, g_ref, dq_ref, own_ref, rim_ref, tx_ref, tc_ref) = rest[:6], rest[6:]
     first = half_of(kind) * HEADS_HALF
 
     def one(h):
         c = lanes(first + h)
         o = lanes(h)
-        q = q_ref[:, c]
-        g = g_ref[:, o]
-        k_oz, v_oz, k_tl, v_tl, k_th, v_th = key_values(k_ref, v_ref, *halo, c)
+        q = both_sides(q_ref, c)
+        g = both_sides(g_ref, o)
+        k_oz, v_oz, k_tx, v_tx, k_tc, v_tc = key_values(k_ref, v_ref, *halo, c)
         p_oz = p_ref[h, :, :256]
         p_t = p_ref[h, :, 256:]
         dp_oz = dot(g, v_oz, 1, 1)
-        dp_t = jnp.concatenate([dot(g[:64], v_tl, 1, 1), dot(g[64:], v_th, 1, 1)], axis=0)
+        dp_t = jnp.concatenate([dot(g[:64], v_tx, 1, 1), dot(g[64:], v_tc, 1, 1)], axis=0)
         w_oz = p_oz.astype(F32)
         w_t = p_t.astype(F32)
         x_oz = w_oz * dp_oz
         row = jnp.sum(x_oz[:, :128] + x_oz[:, 128:] + w_t * dp_t, axis=1, keepdims=True)
         ds_oz = (w_oz * (dp_oz - row) * SCALE).astype(BF16)
         ds_t = (w_t * (dp_t - row) * SCALE).astype(BF16)
-        dq_t = jnp.concatenate([dot(ds_t[:64], k_tl, 1, 0), dot(ds_t[64:], k_th, 1, 0)], axis=0)
-        dq_ref[:, o] = (dot(ds_oz, k_oz, 1, 0) + dq_t).astype(BF16)
+        dq_t = jnp.concatenate([dot(ds_t[:64], k_tx, 1, 0), dot(ds_t[64:], k_tc, 1, 0)], axis=0)
+        put_sides(dq_ref, o, (dot(ds_oz, k_oz, 1, 0) + dq_t).astype(BF16))
         dk_oz = dot(ds_oz, q, 0, 0)
         dv_oz = dot(p_oz, g, 0, 0)
         own_ref[0, :, o] = dk_oz[:128]
         own_ref[1, :, o] = dv_oz[:128]
         rim_ref[0, :, o] = dk_oz[128:]
         rim_ref[1, :, o] = dv_oz[128:]
-        tlo_ref[0, :, o] = dot(ds_t[:64], q[:64], 0, 0).astype(BF16)
-        tlo_ref[1, :, o] = dot(p_t[:64], g[:64], 0, 0).astype(BF16)
-        thi_ref[0, :, o] = dot(ds_t[64:], q[64:], 0, 0).astype(BF16)
-        thi_ref[1, :, o] = dot(p_t[64:], g[64:], 0, 0).astype(BF16)
+        tx_ref[0, :, o] = dot(ds_t[:64], q[:64], 0, 0).astype(BF16)
+        tx_ref[1, :, o] = dot(p_t[:64], g[:64], 0, 0).astype(BF16)
+        tc_ref[0, :, o] = dot(ds_t[64:], q[64:], 0, 0).astype(BF16)
+        tc_ref[1, :, o] = dot(p_t[64:], g[64:], 0, 0).astype(BF16)
 
     def step(i, carry):
         for j in range(HPS):
@@ -225,7 +241,9 @@
 
 
 def gather_rows(own, near, far):
-    return call(gather_kernel, (in_vmem((W_HALF, 2560), BF16),), (own, near, far), moved=10_000_000)[0]
+    return call(
+        gather_kernel, (in_vmem((W_HALF, 2560), BF16),), (own, near, far), moved=10_000_000
+    )[0]
 
 
 def grad_proj_kernel(w_in, c0_ref, c1_ref, mine_ref, theirs_ref, w_ref, o_ref, t_ref):
@@ -268,67 +286,95 @@
     )
 
 
-def rim_kernel(rim_ref, prev_ref, next_ref, lo_ref, hi_ref):
-    for half, out in ((0, lo_ref), (1, hi_ref)):
-        c = slice(64 + 32 * half, 96 + 32 * half)
-        corner = jnp.concatenate([prev_ref[:, c], next_ref[:, c]], axis=1).astype(F32)
-        out[...] = (rim_ref[:, 64 * half : 64 * half + 64] + corner).astype(BF16)
-
-
-def rim_half(rim, from_prev, from_next):
-    return call(
-        rim_kernel, (in_vmem((2, 64, W_HALF), BF16),) * 2, (rim, from_prev, from_next),
+def rim_kernel(rim_ref, fx_ref, fc_ref, lo_ref, hi_ref):
+    for side, src in (("x", fx_ref), ("c", fc_ref)):
+        at = side_rows(side, 32)
+        for half, out in ((0, lo_ref), (1, hi_ref)):
+            corner = src[:, 64 + 32 * half : 96 + 32 * half].astype(F32)
+            here = rim_ref[:, pl.ds(pl.multiple_of(64 * half + at, 32), 32)]
+            out[:, pl.ds(at, 32)] = (here + corner).astype(BF16)
+
+
+def rim_half(rim, from_x, from_c):
+    return call(
+        rim_kernel, (in_vmem((2, 64, W_HALF), BF16),) * 2, (rim, from_x, from_c),
         moved=4_000_000,
     )
 
 
-def final_kernel(kind, own_ref, prev_ref, next_ref, lo_ref, hi_ref, d_ref, *rest):
+def final_kernel(kind, own_ref, fx_ref, fc_ref, lo_ref, hi_ref, d_ref, *rest):
     dk_ref, dv_ref, dq_ref, dk_tile, dv_tile, sems = rest[-6:]
     at = pl.ds(pl.multiple_of(half_of(kind) * W_HALF, W_HALF), W_HALF)
     copies = [pltpu.make_async_copy(d_ref, dq_ref.at[:, at], sems.at[2])]
     copies[0].start()
     for kv, tile, out in ((0, dk_tile, dk_ref), (1, dv_tile, dv_ref)):
-        frames = jnp.concatenate([prev_ref[kv, :64], next_ref[kv, :64]], axis=0).astype(F32)
-        total = own_ref[kv] + frames
-        for f in range(4):
-            low = total[f * 32 : f * 32 + 16] + lo_ref[kv, f * 16 : f * 16 + 16].astype(F32)
-            high = total[f * 32 + 16 : f * 32 + 32] + hi_ref[kv, f * 16 : f * 16 + 16].astype(F32)
-            tile[f * 32 : f * 32 + 16] = low.astype(BF16)
-            tile[f * 32 + 16 : f * 32 + 32] = high.astype(BF16)
+        for side, src in (("x", fx_ref), ("c", fc_ref)):
+            for f in range(2):
+                for n, z_ref in ((0, lo_ref), (1, hi_ref)):
+                    r = pl.ds(pl.multiple_of(side_rows(side) + f * 32 + n * 16, 16), 16)
+                    z = z_ref[kv, pl.ds(pl.multiple_of(side_rows(side, 32) + f * 16, 16), 16)]
+                    t = src[kv, f * 32 + n * 16 : f * 32 + n * 16 + 16]
+                    tile[r] = (own_ref[kv, r] + t.astype(F32) + z.astype(F32)).astype(BF16)
         copies.append(pltpu.make_async_copy(tile, out.at[:, at], sems.at[kv]))
         copies[-1].start()
     for cp in copies:
         cp.wait()
 
 
-def final_half(kind, own, from_prev, from_next, from_lo, from_hi, d_q, *earlier):
+def final_half(kind, own, from_x, from_c, from_lo, from_hi, d_q, *earlier):
     whole = jax.ShapeDtypeStruct((128, 2560), BF16)
     return call(
         functools.partial(final_kernel, kind), (whole,) * 3,
-        (own, from_prev, from_next, from_lo, from_hi, d_q, *earlier), moved=6_000_000,
+        (own, from_x, from_c, from_lo, from_hi, d_q, *earlier), moved=6_000_000,
         scratch=(pltpu.VMEM((128, W_HALF), BF16), pltpu.VMEM((128, W_HALF), BF16), pltpu.SemaphoreType.DMA((3,))),
         aliases={6: 0, 7: 1, 8: 2} if earlier else {}, hbm_in=len(earlier),
     )
 
 
-def prep_kernel(k_ref, v_ref, zlo_ref, zhi_ref, tlo_ref, thi_ref):
+def prep_kernel(k_ref, v_ref, zlo_ref, zhi_ref, tx_ref, tc_ref, sems):
+    copies = []
     for kv, src in ((0, k_ref), (1, v_ref)):
         for f in range(4):
-            zlo_ref[kv, f * 16 : f * 16 + 16] = src[f * 32 : f * 32 + 16]
-            zhi_ref[kv, f * 16 : f * 16 + 16] = src[f * 32 + 16 : f * 32 + 32]
-        tlo_ref[kv] = src[:64]
-        thi_ref[kv] = src[64:]
+            rows = pl.ds(f * 16, 16)
+            copies.append((src.at[pl.ds(f * 32 + 16, 16)], zhi_ref.at[kv, rows]))
+            copies.append((src.at[pl.ds(f * 32, 16)], zlo_ref.at[kv, rows]))
+    for kv, src in ((0, k_ref), (1, v_ref)):
+        copies.append((src.at[pl.ds(side_rows("x"), 64)], tx_ref.at[kv]))
+        copies.append((src.at[pl.ds(side_rows("c"), 64)], tc_ref.at[kv]))
+    copies = [pltpu.make_async_copy(x, y, sems.at[n]) for n, (x, y) in enumerate(copies)]
+    for cp in copies:
+        cp.start()
+    for cp in copies:
+        cp.wait()
 
 
 def prep(keys, values):
-    return call(prep_kernel, (in_vmem((2, 64, 2560), BF16),) * 4, (keys, values), moved=4_000_000)
-
-
-def corner_kernel(lo_ref, hi_ref, down_ref, up_ref):
-    down_ref[:, :32] = lo_ref[:, :32]
-    down_ref[:, 32:] = hi_ref[:, :32]
-    up_ref[:, :32] = lo_ref[:, 32:]
-    up_ref[:, 32:] = hi_ref[:, 32:]
+    return call(
+        prep_kernel, (in_vmem((2, 64, 2560), BF16),) * 4, (keys, values), moved=4_000_000,
+        scratch=(pltpu.SemaphoreType.DMA((20,)),), hbm_in=2,
+    )
+
+
+def slice_kernel(near_ref, part_ref):
+    core = lax.axis_index("tm") % 2
+
+    def step(i, carry):
+        r = pl.multiple_of(i * 32, 32)
+        part_ref[pl.ds(r, 32), :] = near_ref[pl.ds(pl.multiple_of(core * 160 + r, 32), 32), :]
+        return carry
+
+    lax.fori_loop(0, 5, step, 0)
+
+
+def add_kernel(part_ref, remote_ref, out_ref):
+    out_ref[...] = (part_ref[...] + remote_ref[...].astype(F32)).astype(BF16)
+
+
+def corner_kernel(lo_ref, hi_ref, cx_ref, cc_ref):
+    for side, out in (("x", cx_ref), ("c", cc_ref)):
+        r = pl.ds(side_rows(side, 32), 32)
+        out[:, :32] = lo_ref[:, r]
+        out[:, 32:] = hi_ref[:, r]
 
 
 def corners(z_lo, z_hi):
@@ -346,8 +392,9 @@
     ring_y = lambda d, t, h: ((d & 4) | ((d + (1 if t % 2 == 0 else 3)) & 3), t, h)
     up_z = lambda d, t, h: (d, t, h + 1)
     down_z = lambda d, t, h: (d, t, h - 1)
-    up_t = lambda d, t, h: (d, t + 1, h)
-    down_t = lambda d, t, h: (d, t - 1, h)
+    other_chip = lambda d, t, h: (d, 3 - t, h) if t in (1, 2) else (d ^ 4, 3 - t, h)
+    other_chip_mid = lambda d, t, h: (d, 3 - t, h) if t in (1, 2) else (d, t, h ^ 1)
+    other_chip_late = lambda d, t, h: (d, 3 - t, h) if t in (1, 2) else (d ^ 1, t, h)
 
     tokens = queries.shape[1] * queries.shape[2] * queries.shape[3]
     flat = lambda a: a.reshape(tokens, a.shape[-1])
@@ -355,21 +402,21 @@
 
     w_near = send(projection, ring_y)
     their_d_out = send(d_out, pair_chip)
-    z_lo_s, z_hi_s, t_lo_s, t_hi_s = prep(k, v)
+    z_lo_s, z_hi_s, tx_s, tc_s = prep(k, v)
     z_lo = send(z_hi_s, up_z)
     z_hi = send(z_lo_s, down_z)
-    t_lo = send(t_hi_s, up_t)
-    t_hi = send(t_lo_s, down_t)
-    c_down, c_up = corners(z_lo, z_hi)
-    c_lo = send(c_up, up_t)
-    c_hi = send(c_down, down_t)
+    t_x = send(tx_s, other_chip)
+    t_c = send(tc_s, other_core)
+    cx_s, cc_s = corners(z_lo, z_hi)
+    c_x = send(cx_s, other_chip_mid)
+    c_c = send(cc_s, other_core)
     w_far = send(w_near, other_core)
-    core = lax.axis_index("tm") % 2
-    w_c0 = send(lax.dynamic_slice_in_dim(w_near, core * 160, 160, 0), ring_y)
+    (w_part,) = call(slice_kernel, (in_vmem((160, 2560), BF16),), (w_near,))
+    w_c0 = send(w_part, ring_y)
     w_c1 = send(w_c0, other_core)
     rows = gather_rows(projection, w_near, w_far)
 
-    operands = (q, k, v, z_lo, z_hi, t_lo, c_lo, t_hi, c_hi)
+    operands = (q, k, v, z_lo, z_hi, t_x, c_x, t_c, c_c)
     att_remote, p_remote = forward_half("remote", operands)
     their_att = send(att_remote, pair_chip)
     att_local, p_local = forward_half("local", operands)
@@ -377,26 +424,26 @@
     rows, g_local, g_theirs = grad_proj(rows, w_c0, w_c1, d_out, their_d_out)
     g_remote = send(g_theirs, pair_chip)
 
-    dq_a, own_a, rim_a, tlo_a, thi_a = backward_half("local", operands, p_local, g_local)
-    prev_a = send(thi_a, up_t)
-    next_a = send(tlo_a, down_t)
-    dq_b, own_b, rim_b, tlo_b, thi_b = backward_half("remote", operands, p_remote, g_remote)
-    prev_b = send(thi_b, up_t)
-    next_b = send(tlo_b, down_t)
+    dq_a, own_a, rim_a, tx_a, tc_a = backward_half("local", operands, p_local, g_local)
+    fx_a = send(tx_a, other_chip_late)
+    fc_a = send(tc_a, other_core)
+    dq_b, own_b, rim_b, tx_b, tc_b = backward_half("remote", operands, p_remote, g_remote)
+    fx_b = send(tx_b, other_chip_late)
+    fc_b = send(tc_b, other_core)
 
     part, part_theirs = out_proj(rows, att_local, their_att)
     part_remote = send(part_theirs, pair_chip)
 
-    rlo_a, rhi_a = rim_half(rim_a, prev_a, next_a)
+    rlo_a, rhi_a = rim_half(rim_a, fx_a, fc_a)
     from_lo_a = send(rhi_a, up_z)
     from_hi_a = send(rlo_a, down_z)
-    rlo_b, rhi_b = rim_half(rim_b, prev_b, next_b)
+    rlo_b, rhi_b = rim_half(rim_b, fx_b, fc_b)
     from_lo_b = send(rhi_b, up_z)
     from_hi_b = send(rlo_b, down_z)
 
-    outputs = (part + part_remote.astype(F32)).astype(BF16)
-    done = final_half("local", own_a, prev_a, next_a, from_lo_a, from_hi_a, dq_a)
-    dk, dv, dq = final_half("remote", own_b, prev_b, next_b, from_lo_b, from_hi_b, dq_b, *done)
+    (outputs,) = call(add_kernel, (pltpu.HBM((128, 2560), BF16),), (part, part_remote))
+    done = final_half("local", own_a, fx_a, fc_a, from_lo_a, from_hi_a, dq_a)
+    dk, dv, dq = final_half("remote", own_b, fx_b, fc_b, from_lo_b, from_hi_b, dq_b, *done)
     return (
         outputs.reshape(d_outputs.shape),
         dq.reshape(queries.shape),

time: 126 us -> 113 us (0.90)
  the two profiles are of different devices: /device:TPU:104 before, /device:TPU:1 now
where the time goes in v2:
time: 113 us
  waiting for transfers between devices  44.4 us (39%)
  starting transfers between devices  34.5 us (31%)
  Pallas kernels  32.6 us (29%)
    ppermute x22, waiting for transfers between devices, send(): return lax.ppermute(x, AXES, make_perm(shape, fn))  44.4 us
    ppermute x22, starting transfers between devices, send(): return lax.ppermute(x, AXES, make_perm(shape, fn))  34.5 us
    pallas_call x15, Pallas kernels, call(): pl.pallas_call(kernel, out_shape=tuple(outs), in_specs=[vm] * len(near) +...  32.6 us
  transfers between devices with their start and end apart: 22, of which 7 were waited for; matrix products, arithmetic and copies ran while one was open for 0% of the time, Pallas kernels for 28%

profile of v2, /device:TPU:1, one launch (start us, length us, event | category | flops | bytes accessed | tf_op | source)
XLA Modules:
  0.0 112.5 jit_solution(15688692584237472786)
XLA Ops:
  0.6 3.6 %collective-permute-start = (bf16[320,2560]{1,0:T(8,128)(2,1)}, bf16[320,2560]{1,0:T(8,128)(2,1)S(1)}, u32[]{:S(2)}, u32[]{:S(2)}) collective-permute-start(bf16[320,2560]{1,0:T(8,128)(2,1)} %own_ref.1), channel_id=1, source_target_pairs={{0,32},{1,33},{2,34},{3,35},{4,36},{5,37},{6,38},{7,39},{8,104},{9... | collective-permute-start | bytes 4915208 | tf_op jit(solution)/shard_map/ppermute | solution.py:388
  4.3 18.4 %collective-permute-done.near_ref = bf16[320,2560]{1,0:T(8,128)(2,1)S(1)} collective-permute-done((bf16[320,2560]{1,0:T(8,128)(2,1)}, bf16[320,2560]{1,0:T(8,128)(2,1)S(1)}, u32[]{:S(2)}, u32[]{:S(2)}) %collective-permute-start) | collective-permute-done | bytes 1638432 | tf_op jit(solution)/shard_map/ppermute | solution.py:388
  22.6 3.8 %collective-permute-start.1 = (bf16[320,2560]{1,0:T(8,128)(2,1)S(1)}, bf16[320,2560]{1,0:T(8,128)(2,1)S(1)}, u32[]{:S(2)}, u32[]{:S(2)}) collective-permute-start(bf16[320,2560]{1,0:T(8,128)(2,1)S(1)} %collective-permute-done.near_ref), channel_id=1, source_target_pairs={{0,8},{1,9},{2,10},{3,11},{4,12},{5,13},{6,14},{7,15},{8,0},{9,1},... | collective-permute-start | bytes 4915208 | tf_op jit(solution)/shard_map/ppermute | solution.py:388
  26.6 2.0 %shard_map.87 = (bf16[2,64,2560]{2,1,0:T(8,128)(2,1)S(1)}, bf16[2,64,2560]{2,1,0:T(8,128)(2,1)S(1)}, bf16[2,64,2560]{2,1,0:T(8,128)(2,1)S(1)}, bf16[2,64,2560]{2,1,0:T(8,128)(2,1)S(1)}) custom-call(bf16[128,2560]{1,0:T(8,128)(2,1)} %bitcast.8, bf16[128,2560]{1,0:T(8,128)(2,1)} %bitcast.13), custom_call_target="tpu_custom_call" | custom-call | bytes 4000000 | tf_op jit(solution)/shard_map/pallas_call | solution.py:50
  28.7 1.4 %collective-permute-start.5 = (bf16[2,64,2560]{2,1,0:T(8,128)(2,1)S(1)}, bf16[2,64,2560]{2,1,0:T(8,128)(2,1)S(1)}, u32[]{:S(2)}, u32[]{:S(2)}) collective-permute-start(bf16[2,64,2560]{2,1,0:T(8,128)(2,1)S(1)} %get-tuple-element.40), channel_id=1, source_target_pairs={{0,1},{1,2},{2,3},{3,4},{4,5},{5,6},{6,7},{7,0},{8,9},{9,10},{10,1... | collective-permute-start | bytes 1966088 | tf_op jit(solution)/shard_map/ppermute | solution.py:388
  30.1 4.0 %collective-permute-start.6 = (bf16[2,64,2560]{2,1,0:T(8,128)(2,1)S(1)}, bf16[2,64,2560]{2,1,0:T(8,128)(2,1)S(1)}, u32[]{:S(2)}, u32[]{:S(2)}) collective-permute-start(bf16[2,64,2560]{2,1,0:T(8,128)(2,1)S(1)} %get-tuple-element.41), channel_id=1, source_target_pairs={{0,7},{1,0},{2,1},{3,2},{4,3},{5,4},{6,5},{7,6},{8,15},{9,8},{10,9... | collective-permute-start | bytes 1966088 | tf_op jit(solution)/shard_map/ppermute | solution.py:388
  34.1 2.5 %collective-permute-start.4 = (bf16[128,2560]{1,0:T(8,128)(2,1)S(1)}, bf16[128,2560]{1,0:T(8,128)(2,1)S(1)}, u32[]{:S(2)}, u32[]{:S(2)}) collective-permute-start(bf16[128,2560]{1,0:T(8,128)(2,1)S(1)} %bitcast.22), channel_id=1, source_target_pairs={{0,144},{1,145},{2,146},{3,147},{4,148},{5,149},{6,150},{7,151},{8... | collective-permute-start | bytes 1966088 | tf_op jit(solution)/shard_map/ppermute | solution.py:388
  36.6 1.5 %collective-permute-done.2.c0_ref = bf16[160,2560]{1,0:T(8,128)(2,1)S(1)} collective-permute-done((bf16[160,2560]{1,0:T(8,128)(2,1)S(1)}, bf16[160,2560]{1,0:T(8,128)(2,1)S(1)}, u32[]{:S(2)}, u32[]{:S(2)}) %collective-permute-start.2) | collective-permute-done | bytes 819232 | tf_op jit(solution)/shard_map/ppermute | solution.py:388
  38.1 2.1 %collective-permute-start.3 = (bf16[160,2560]{1,0:T(8,128)(2,1)S(1)}, bf16[160,2560]{1,0:T(8,128)(2,1)S(1)}, u32[]{:S(2)}, u32[]{:S(2)}) collective-permute-start(bf16[160,2560]{1,0:T(8,128)(2,1)S(1)} %collective-permute-done.2.c0_ref), channel_id=1, source_target_pairs={{0,8},{1,9},{2,10},{3,11},{4,12},{5,13},{6,14},{7,15},{8,0},{9,1},... | collective-permute-start | bytes 2457608 | tf_op jit(solution)/shard_map/ppermute | solution.py:388
  40.2 8.2 %collective-permute-done.5.lo_ref.rest_0_ = bf16[2,64,2560]{2,1,0:T(8,128)(2,1)S(1)} collective-permute-done((bf16[2,64,2560]{2,1,0:T(8,128)(2,1)S(1)}, bf16[2,64,2560]{2,1,0:T(8,128)(2,1)S(1)}, u32[]{:S(2)}, u32[]{:S(2)}) %collective-permute-start.5) | collective-permute-done | bytes 655392 | tf_op jit(solution)/shard_map/ppermute | solution.py:388
  48.9 2.3 %collective-permute-start.9 = (bf16[2,64,2560]{2,1,0:T(8,128)(2,1)S(1)}, bf16[2,64,2560]{2,1,0:T(8,128)(2,1)S(1)}, u32[]{:S(2)}, u32[]{:S(2)}) collective-permute-start(bf16[2,64,2560]{2,1,0:T(8,128)(2,1)S(1)} %get-tuple-element.44), channel_id=1, source_target_pairs={{0,8},{1,9},{2,10},{3,11},{4,12},{5,13},{6,14},{7,15},{8,0},{9,1},... | collective-permute-start | bytes 1966088 | tf_op jit(solution)/shard_map/ppermute | solution.py:388
  52.2 5.0 %shard_map.86 = (bf16[1280,2560]{1,0:T(8,128)(2,1)S(1)}, bf16[128,1280]{1,0:T(8,128)(2,1)S(1)}, bf16[128,1280]{1,0:T(8,128)(2,1)S(1)}) custom-call(bf16[1280,2560]{1,0:T(8,128)(2,1)S(1)} %shard_map.84.w_in, bf16[160,2560]{1,0:T(8,128)(2,1)S(1)} %collective-permute-done.2.c0_ref, ...), custom_call_target="tpu_custom_call", output_to_operand_aliasing={{0}: (0, {})} | custom-call | flops 1677721600 | bytes 9000000 | tf_op jit(solution)/shard_map/pallas_call | solution.py:50
  57.2 2.6 %collective-permute-start.13 = (bf16[128,1280]{1,0:T(8,128)(2,1)S(1)}, bf16[128,1280]{1,0:T(8,128)(2,1)S(1)}, u32[]{:S(2)}, u32[]{:S(2)}) collective-permute-start(bf16[128,1280]{1,0:T(8,128)(2,1)S(1)} %get-tuple-element.51), channel_id=1, source_target_pairs={{0,144},{1,145},{2,146},{3,147},{4,148},{5,149},{6,150},{7,151},{8... | collective-permute-start | bytes 983048 | tf_op jit(solution)/shard_map/ppermute | solution.py:388
  59.8 6.0 %collective-permute-done.8.rest_3_ = bf16[2,64,2560]{2,1,0:T(8,128)(2,1)S(1)} collective-permute-done((bf16[2,64,2560]{2,1,0:T(8,128)(2,1)S(1)}, bf16[2,64,2560]{2,1,0:T(8,128)(2,1)S(1)}, u32[]{:S(2)}, u32[]{:S(2)}) %collective-permute-start.8) | collective-permute-done | bytes 655392 | tf_op jit(solution)/shard_map/ppermute | solution.py:388
  65.7 4.4 %shard_map.90 = (bf16[128,1280]{1,0:T(8,128)(2,1)S(1)}, bf16[10,128,384]{2,1,0:T(8,128)(2,1)S(1)}) custom-call(bf16[128,2560]{1,0:T(8,128)(2,1)S(1)} %bitcast.18, bf16[128,2560]{1,0:T(8,128)(2,1)S(1)} %bitcast.9, bf16[128,2560]{1,0:T(8,128)(2,1)S(1)} %bitcast.14, bf16[2,64,2560]{2,1,0:T(8,128)(2,1)S(1)} %collective-permute-done.5.lo_ref.rest_0_, ...), custom_call_target="tpu_custom_call" | custom-call | flops 251658240 | bytes 6000000 | tf_op jit(solution)/shard_map/pallas_call | solution.py:50
  70.3 4.4 %shard_map.89 = (bf16[128,1280]{1,0:T(8,128)(2,1)S(1)}, bf16[10,128,384]{2,1,0:T(8,128)(2,1)S(1)}) custom-call(bf16[128,2560]{1,0:T(8,128)(2,1)S(1)} %bitcast.19, bf16[128,2560]{1,0:T(8,128)(2,1)S(1)} %bitcast.10, bf16[128,2560]{1,0:T(8,128)(2,1)S(1)} %bitcast.15, bf16[2,64,2560]{2,1,0:T(8,128)(2,1)S(1)} %collective-permute-done.5.lo_ref.rest_0_, ...), custom_call_target="tpu_custom_call" | custom-call | flops 251658240 | bytes 6000000 | tf_op jit(solution)/shard_map/pallas_call | solution.py:50
  74.7 4.8 %shard_map.95 = (bf16[128,1280]{1,0:T(8,128)(2,1)S(1)}, f32[2,128,1280]{2,1,0:T(8,128)S(1)}, f32[2,128,1280]{2,1,0:T(8,128)S(1)}, bf16[2,128,1280]{2,1,0:T(8,128)(2,1)S(1)}, bf16[2,128,1280]{2,1,0:T(8,128)(2,1)S(1)}) custom-call(bf16[128,2560]{1,0:T(8,128)(2,1)S(1)} %bitcast.20, bf16[128,2560]{1,0:T(8,128)(2,1)S(1)} %bitcast.11, ...), custom_call_target="tpu_custom_call" | custom-call | flops 503316480 | bytes 12000000 | tf_op jit(solution)/shard_map/pallas_call | solution.py:50
  79.8 3.8 %collective-permute-start.19 = (bf16[2,128,1280]{2,1,0:T(8,128)(2,1)S(1)}, bf16[2,128,1280]{2,1,0:T(8,128)(2,1)S(1)}, u32[]{:S(2)}, u32[]{:S(2)}) collective-permute-start(bf16[2,128,1280]{2,1,0:T(8,128)(2,1)S(1)} %get-tuple-element.63), channel_id=1, source_target_pairs={{0,8},{1,9},{2,10},{3,11},{4,12},{5,13},{6,14},{7,15},{8,0},{9,1},... | collective-permute-start | bytes 1966088 | tf_op jit(solution)/shard_map/ppermute | solution.py:388
  83.6 4.7 %shard_map.93 = (bf16[128,1280]{1,0:T(8,128)(2,1)S(1)}, f32[2,128,1280]{2,1,0:T(8,128)S(1)}, f32[2,128,1280]{2,1,0:T(8,128)S(1)}, bf16[2,128,1280]{2,1,0:T(8,128)(2,1)S(1)}, bf16[2,128,1280]{2,1,0:T(8,128)(2,1)S(1)}) custom-call(bf16[128,2560]{1,0:T(8,128)(2,1)S(1)} %bitcast.21, bf16[128,2560]{1,0:T(8,128)(2,1)S(1)} %bitcast.12, ...), custom_call_target="tpu_custom_call" | custom-call | flops 503316480 | bytes 12000000 | tf_op jit(solution)/shard_map/pallas_call | solution.py:50
  88.7 3.5 %shard_map.91 = (f32[128,2560]{1,0:T(8,128)S(1)}, bf16[128,2560]{1,0:T(8,128)(2,1)S(1)}) custom-call(bf16[1280,2560]{1,0:T(8,128)(2,1)S(1)} %get-tuple-element.39.w_ref, bf16[128,1280]{1,0:T(8,128)(2,1)S(1)} %get-tuple-element.46.mine_ref, bf16[128,1280]{1,0:T(8,128)(2,1)S(1)} %collective-permute-done.11.theirs_ref), custom_call_target="tpu_custom_call" | custom-call | flops 1677721600 | bytes 9000000 | tf_op jit(solution)/shard_map/pallas_call | solution.py:50
  93.6 2.7 %collective-permute-start.21 = (bf16[2,64,1280]{2,1,0:T(8,128)(2,1)S(1)}, bf16[2,64,1280]{2,1,0:T(8,128)(2,1)S(1)}, u32[]{:S(2)}, u32[]{:S(2)}) collective-permute-start(bf16[2,64,1280]{2,1,0:T(8,128)(2,1)S(1)} %get-tuple-element.66), channel_id=1, source_target_pairs={{0,7},{1,0},{2,1},{3,2},{4,3},{5,4},{6,5},{7,6},{8,15},{9,8},{10,9... | collective-permute-start | bytes 983048 | tf_op jit(solution)/shard_map/ppermute | solution.py:388
  96.3 2.6 %collective-permute-done.14.fx_ref = bf16[2,128,1280]{2,1,0:T(8,128)(2,1)S(1)} collective-permute-done((bf16[2,128,1280]{2,1,0:T(8,128)(2,1)S(1)}, bf16[2,128,1280]{2,1,0:T(8,128)(2,1)S(1)}, u32[]{:S(2)}, u32[]{:S(2)}) %collective-permute-start.14) | collective-permute-done | bytes 655392 | tf_op jit(solution)/shard_map/ppermute | solution.py:388
  99.1 2.7 %collective-permute-start.17 = (bf16[2,64,1280]{2,1,0:T(8,128)(2,1)S(1)}, bf16[2,64,1280]{2,1,0:T(8,128)(2,1)S(1)}, u32[]{:S(2)}, u32[]{:S(2)}) collective-permute-start(bf16[2,64,1280]{2,1,0:T(8,128)(2,1)S(1)} %get-tuple-element.57), channel_id=1, source_target_pairs={{0,7},{1,0},{2,1},{3,2},{4,3},{5,4},{6,5},{7,6},{8,15},{9,8},{10,9... | collective-permute-start | bytes 983048 | tf_op jit(solution)/shard_map/ppermute | solution.py:388
  101.8 7.6 %collective-permute-done.12.remote_ref = bf16[128,2560]{1,0:T(8,128)(2,1)S(1)} collective-permute-done((bf16[128,2560]{1,0:T(8,128)(2,1)S(1)}, bf16[128,2560]{1,0:T(8,128)(2,1)S(1)}, u32[]{:S(2)}, u32[]{:S(2)}) %collective-permute-start.12) | collective-permute-done | bytes 655392 | tf_op jit(solution)/shard_map/ppermute | solution.py:388
  (45 shorter events, 7.0 us)
Async XLA Ops:
  0.6 33.5 %copy-start.4 = (bf16[1,4,4,8,2560]{4,3,2,1,0:T(8,128)(2,1)S(1)}, bf16[1,4,4,8,2560]{4,3,2,1,0:T(8,128)(2,1)}, u32[]{:S(2)}) copy-start(bf16[1,4,4,8,2560]{4,3,2,1,0:T(8,128)(2,1)} %param.9) | copy-start | bytes 1966084
  0.6 22.0 %collective-permute-start = (bf16[320,2560]{1,0:T(8,128)(2,1)}, bf16[320,2560]{1,0:T(8,128)(2,1)S(1)}, u32[]{:S(2)}, u32[]{:S(2)}) collective-permute-start(bf16[320,2560]{1,0:T(8,128)(2,1)} %own_ref.1), channel_id=1, source_target_pairs={{0,32},{1,33},{2,34},{3,35},{4,36},{5,37},{6,38},{7,39},{8,104},{9... | collective-permute-start | bytes 4915208 | tf_op jit(solution)/shard_map/ppermute | solution.py:388
  22.6 29.0 %collective-permute-start.1 = (bf16[320,2560]{1,0:T(8,128)(2,1)S(1)}, bf16[320,2560]{1,0:T(8,128)(2,1)S(1)}, u32[]{:S(2)}, u32[]{:S(2)}) collective-permute-start(bf16[320,2560]{1,0:T(8,128)(2,1)S(1)} %collective-permute-done.near_ref), channel_id=1, source_target_pairs={{0,8},{1,9},{2,10},{3,11},{4,12},{5,13},{6,14},{7,15},{8,0},{9,1},... | collective-permute-start | bytes 4915208 | tf_op jit(solution)/shard_map/ppermute | solution.py:388
  26.5 25.2 %copy-start.3 = (bf16[320,2560]{1,0:T(8,128)(2,1)S(1)}, bf16[320,2560]{1,0:T(8,128)(2,1)}, u32[]{:S(2)}) copy-start(bf16[320,2560]{1,0:T(8,128)(2,1)} %own_ref.1) | copy-start | bytes 4915204
  26.5 11.6 %collective-permute-start.2 = (bf16[160,2560]{1,0:T(8,128)(2,1)S(1)}, bf16[160,2560]{1,0:T(8,128)(2,1)S(1)}, u32[]{:S(2)}, u32[]{:S(2)}) collective-permute-start(bf16[160,2560]{1,0:T(8,128)(2,1)S(1)} %shard_map.85), channel_id=1, source_target_pairs={{0,32},{1,33},{2,34},{3,35},{4,36},{5,37},{6,38},{7,39},{8,104},{9... | collective-permute-start | bytes 2457608 | tf_op jit(solution)/shard_map/ppermute | solution.py:388
  28.7 19.7 %collective-permute-start.5 = (bf16[2,64,2560]{2,1,0:T(8,128)(2,1)S(1)}, bf16[2,64,2560]{2,1,0:T(8,128)(2,1)S(1)}, u32[]{:S(2)}, u32[]{:S(2)}) collective-permute-start(bf16[2,64,2560]{2,1,0:T(8,128)(2,1)S(1)} %get-tuple-element.40), channel_id=1, source_target_pairs={{0,1},{1,2},{2,3},{3,4},{4,5},{5,6},{6,7},{7,0},{8,9},{9,10},{10,1... | collective-permute-start | bytes 1966088 | tf_op jit(solution)/shard_map/ppermute | solution.py:388
  30.1 18.8 %collective-permute-start.6 = (bf16[2,64,2560]{2,1,0:T(8,128)(2,1)S(1)}, bf16[2,64,2560]{2,1,0:T(8,128)(2,1)S(1)}, u32[]{:S(2)}, u32[]{:S(2)}) collective-permute-start(bf16[2,64,2560]{2,1,0:T(8,128)(2,1)S(1)} %get-tuple-element.41), channel_id=1, source_target_pairs={{0,7},{1,0},{2,1},{3,2},{4,3},{5,4},{6,5},{7,6},{8,15},{9,8},{10,9... | collective-permute-start | bytes 1966088 | tf_op jit(solution)/shard_map/ppermute | solution.py:388
  34.1 17.3 %collective-permute-start.4 = (bf16[128,2560]{1,0:T(8,128)(2,1)S(1)}, bf16[128,2560]{1,0:T(8,128)(2,1)S(1)}, u32[]{:S(2)}, u32[]{:S(2)}) collective-permute-start(bf16[128,2560]{1,0:T(8,128)(2,1)S(1)} %bitcast.22), channel_id=1, source_target_pairs={{0,144},{1,145},{2,146},{3,147},{4,148},{5,149},{6,150},{7,151},{8... | collective-permute-start | bytes 1966088 | tf_op jit(solution)/shard_map/ppermute | solution.py:388
  38.1 14.1 %collective-permute-start.3 = (bf16[160,2560]{1,0:T(8,128)(2,1)S(1)}, bf16[160,2560]{1,0:T(8,128)(2,1)S(1)}, u32[]{:S(2)}, u32[]{:S(2)}) collective-permute-start(bf16[160,2560]{1,0:T(8,128)(2,1)S(1)} %collective-permute-done.2.c0_ref), channel_id=1, source_target_pairs={{0,8},{1,9},{2,10},{3,11},{4,12},{5,13},{6,14},{7,15},{8,0},{9,1},... | collective-permute-start | bytes 2457608 | tf_op jit(solution)/shard_map/ppermute | solution.py:388
  48.4 11.4 %collective-permute-start.7 = (bf16[2,64,2560]{2,1,0:T(8,128)(2,1)S(1)}, bf16[2,64,2560]{2,1,0:T(8,128)(2,1)S(1)}, u32[]{:S(2)}, u32[]{:S(2)}) collective-permute-start(bf16[2,64,2560]{2,1,0:T(8,128)(2,1)S(1)} %get-tuple-element.42), channel_id=1, source_target_pairs={{0,152},{1,153},{2,154},{3,155},{4,156},{5,157},{6,158},{7,159},{8... | collective-permute-start | bytes 1966088 | tf_op jit(solution)/shard_map/ppermute | solution.py:388
  48.9 10.8 %collective-permute-start.9 = (bf16[2,64,2560]{2,1,0:T(8,128)(2,1)S(1)}, bf16[2,64,2560]{2,1,0:T(8,128)(2,1)S(1)}, u32[]{:S(2)}, u32[]{:S(2)}) collective-permute-start(bf16[2,64,2560]{2,1,0:T(8,128)(2,1)S(1)} %get-tuple-element.44), channel_id=1, source_target_pairs={{0,8},{1,9},{2,10},{3,11},{4,12},{5,13},{6,14},{7,15},{8,0},{9,1},... | collective-permute-start | bytes 1966088 | tf_op jit(solution)/shard_map/ppermute | solution.py:388
  51.4 14.3 %collective-permute-start.8 = (bf16[2,64,2560]{2,1,0:T(8,128)(2,1)S(1)}, bf16[2,64,2560]{2,1,0:T(8,128)(2,1)S(1)}, u32[]{:S(2)}, u32[]{:S(2)}) collective-permute-start(bf16[2,64,2560]{2,1,0:T(8,128)(2,1)S(1)} %get-tuple-element.43), channel_id=1, source_target_pairs={{0,1},{1,0},{2,3},{3,2},{4,5},{5,4},{6,7},{7,6},{8,16},{9,17},{10,... | collective-permute-start | bytes 1966088 | tf_op jit(solution)/shard_map/ppermute | solution.py:388
  51.6 14.1 %collective-permute-start.10 = (bf16[2,64,2560]{2,1,0:T(8,128)(2,1)S(1)}, bf16[2,64,2560]{2,1,0:T(8,128)(2,1)S(1)}, u32[]{:S(2)}, u32[]{:S(2)}) collective-permute-start(bf16[2,64,2560]{2,1,0:T(8,128)(2,1)S(1)} %get-tuple-element.45), channel_id=1, source_target_pairs={{0,8},{1,9},{2,10},{3,11},{4,12},{5,13},{6,14},{7,15},{8,0},{9,1},... | collective-permute-start | bytes 1966088 | tf_op jit(solution)/shard_map/ppermute | solution.py:388
  57.2 26.4 %collective-permute-start.13 = (bf16[128,1280]{1,0:T(8,128)(2,1)S(1)}, bf16[128,1280]{1,0:T(8,128)(2,1)S(1)}, u32[]{:S(2)}, u32[]{:S(2)}) collective-permute-start(bf16[128,1280]{1,0:T(8,128)(2,1)S(1)} %get-tuple-element.51), channel_id=1, source_target_pairs={{0,144},{1,145},{2,146},{3,147},{4,148},{5,149},{6,150},{7,151},{8... | collective-permute-start | bytes 983048 | tf_op jit(solution)/shard_map/ppermute | solution.py:388
  70.2 18.6 %collective-permute-start.11 = (bf16[128,1280]{1,0:T(8,128)(2,1)S(1)}, bf16[128,1280]{1,0:T(8,128)(2,1)S(1)}, u32[]{:S(2)}, u32[]{:S(2)}) collective-permute-start(bf16[128,1280]{1,0:T(8,128)(2,1)S(1)} %get-tuple-element.47), channel_id=1, source_target_pairs={{0,144},{1,145},{2,146},{3,147},{4,148},{5,149},{6,150},{7,151},{8... | collective-permute-start | bytes 983048 | tf_op jit(solution)/shard_map/ppermute | solution.py:388
  79.5 13.9 %collective-permute-start.18 = (bf16[2,128,1280]{2,1,0:T(8,128)(2,1)S(1)}, bf16[2,128,1280]{2,1,0:T(8,128)(2,1)S(1)}, u32[]{:S(2)}, u32[]{:S(2)}) collective-permute-start(bf16[2,128,1280]{2,1,0:T(8,128)(2,1)S(1)} %get-tuple-element.62), channel_id=1, source_target_pairs={{0,32},{1,33},{2,34},{3,35},{4,36},{5,37},{6,38},{7,39},{8,16},{9,... | collective-permute-start | bytes 1966088 | tf_op jit(solution)/shard_map/ppermute | solution.py:388
  79.8 13.6 %collective-permute-start.19 = (bf16[2,128,1280]{2,1,0:T(8,128)(2,1)S(1)}, bf16[2,128,1280]{2,1,0:T(8,128)(2,1)S(1)}, u32[]{:S(2)}, u32[]{:S(2)}) collective-permute-start(bf16[2,128,1280]{2,1,0:T(8,128)(2,1)S(1)} %get-tuple-element.63), channel_id=1, source_target_pairs={{0,8},{1,9},{2,10},{3,11},{4,12},{5,13},{6,14},{7,15},{8,0},{9,1},... | collective-permute-start | bytes 1966088 | tf_op jit(solution)/shard_map/ppermute | solution.py:388
  88.3 10.6 %collective-permute-start.14 = (bf16[2,128,1280]{2,1,0:T(8,128)(2,1)S(1)}, bf16[2,128,1280]{2,1,0:T(8,128)(2,1)S(1)}, u32[]{:S(2)}, u32[]{:S(2)}) collective-permute-start(bf16[2,128,1280]{2,1,0:T(8,128)(2,1)S(1)} %get-tuple-element.53), channel_id=1, source_target_pairs={{0,32},{1,33},{2,34},{3,35},{4,36},{5,37},{6,38},{7,39},{8,16},{9,... | collective-permute-start | bytes 1966088 | tf_op jit(solution)/shard_map/ppermute | solution.py:388
  88.6 10.3 %collective-permute-start.15 = (bf16[2,128,1280]{2,1,0:T(8,128)(2,1)S(1)}, bf16[2,128,1280]{2,1,0:T(8,128)(2,1)S(1)}, u32[]{:S(2)}, u32[]{:S(2)}) collective-permute-start(bf16[2,128,1280]{2,1,0:T(8,128)(2,1)S(1)} %get-tuple-element.54), channel_id=1, source_target_pairs={{0,8},{1,9},{2,10},{3,11},{4,12},{5,13},{6,14},{7,15},{8,0},{9,1},... | collective-permute-start | bytes 1966088 | tf_op jit(solution)/shard_map/ppermute | solution.py:388
  92.2 17.1 %collective-permute-start.12 = (bf16[128,2560]{1,0:T(8,128)(2,1)S(1)}, bf16[128,2560]{1,0:T(8,128)(2,1)S(1)}, u32[]{:S(2)}, u32[]{:S(2)}) collective-permute-start(bf16[128,2560]{1,0:T(8,128)(2,1)S(1)} %get-tuple-element.49), channel_id=1, source_target_pairs={{0,144},{1,145},{2,146},{3,147},{4,148},{5,149},{6,150},{7,151},{8... | collective-permute-start | bytes 1966088 | tf_op jit(solution)/shard_map/ppermute | solution.py:388
  93.5 16.8 %collective-permute-start.20 = (bf16[2,64,1280]{2,1,0:T(8,128)(2,1)S(1)}, bf16[2,64,1280]{2,1,0:T(8,128)(2,1)S(1)}, u32[]{:S(2)}, u32[]{:S(2)}) collective-permute-start(bf16[2,64,1280]{2,1,0:T(8,128)(2,1)S(1)} %get-tuple-element.65), channel_id=1, source_target_pairs={{0,1},{1,2},{2,3},{3,4},{4,5},{5,6},{6,7},{7,0},{8,9},{9,10},{10,1... | collective-permute-start | bytes 983048 | tf_op jit(solution)/shard_map/ppermute | solution.py:388
  93.6 16.7 %collective-permute-start.21 = (bf16[2,64,1280]{2,1,0:T(8,128)(2,1)S(1)}, bf16[2,64,1280]{2,1,0:T(8,128)(2,1)S(1)}, u32[]{:S(2)}, u32[]{:S(2)}) collective-permute-start(bf16[2,64,1280]{2,1,0:T(8,128)(2,1)S(1)} %get-tuple-element.66), channel_id=1, source_target_pairs={{0,7},{1,0},{2,1},{3,2},{4,3},{5,4},{6,5},{7,6},{8,15},{9,8},{10,9... | collective-permute-start | bytes 983048 | tf_op jit(solution)/shard_map/ppermute | solution.py:388
  99.0 12.3 %collective-permute-start.16 = (bf16[2,64,1280]{2,1,0:T(8,128)(2,1)S(1)}, bf16[2,64,1280]{2,1,0:T(8,128)(2,1)S(1)}, u32[]{:S(2)}, u32[]{:S(2)}) collective-permute-start(bf16[2,64,1280]{2,1,0:T(8,128)(2,1)S(1)} %get-tuple-element.56), channel_id=1, source_target_pairs={{0,1},{1,2},{2,3},{3,4},{4,5},{5,6},{6,7},{7,0},{8,9},{9,10},{10,1... | collective-permute-start | bytes 983048 | tf_op jit(solution)/shard_map/ppermute | solution.py:388
  99.1 12.2 %collective-permute-start.17 = (bf16[2,64,1280]{2,1,0:T(8,128)(2,1)S(1)}, bf16[2,64,1280]{2,1,0:T(8,128)(2,1)S(1)}, u32[]{:S(2)}, u32[]{:S(2)}) collective-permute-start(bf16[2,64,1280]{2,1,0:T(8,128)(2,1)S(1)} %get-tuple-element.57), channel_id=1, source_target_pairs={{0,7},{1,0},{2,1},{3,2},{4,3},{5,4},{6,5},{7,6},{8,15},{9,8},{10,9... | collective-permute-start | bytes 983048 | tf_op jit(solution)/shard_map/ppermute | solution.py:388
  (3 other events, 40.6 us)

commit v3 on v2

--- a/solution.py
+++ b/solution.py
@@ -16,7 +16,8 @@
 F32 = jnp.float32
 BF16 = jnp.bfloat16
 
-HPS = 2
+HPS = 5
+HPS_BWD = 5
 HEADS_HALF = 10
 W_HALF = 1280
 VMEM_LIMIT = 10 * 1024 * 1024
@@ -89,14 +90,17 @@
     tb_ref[...] = jnp.where(t_in & (t_ok > 0), 0.0, NEG).astype(F32)
 
 
-def key_values(k_ref, v_ref, zl_ref, zh_ref, tx_ref, cx_ref, tc_ref, cc_ref, c):
+HALOS = 10
+
+
+def key_values(k_ref, v_ref, zlk_ref, zhk_ref, zlv_ref, zhv_ref, tx_ref, tc_ref, cxk_ref, cck_ref, cxv_ref, ccv_ref, c):
     cat = lambda *a: jnp.concatenate(a, axis=0)
-    k_oz = cat(k_ref[:, c], zl_ref[0, :, c], zh_ref[0, :, c])
-    v_oz = cat(v_ref[:, c], zl_ref[1, :, c], zh_ref[1, :, c])
-    k_tx = cat(tx_ref[0, :, c], cx_ref[0, :, c])
-    v_tx = cat(tx_ref[1, :, c], cx_ref[1, :, c])
-    k_tc = cat(tc_ref[0, :, c], cc_ref[0, :, c])
-    v_tc = cat(tc_ref[1, :, c], cc_ref[1, :, c])
+    k_oz = cat(k_ref[:, c], zlk_ref[:, c], zhk_ref[:, c])
+    v_oz = cat(v_ref[:, c], zlv_ref[:, c], zhv_ref[:, c])
+    k_tx = cat(tx_ref[0, :, c], cxk_ref[:, c])
+    v_tx = cat(tx_ref[1, :, c], cxv_ref[:, c])
+    k_tc = cat(tc_ref[0, :, c], cck_ref[:, c])
+    v_tc = cat(tc_ref[1, :, c], ccv_ref[:, c])
     return k_oz, v_oz, k_tx, v_tx, k_tc, v_tc
 
 
@@ -116,16 +120,19 @@
 
 
 def forward_kernel(kind, q_ref, k_ref, v_ref, *rest):
-    halo, (att_ref, p_ref, zb_ref, tb_ref) = rest[:6], rest[6:]
+    halo, (att_ref, p_ref, zb_ref, tb_ref) = rest[:HALOS], rest[HALOS:]
     window_bias(zb_ref, tb_ref)
     first = half_of(kind) * HEADS_HALF
 
-    def one(h):
+    def scores(h):
         c = lanes(first + h)
         q = both_sides(q_ref, c)
         k_oz, v_oz, k_tx, v_tx, k_tc, v_tc = key_values(k_ref, v_ref, *halo, c)
         s_oz = dot(q, k_oz, 1, 1)
         s_t = jnp.concatenate([dot(q[:64], k_tx, 1, 1), dot(q[64:], k_tc, 1, 1)], axis=0)
+        return s_oz, s_t, v_oz, v_tx, v_tc
+
+    def softmax(s_oz, s_t):
         s_o = s_oz[:, :128]
         s_z = s_oz[:, 128:] + zb_ref[...]
         s_t = s_t + tb_ref[...]
@@ -135,15 +142,21 @@
         e_t = jnp.exp2((s_t - m) * EXP2_SCALE)
         inv = 1.0 / jnp.sum(e_o + e_z + e_t, axis=1, keepdims=True)
         p_oz = jnp.concatenate([e_o * inv, e_z * inv], axis=1).astype(BF16)
-        p_t = (e_t * inv).astype(BF16)
-        p_ref[h, :, :256] = p_oz
-        p_ref[h, :, 256:] = p_t
+        return p_oz, (e_t * inv).astype(BF16)
+
+    def attend(p_oz, p_t, v_oz, v_tx, v_tc):
         a_t = jnp.concatenate([dot(p_t[:64], v_tx, 1, 0), dot(p_t[64:], v_tc, 1, 0)], axis=0)
-        put_sides(att_ref, lanes(h), (dot(p_oz, v_oz, 1, 0) + a_t).astype(BF16))
+        return (dot(p_oz, v_oz, 1, 0) + a_t).astype(BF16)
 
     def step(i, carry):
-        for j in range(HPS):
-            one(i * HPS + j)
+        heads = [i * HPS + j for j in range(HPS)]
+        scored = [scores(h) for h in heads]
+        probs = [softmax(*x[:2]) for x in scored]
+        att = [attend(*p, *x[2:]) for p, x in zip(probs, scored)]
+        for h, (p_oz, p_t), value in zip(heads, probs, att):
+            p_ref[h, :, :256] = p_oz
+            p_ref[h, :, 256:] = p_t
+            put_sides(att_ref, lanes(h), value)
         return carry
 
     lax.fori_loop(0, HEADS_HALF // HPS, step, 0)
@@ -159,10 +172,11 @@
 
 
 def backward_kernel(kind, q_ref, k_ref, v_ref, *rest):
-    halo, (p_ref, g_ref, dq_ref, own_ref, rim_ref, tx_ref, tc_ref) = rest[:6], rest[6:]
+    halo, (p_ref, g_ref, dq_ref, own_ref, rim_ref, *t_refs) = rest[:HALOS], rest[HALOS:]
+    tx_ref, cx_ref, tc_ref = t_refs
     first = half_of(kind) * HEADS_HALF
 
-    def one(h):
+    def probs_grad(h):
         c = lanes(first + h)
         o = lanes(h)
         q = both_sides(q_ref, c)
@@ -172,31 +186,42 @@
         p_t = p_ref[h, :, 256:]
         dp_oz = dot(g, v_oz, 1, 1)
         dp_t = jnp.concatenate([dot(g[:64], v_tx, 1, 1), dot(g[64:], v_tc, 1, 1)], axis=0)
+        return q, g, k_oz, k_tx, k_tc, p_oz, p_t, dp_oz, dp_t
+
+    def scores_grad(p_oz, p_t, dp_oz, dp_t):
         w_oz = p_oz.astype(F32)
         w_t = p_t.astype(F32)
         x_oz = w_oz * dp_oz
         row = jnp.sum(x_oz[:, :128] + x_oz[:, 128:] + w_t * dp_t, axis=1, keepdims=True)
         ds_oz = (w_oz * (dp_oz - row) * SCALE).astype(BF16)
-        ds_t = (w_t * (dp_t - row) * SCALE).astype(BF16)
-        dq_t = jnp.concatenate([dot(ds_t[:64], k_tx, 1, 0), dot(ds_t[64:], k_tc, 1, 0)], axis=0)
-        put_sides(dq_ref, o, (dot(ds_oz, k_oz, 1, 0) + dq_t).astype(BF16))
-        dk_oz = dot(ds_oz, q, 0, 0)
-        dv_oz = dot(p_oz, g, 0, 0)
-        own_ref[0, :, o] = dk_oz[:128]
-        own_ref[1, :, o] = dv_oz[:128]
-        rim_ref[0, :, o] = dk_oz[128:]
-        rim_ref[1, :, o] = dv_oz[128:]
-        tx_ref[0, :, o] = dot(ds_t[:64], q[:64], 0, 0).astype(BF16)
-        tx_ref[1, :, o] = dot(p_t[:64], g[:64], 0, 0).astype(BF16)
-        tc_ref[0, :, o] = dot(ds_t[64:], q[64:], 0, 0).astype(BF16)
-        tc_ref[1, :, o] = dot(p_t[64:], g[64:], 0, 0).astype(BF16)
+        return ds_oz, (w_t * (dp_t - row) * SCALE).astype(BF16)
 
     def step(i, carry):
-        for j in range(HPS):
-            one(i * HPS + j)
-        return carry
-
-    lax.fori_loop(0, HEADS_HALF // HPS, step, 0)
+        heads = [i * HPS_BWD + j for j in range(HPS_BWD)]
+        held = [probs_grad(h) for h in heads]
+        values = [(dot(x[5], x[1], 0, 0), dot(x[6][:64], x[1][:64], 0, 0), dot(x[6][64:], x[1][64:], 0, 0)) for x in held]
+        grads = [scores_grad(*x[5:]) for x in held]
+        keys = [
+            (dot(d, x[0], 0, 0), dot(t[:64], x[0][:64], 0, 0), dot(t[64:], x[0][64:], 0, 0))
+            for (d, t), x in zip(grads, held)
+        ]
+        queries = [
+            dot(d, x[2], 1, 0) + jnp.concatenate([dot(t[:64], x[3], 1, 0), dot(t[64:], x[4], 1, 0)], axis=0)
+            for (d, t), x in zip(grads, held)
+        ]
+        for h, key, value, query in zip(heads, keys, values, queries):
+            o = lanes(h)
+            put_sides(dq_ref, o, query.astype(BF16))
+            for kv, (d_oz, d_x, d_c) in ((0, key), (1, value)):
+                own_ref[kv, :, o] = d_oz[:128]
+                rim_ref[kv, :, o] = d_oz[128:]
+                d_x = d_x.astype(BF16)
+                tx_ref[kv, :, o] = d_x[:64]
+                cx_ref[kv, :, o] = d_x[64:]
+                tc_ref[kv, :, o] = d_c.astype(BF16)
+        return carry
+
+    lax.fori_loop(0, HEADS_HALF // HPS_BWD, step, 0)
 
 
 def backward_half(kind, operands, probs, grad):
@@ -204,7 +229,7 @@
     return call(
         functools.partial(backward_kernel, kind),
         (in_vmem((128, W_HALF), BF16), in_vmem(pair, F32), in_vmem(pair, F32),
-         in_vmem(pair, BF16), in_vmem(pair, BF16)),
+         *(in_vmem((2, 64, W_HALF), BF16),) * 2, in_vmem(pair, BF16)),
         (*operands, probs, grad), flops=4 * 2 * 10 * 128 * 384 * 128, moved=12_000_000,
     )
 
@@ -287,10 +312,10 @@
 
 
 def rim_kernel(rim_ref, fx_ref, fc_ref, lo_ref, hi_ref):
-    for side, src in (("x", fx_ref), ("c", fc_ref)):
+    for side, src, first in (("x", fx_ref, 0), ("c", fc_ref, 64)):
         at = side_rows(side, 32)
         for half, out in ((0, lo_ref), (1, hi_ref)):
-            corner = src[:, 64 + 32 * half : 96 + 32 * half].astype(F32)
+            corner = src[:, first + 32 * half : first + 32 * half + 32].astype(F32)
             here = rim_ref[:, pl.ds(pl.multiple_of(64 * half + at, 32), 32)]
             out[:, pl.ds(at, 32)] = (here + corner).astype(BF16)
 
@@ -331,13 +356,13 @@
     )
 
 
-def prep_kernel(k_ref, v_ref, zlo_ref, zhi_ref, tx_ref, tc_ref, sems):
+def prep_kernel(k_ref, v_ref, zlk_ref, zhk_ref, zlv_ref, zhv_ref, tx_ref, tc_ref, sems):
     copies = []
-    for kv, src in ((0, k_ref), (1, v_ref)):
+    for src, lo_ref, hi_ref in ((k_ref, zlk_ref, zhk_ref), (v_ref, zlv_ref, zhv_ref)):
         for f in range(4):
             rows = pl.ds(f * 16, 16)
-            copies.append((src.at[pl.ds(f * 32 + 16, 16)], zhi_ref.at[kv, rows]))
-            copies.append((src.at[pl.ds(f * 32, 16)], zlo_ref.at[kv, rows]))
+            copies.append((src.at[pl.ds(f * 32 + 16, 16)], hi_ref.at[rows]))
+            copies.append((src.at[pl.ds(f * 32, 16)], lo_ref.at[rows]))
     for kv, src in ((0, k_ref), (1, v_ref)):
         copies.append((src.at[pl.ds(side_rows("x"), 64)], tx_ref.at[kv]))
         copies.append((src.at[pl.ds(side_rows("c"), 64)], tc_ref.at[kv]))
@@ -350,8 +375,8 @@
 
 def prep(keys, values):
     return call(
-        prep_kernel, (in_vmem((2, 64, 2560), BF16),) * 4, (keys, values), moved=4_000_000,
-        scratch=(pltpu.SemaphoreType.DMA((20,)),), hbm_in=2,
+        prep_kernel, (in_vmem((64, 2560), BF16),) * 4 + (in_vmem((2, 64, 2560), BF16),) * 2,
+        (keys, values), moved=4_000_000, scratch=(pltpu.SemaphoreType.DMA((20,)),), hbm_in=2,
     )
 
 
@@ -373,12 +398,12 @@
 def corner_kernel(lo_ref, hi_ref, cx_ref, cc_ref):
     for side, out in (("x", cx_ref), ("c", cc_ref)):
         r = pl.ds(side_rows(side, 32), 32)
-        out[:, :32] = lo_ref[:, r]
-        out[:, 32:] = hi_ref[:, r]
+        out[:32] = lo_ref[r]
+        out[32:] = hi_ref[r]
 
 
 def corners(z_lo, z_hi):
-    return call(corner_kernel, (in_vmem((2, 64, 2560), BF16),) * 2, (z_lo, z_hi), moved=2_600_000)
+    return call(corner_kernel, (in_vmem((64, 2560), BF16),) * 2, (z_lo, z_hi), moved=1_300_000)
 
 
 def body(queries, keys, values, projection, d_outputs):
@@ -402,21 +427,26 @@
 
     w_near = send(projection, ring_y)
     their_d_out = send(d_out, pair_chip)
-    z_lo_s, z_hi_s, tx_s, tc_s = prep(k, v)
-    z_lo = send(z_hi_s, up_z)
-    z_hi = send(z_lo_s, down_z)
+    k_lo_s, k_hi_s, v_lo_s, v_hi_s, tx_s, tc_s = prep(k, v)
+    k_lo = send(k_hi_s, up_z)
+    k_hi = send(k_lo_s, down_z)
+    v_lo = send(v_hi_s, up_z)
+    v_hi = send(v_lo_s, down_z)
     t_x = send(tx_s, other_chip)
     t_c = send(tc_s, other_core)
-    cx_s, cc_s = corners(z_lo, z_hi)
-    c_x = send(cx_s, other_chip_mid)
-    c_c = send(cc_s, other_core)
+    cxk_s, cck_s = corners(k_lo, k_hi)
+    cxk = send(cxk_s, other_chip)
+    cck = send(cck_s, other_core)
+    cxv_s, ccv_s = corners(v_lo, v_hi)
+    cxv = send(cxv_s, other_chip_mid)
+    ccv = send(ccv_s, other_core)
     w_far = send(w_near, other_core)
     (w_part,) = call(slice_kernel, (in_vmem((160, 2560), BF16),), (w_near,))
     w_c0 = send(w_part, ring_y)
     w_c1 = send(w_c0, other_core)
     rows = gather_rows(projection, w_near, w_far)
 
-    operands = (q, k, v, z_lo, z_hi, t_x, c_x, t_c, c_c)
+    operands = (q, k, v, k_lo, k_hi, v_lo, v_hi, t_x, t_c, cxk, cck, cxv, ccv)
     att_remote, p_remote = forward_half("remote", operands)
     their_att = send(att_remote, pair_chip)
     att_local, p_local = forward_half("local", operands)
@@ -424,20 +454,22 @@
     rows, g_local, g_theirs = grad_proj(rows, w_c0, w_c1, d_out, their_d_out)
     g_remote = send(g_theirs, pair_chip)
 
-    dq_a, own_a, rim_a, tx_a, tc_a = backward_half("local", operands, p_local, g_local)
+    dq_a, own_a, rim_a, tx_a, cx_a, tc_a = backward_half("local", operands, p_local, g_local)
+    ex_a = send(cx_a, other_chip_late)
     fx_a = send(tx_a, other_chip_late)
     fc_a = send(tc_a, other_core)
-    dq_b, own_b, rim_b, tx_b, tc_b = backward_half("remote", operands, p_remote, g_remote)
+    dq_b, own_b, rim_b, tx_b, cx_b, tc_b = backward_half("remote", operands, p_remote, g_remote)
+    ex_b = send(cx_b, other_chip_late)
     fx_b = send(tx_b, other_chip_late)
     fc_b = send(tc_b, other_core)
 
     part, part_theirs = out_proj(rows, att_local, their_att)
     part_remote = send(part_theirs, pair_chip)
 
-    rlo_a, rhi_a = rim_half(rim_a, fx_a, fc_a)
+    rlo_a, rhi_a = rim_half(rim_a, ex_a, fc_a)
     from_lo_a = send(rhi_a, up_z)
     from_hi_a = send(rlo_a, down_z)
-    rlo_b, rhi_b = rim_half(rim_b, fx_b, fc_b)
+    rlo_b, rhi_b = rim_half(rim_b, ex_b, fc_b)
     from_lo_b = send(rhi_b, up_z)
     from_hi_b = send(rlo_b, down_z)
 

time: 113 us -> 123 us (1.088)
  starting transfers between devices: 34.5 us -> 46.4 us
  Pallas kernels: 32.6 us -> 22.2 us
  waiting for transfers between devices: 44.4 us -> 52.8 us
    ppermute x22 -> x28, starting transfers between devices: 34.5 us -> 46.4 us  [send(): return lax.ppermute(x, AXES, make_perm(shape, fn))]
    pallas_call x15 -> x16, Pallas kernels: 32.6 us -> 22.2 us  [call(): pl.pallas_call(kernel, out_shape=tuple(outs), in_specs=[vm] * len(near) +...]
    ppermute x22 -> x28, waiting for transfers between devices: 44.4 us -> 52.8 us  [send(): return lax.ppermute(x, AXES, make_perm(shape, fn))]
  transfers between devices with their start and end apart: 22 -> 28, of which waited for: 7 -> 12; matrix products, arithmetic and copies ran while one was open for 0% -> 0% of each run, Pallas kernels for 28% -> 17%
where the time goes in v3:
time: 123 us; the launch traced here: 122 us
  waiting for transfers between devices  52.8 us (43%)
  starting transfers between devices  46.4 us (38%)
  Pallas kernels  22.2 us (18%)
    ppermute x28, waiting for transfers between devices, send(): return lax.ppermute(x, AXES, make_perm(shape, fn))  52.8 us
    ppermute x28, starting transfers between devices, send(): return lax.ppermute(x, AXES, make_perm(shape, fn))  46.4 us
    pallas_call x16, Pallas kernels, call(): pl.pallas_call(kernel, out_shape=tuple(outs), in_specs=[vm] * len(near) +...  22.2 us
  transfers between devices with their start and end apart: 28, of which 12 were waited for; matrix products, arithmetic and copies ran while one was open for 0% of the time, Pallas kernels for 17%

profile of v3, /device:TPU:1, one launch (start us, length us, event | category | flops | bytes accessed | tf_op | source)
XLA Modules:
  0.0 122.4 jit_solution(3712789886245360018)
XLA Ops:
  0.6 3.6 %collective-permute-start = (bf16[320,2560]{1,0:T(8,128)(2,1)}, bf16[320,2560]{1,0:T(8,128)(2,1)S(1)}, u32[]{:S(2)}, u32[]{:S(2)}) collective-permute-start(bf16[320,2560]{1,0:T(8,128)(2,1)} %own_ref.1), channel_id=1, source_target_pairs={{0,32},{1,33},{2,34},{3,35},{4,36},{5,37},{6,38},{7,39},{8,104},{9... | collective-permute-start | bytes 4915208 | tf_op jit(solution)/shard_map/ppermute | solution.py:413
  4.3 18.4 %collective-permute-done.near_ref = bf16[320,2560]{1,0:T(8,128)(2,1)S(1)} collective-permute-done((bf16[320,2560]{1,0:T(8,128)(2,1)}, bf16[320,2560]{1,0:T(8,128)(2,1)S(1)}, u32[]{:S(2)}, u32[]{:S(2)}) %collective-permute-start) | collective-permute-done | bytes 1638432 | tf_op jit(solution)/shard_map/ppermute | solution.py:413
  22.6 3.8 %collective-permute-start.1 = (bf16[320,2560]{1,0:T(8,128)(2,1)S(1)}, bf16[320,2560]{1,0:T(8,128)(2,1)S(1)}, u32[]{:S(2)}, u32[]{:S(2)}) collective-permute-start(bf16[320,2560]{1,0:T(8,128)(2,1)S(1)} %collective-permute-done.near_ref), channel_id=1, source_target_pairs={{0,8},{1,9},{2,10},{3,11},{4,12},{5,13},{6,14},{7,15},{8,0},{9,1},... | collective-permute-start | bytes 4915208 | tf_op jit(solution)/shard_map/ppermute | solution.py:413
  30.1 4.0 %collective-permute-start.6 = (bf16[64,2560]{1,0:T(8,128)(2,1)S(1)}, bf16[64,2560]{1,0:T(8,128)(2,1)S(1)}, u32[]{:S(2)}, u32[]{:S(2)}) collective-permute-start(bf16[64,2560]{1,0:T(8,128)(2,1)S(1)} %get-tuple-element.47), channel_id=1, source_target_pairs={{0,7},{1,0},{2,1},{3,2},{4,3},{5,4},{6,5},{7,6},{8,15},{9,8},{10,9... | collective-permute-start | bytes 983048 | tf_op jit(solution)/shard_map/ppermute | solution.py:413
  34.2 4.0 %collective-permute-done.2.c0_ref = bf16[160,2560]{1,0:T(8,128)(2,1)S(1)} collective-permute-done((bf16[160,2560]{1,0:T(8,128)(2,1)S(1)}, bf16[160,2560]{1,0:T(8,128)(2,1)S(1)}, u32[]{:S(2)}, u32[]{:S(2)}) %collective-permute-start.2) | collective-permute-done | bytes 819232 | tf_op jit(solution)/shard_map/ppermute | solution.py:413
  38.1 2.1 %collective-permute-start.3 = (bf16[160,2560]{1,0:T(8,128)(2,1)S(1)}, bf16[160,2560]{1,0:T(8,128)(2,1)S(1)}, u32[]{:S(2)}, u32[]{:S(2)}) collective-permute-start(bf16[160,2560]{1,0:T(8,128)(2,1)S(1)} %collective-permute-done.2.c0_ref), channel_id=1, source_target_pairs={{0,8},{1,9},{2,10},{3,11},{4,12},{5,13},{6,14},{7,15},{8,0},{9,1},... | collective-permute-start | bytes 2457608 | tf_op jit(solution)/shard_map/ppermute | solution.py:413
  40.2 2.2 %collective-permute-done.5.lo_ref.rest_0_ = bf16[64,2560]{1,0:T(8,128)(2,1)S(1)} collective-permute-done((bf16[64,2560]{1,0:T(8,128)(2,1)S(1)}, bf16[64,2560]{1,0:T(8,128)(2,1)S(1)}, u32[]{:S(2)}, u32[]{:S(2)}) %collective-permute-start.5) | collective-permute-done | bytes 327712 | tf_op jit(solution)/shard_map/ppermute | solution.py:413
  44.1 2.5 %collective-permute-start.4 = (bf16[128,2560]{1,0:T(8,128)(2,1)S(1)}, bf16[128,2560]{1,0:T(8,128)(2,1)S(1)}, u32[]{:S(2)}, u32[]{:S(2)}) collective-permute-start(bf16[128,2560]{1,0:T(8,128)(2,1)S(1)} %bitcast.22), channel_id=1, source_target_pairs={{0,144},{1,145},{2,146},{3,147},{4,148},{5,149},{6,150},{7,151},{8... | collective-permute-start | bytes 1966088 | tf_op jit(solution)/shard_map/ppermute | solution.py:413
  49.0 2.1 %collective-permute-done.8.hi_ref.rest_3_ = bf16[64,2560]{1,0:T(8,128)(2,1)S(1)} collective-permute-done((bf16[64,2560]{1,0:T(8,128)(2,1)S(1)}, bf16[64,2560]{1,0:T(8,128)(2,1)S(1)}, u32[]{:S(2)}, u32[]{:S(2)}) %collective-permute-start.8) | collective-permute-done | bytes 327712 | tf_op jit(solution)/shard_map/ppermute | solution.py:413
  52.1 9.2 %collective-permute-done.4.theirs_ref = bf16[128,2560]{1,0:T(8,128)(2,1)S(1)} collective-permute-done((bf16[128,2560]{1,0:T(8,128)(2,1)S(1)}, bf16[128,2560]{1,0:T(8,128)(2,1)S(1)}, u32[]{:S(2)}, u32[]{:S(2)}) %collective-permute-start.4) | collective-permute-done | bytes 655392 | tf_op jit(solution)/shard_map/ppermute | solution.py:413
  62.3 7.1 %collective-permute-start.12 = (bf16[64,2560]{1,0:T(8,128)(2,1)S(1)}, bf16[64,2560]{1,0:T(8,128)(2,1)S(1)}, u32[]{:S(2)}, u32[]{:S(2)}) collective-permute-start(bf16[64,2560]{1,0:T(8,128)(2,1)S(1)} %get-tuple-element.53), channel_id=1, source_target_pairs={{0,8},{1,9},{2,10},{3,11},{4,12},{5,13},{6,14},{7,15},{8,0},{9,1},... | collective-permute-start | bytes 983048 | tf_op jit(solution)/shard_map/ppermute | solution.py:413
  70.1 5.0 %shard_map.86 = (bf16[1280,2560]{1,0:T(8,128)(2,1)S(1)}, bf16[128,1280]{1,0:T(8,128)(2,1)S(1)}, bf16[128,1280]{1,0:T(8,128)(2,1)S(1)}) custom-call(bf16[1280,2560]{1,0:T(8,128)(2,1)S(1)} %shard_map.84.w_in, bf16[160,2560]{1,0:T(8,128)(2,1)S(1)} %collective-permute-done.2.c0_ref, ...), custom_call_target="tpu_custom_call", output_to_operand_aliasing={{0}: (0, {})} | custom-call | flops 1677721600 | bytes 9000000 | tf_op jit(solution)/shard_map/pallas_call | solution.py:51
  75.0 2.3 %collective-permute-start.17 = (bf16[128,1280]{1,0:T(8,128)(2,1)S(1)}, bf16[128,1280]{1,0:T(8,128)(2,1)S(1)}, u32[]{:S(2)}, u32[]{:S(2)}) collective-permute-start(bf16[128,1280]{1,0:T(8,128)(2,1)S(1)} %get-tuple-element.61), channel_id=1, source_target_pairs={{0,144},{1,145},{2,146},{3,147},{4,148},{5,149},{6,150},{7,151},{8... | collective-permute-start | bytes 983048 | tf_op jit(solution)/shard_map/ppermute | solution.py:413
  81.5 2.2 %shard_map.96 = (bf16[128,1280]{1,0:T(8,128)(2,1)S(1)}, f32[2,128,1280]{2,1,0:T(8,128)S(1)}, f32[2,128,1280]{2,1,0:T(8,128)S(1)}, bf16[2,64,1280]{2,1,0:T(8,128)...) custom-call(bf16[128,2560]{1,0:T(8,128)(2,1)S(1)} %bitcast.20, ...), custom_call_target="tpu_custom_call" | custom-call | flops 503316480 | bytes 12000000 | tf_op jit(solution)/shard_map/pallas_call | solution.py:51
  85.1 2.2 %shard_map.94 = (bf16[128,1280]{1,0:T(8,128)(2,1)S(1)}, f32[2,128,1280]{2,1,0:T(8,128)S(1)}, f32[2,128,1280]{2,1,0:T(8,128)S(1)}, bf16[2,64,1280]{2,1,0:T(8,128)...) custom-call(bf16[128,2560]{1,0:T(8,128)(2,1)S(1)} %bitcast.21, ...), custom_call_target="tpu_custom_call" | custom-call | flops 503316480 | bytes 12000000 | tf_op jit(solution)/shard_map/pallas_call | solution.py:51
  87.4 2.3 %collective-permute-start.19 = (bf16[2,128,1280]{2,1,0:T(8,128)(2,1)S(1)}, bf16[2,128,1280]{2,1,0:T(8,128)(2,1)S(1)}, u32[]{:S(2)}, u32[]{:S(2)}) collective-permute-start(bf16[2,128,1280]{2,1,0:T(8,128)(2,1)S(1)} %get-tuple-element.64), channel_id=1, source_target_pairs={{0,8},{1,9},{2,10},{3,11},{4,12},{5,13},{6,14},{7,15},{8,0},{9,1},... | collective-permute-start | bytes 1966088 | tf_op jit(solution)/shard_map/ppermute | solution.py:413
  89.7 2.5 %collective-permute-done.15.theirs_ref = bf16[128,1280]{1,0:T(8,128)(2,1)S(1)} collective-permute-done((bf16[128,1280]{1,0:T(8,128)(2,1)S(1)}, bf16[128,1280]{1,0:T(8,128)(2,1)S(1)}, u32[]{:S(2)}, u32[]{:S(2)}) %collective-permute-start.15) | collective-permute-done | bytes 327712 | tf_op jit(solution)/shard_map/ppermute | solution.py:413
  92.2 3.5 %shard_map.92 = (f32[128,2560]{1,0:T(8,128)S(1)}, bf16[128,2560]{1,0:T(8,128)(2,1)S(1)}) custom-call(bf16[1280,2560]{1,0:T(8,128)(2,1)S(1)} %get-tuple-element.45.w_ref, bf16[128,1280]{1,0:T(8,128)(2,1)S(1)} %get-tuple-element.56.mine_ref, bf16[128,1280]{1,0:T(8,128)(2,1)S(1)} %collective-permute-done.15.theirs_ref), custom_call_target="tpu_custom_call" | custom-call | flops 1677721600 | bytes 9000000 | tf_op jit(solution)/shard_map/pallas_call | solution.py:51
  95.7 2.7 %collective-permute-start.16 = (bf16[128,2560]{1,0:T(8,128)(2,1)S(1)}, bf16[128,2560]{1,0:T(8,128)(2,1)S(1)}, u32[]{:S(2)}, u32[]{:S(2)}) collective-permute-start(bf16[128,2560]{1,0:T(8,128)(2,1)S(1)} %get-tuple-element.59), channel_id=1, source_target_pairs={{0,144},{1,145},{2,146},{3,147},{4,148},{5,149},{6,150},{7,151},{8... | collective-permute-start | bytes 1966088 | tf_op jit(solution)/shard_map/ppermute | solution.py:413
  100.8 4.3 %collective-permute-done.20.fx_ref = bf16[2,64,1280]{2,1,0:T(8,128)(2,1)S(1)} collective-permute-done((bf16[2,64,1280]{2,1,0:T(8,128)(2,1)S(1)}, bf16[2,64,1280]{2,1,0:T(8,128)(2,1)S(1)}, u32[]{:S(2)}, u32[]{:S(2)}) %collective-permute-start.20) | collective-permute-done | bytes 327712 | tf_op jit(solution)/shard_map/ppermute | solution.py:413
  105.7 2.2 %collective-permute-start.27 = (bf16[2,64,1280]{2,1,0:T(8,128)(2,1)S(1)}, bf16[2,64,1280]{2,1,0:T(8,128)(2,1)S(1)}, u32[]{:S(2)}, u32[]{:S(2)}) collective-permute-start(bf16[2,64,1280]{2,1,0:T(8,128)(2,1)S(1)} %get-tuple-element.78), channel_id=1, source_target_pairs={{0,7},{1,0},{2,1},{3,2},{4,3},{5,4},{6,5},{7,6},{8,15},{9,8},{10,9... | collective-permute-start | bytes 983048 | tf_op jit(solution)/shard_map/ppermute | solution.py:413
  109.2 2.7 %collective-permute-done.16.remote_ref = bf16[128,2560]{1,0:T(8,128)(2,1)S(1)} collective-permute-done((bf16[128,2560]{1,0:T(8,128)(2,1)S(1)}, bf16[128,2560]{1,0:T(8,128)(2,1)S(1)}, u32[]{:S(2)}, u32[]{:S(2)}) %collective-permute-start.16) | collective-permute-done | bytes 655392 | tf_op jit(solution)/shard_map/ppermute | solution.py:413
  111.9 2.4 %collective-permute-start.22 = (bf16[2,64,1280]{2,1,0:T(8,128)(2,1)S(1)}, bf16[2,64,1280]{2,1,0:T(8,128)(2,1)S(1)}, u32[]{:S(2)}, u32[]{:S(2)}) collective-permute-start(bf16[2,64,1280]{2,1,0:T(8,128)(2,1)S(1)} %get-tuple-element.68), channel_id=1, source_target_pairs={{0,7},{1,0},{2,1},{3,2},{4,3},{5,4},{6,5},{7,6},{8,15},{9,8},{10,9... | collective-permute-start | bytes 983048 | tf_op jit(solution)/shard_map/ppermute | solution.py:413
  116.3 4.9 %collective-permute-done.21.lo_ref = bf16[2,64,1280]{2,1,0:T(8,128)(2,1)S(1)} collective-permute-done((bf16[2,64,1280]{2,1,0:T(8,128)(2,1)S(1)}, bf16[2,64,1280]{2,1,0:T(8,128)(2,1)S(1)}, u32[]{:S(2)}, u32[]{:S(2)}) %collective-permute-start.21) | collective-permute-done | bytes 327712 | tf_op jit(solution)/shard_map/ppermute | solution.py:413
  (58 shorter events, 23.1 us)
Async XLA Ops:
  0.6 22.0 %collective-permute-start = (bf16[320,2560]{1,0:T(8,128)(2,1)}, bf16[320,2560]{1,0:T(8,128)(2,1)S(1)}, u32[]{:S(2)}, u32[]{:S(2)}) collective-permute-start(bf16[320,2560]{1,0:T(8,128)(2,1)} %own_ref.1), channel_id=1, source_target_pairs={{0,32},{1,33},{2,34},{3,35},{4,36},{5,37},{6,38},{7,39},{8,104},{9... | collective-permute-start | bytes 4915208 | tf_op jit(solution)/shard_map/ppermute | solution.py:413
  22.6 46.8 %collective-permute-start.1 = (bf16[320,2560]{1,0:T(8,128)(2,1)S(1)}, bf16[320,2560]{1,0:T(8,128)(2,1)S(1)}, u32[]{:S(2)}, u32[]{:S(2)}) collective-permute-start(bf16[320,2560]{1,0:T(8,128)(2,1)S(1)} %collective-permute-done.near_ref), channel_id=1, source_target_pairs={{0,8},{1,9},{2,10},{3,11},{4,12},{5,13},{6,14},{7,15},{8,0},{9,1},... | collective-permute-start | bytes 4915208 | tf_op jit(solution)/shard_map/ppermute | solution.py:413
  26.5 11.6 %collective-permute-start.2 = (bf16[160,2560]{1,0:T(8,128)(2,1)S(1)}, bf16[160,2560]{1,0:T(8,128)(2,1)S(1)}, u32[]{:S(2)}, u32[]{:S(2)}) collective-permute-start(bf16[160,2560]{1,0:T(8,128)(2,1)S(1)} %shard_map.85), channel_id=1, source_target_pairs={{0,32},{1,33},{2,34},{3,35},{4,36},{5,37},{6,38},{7,39},{8,104},{9... | collective-permute-start | bytes 2457608 | tf_op jit(solution)/shard_map/ppermute | solution.py:413
  28.7 13.6 %collective-permute-start.5 = (bf16[64,2560]{1,0:T(8,128)(2,1)S(1)}, bf16[64,2560]{1,0:T(8,128)(2,1)S(1)}, u32[]{:S(2)}, u32[]{:S(2)}) collective-permute-start(bf16[64,2560]{1,0:T(8,128)(2,1)S(1)} %get-tuple-element.46), channel_id=1, source_target_pairs={{0,1},{1,2},{2,3},{3,4},{4,5},{5,6},{6,7},{7,0},{8,9},{9,10},{10,1... | collective-permute-start | bytes 983048 | tf_op jit(solution)/shard_map/ppermute | solution.py:413
  30.1 13.9 %collective-permute-start.6 = (bf16[64,2560]{1,0:T(8,128)(2,1)S(1)}, bf16[64,2560]{1,0:T(8,128)(2,1)S(1)}, u32[]{:S(2)}, u32[]{:S(2)}) collective-permute-start(bf16[64,2560]{1,0:T(8,128)(2,1)S(1)} %get-tuple-element.47), channel_id=1, source_target_pairs={{0,7},{1,0},{2,1},{3,2},{4,3},{5,4},{6,5},{7,6},{8,15},{9,8},{10,9... | collective-permute-start | bytes 983048 | tf_op jit(solution)/shard_map/ppermute | solution.py:413
  34.2 14.0 %collective-permute-start.7 = (bf16[64,2560]{1,0:T(8,128)(2,1)S(1)}, bf16[64,2560]{1,0:T(8,128)(2,1)S(1)}, u32[]{:S(2)}, u32[]{:S(2)}) collective-permute-start(bf16[64,2560]{1,0:T(8,128)(2,1)S(1)} %get-tuple-element.48), channel_id=1, source_target_pairs={{0,1},{1,2},{2,3},{3,4},{4,5},{5,6},{6,7},{7,0},{8,9},{9,10},{10,1... | collective-permute-start | bytes 983048 | tf_op jit(solution)/shard_map/ppermute | solution.py:413
  38.1 31.3 %collective-permute-start.3 = (bf16[160,2560]{1,0:T(8,128)(2,1)S(1)}, bf16[160,2560]{1,0:T(8,128)(2,1)S(1)}, u32[]{:S(2)}, u32[]{:S(2)}) collective-permute-start(bf16[160,2560]{1,0:T(8,128)(2,1)S(1)} %collective-permute-done.2.c0_ref), channel_id=1, source_target_pairs={{0,8},{1,9},{2,10},{3,11},{4,12},{5,13},{6,14},{7,15},{8,0},{9,1},... | collective-permute-start | bytes 2457608 | tf_op jit(solution)/shard_map/ppermute | solution.py:413
  44.1 17.2 %collective-permute-start.4 = (bf16[128,2560]{1,0:T(8,128)(2,1)S(1)}, bf16[128,2560]{1,0:T(8,128)(2,1)S(1)}, u32[]{:S(2)}, u32[]{:S(2)}) collective-permute-start(bf16[128,2560]{1,0:T(8,128)(2,1)S(1)} %bitcast.22), channel_id=1, source_target_pairs={{0,144},{1,145},{2,146},{3,147},{4,148},{5,149},{6,150},{7,151},{8... | collective-permute-start | bytes 1966088 | tf_op jit(solution)/shard_map/ppermute | solution.py:413
  48.1 14.2 %collective-permute-start.9 = (bf16[2,64,2560]{2,1,0:T(8,128)(2,1)S(1)}, bf16[2,64,2560]{2,1,0:T(8,128)(2,1)S(1)}, u32[]{:S(2)}, u32[]{:S(2)}) collective-permute-start(bf16[2,64,2560]{2,1,0:T(8,128)(2,1)S(1)} %get-tuple-element.50), channel_id=1, source_target_pairs={{0,152},{1,153},{2,154},{3,155},{4,156},{5,157},{6,158},{7,159},{8... | collective-permute-start | bytes 1966088 | tf_op jit(solution)/shard_map/ppermute | solution.py:413
  51.1 23.9 %collective-permute-start.10 = (bf16[2,64,2560]{2,1,0:T(8,128)(2,1)S(1)}, bf16[2,64,2560]{2,1,0:T(8,128)(2,1)S(1)}, u32[]{:S(2)}, u32[]{:S(2)}) collective-permute-start(bf16[2,64,2560]{2,1,0:T(8,128)(2,1)S(1)} %get-tuple-element.51), channel_id=1, source_target_pairs={{0,8},{1,9},{2,10},{3,11},{4,12},{5,13},{6,14},{7,15},{8,0},{9,1},... | collective-permute-start | bytes 1966088 | tf_op jit(solution)/shard_map/ppermute | solution.py:413
  61.3 16.1 %collective-permute-start.11 = (bf16[64,2560]{1,0:T(8,128)(2,1)S(1)}, bf16[64,2560]{1,0:T(8,128)(2,1)S(1)}, u32[]{:S(2)}, u32[]{:S(2)}) collective-permute-start(bf16[64,2560]{1,0:T(8,128)(2,1)S(1)} %get-tuple-element.52), channel_id=1, source_target_pairs={{0,152},{1,153},{2,154},{3,155},{4,156},{5,157},{6,158},{7,159},{8... | collective-permute-start | bytes 983048 | tf_op jit(solution)/shard_map/ppermute | solution.py:413
  62.3 15.1 %collective-permute-start.12 = (bf16[64,2560]{1,0:T(8,128)(2,1)S(1)}, bf16[64,2560]{1,0:T(8,128)(2,1)S(1)}, u32[]{:S(2)}, u32[]{:S(2)}) collective-permute-start(bf16[64,2560]{1,0:T(8,128)(2,1)S(1)} %get-tuple-element.53), channel_id=1, source_target_pairs={{0,8},{1,9},{2,10},{3,11},{4,12},{5,13},{6,14},{7,15},{8,0},{9,1},... | collective-permute-start | bytes 983048 | tf_op jit(solution)/shard_map/ppermute | solution.py:413
  75.0 10.1 %collective-permute-start.17 = (bf16[128,1280]{1,0:T(8,128)(2,1)S(1)}, bf16[128,1280]{1,0:T(8,128)(2,1)S(1)}, u32[]{:S(2)}, u32[]{:S(2)}) collective-permute-start(bf16[128,1280]{1,0:T(8,128)(2,1)S(1)} %get-tuple-element.61), channel_id=1, source_target_pairs={{0,144},{1,145},{2,146},{3,147},{4,148},{5,149},{6,150},{7,151},{8... | collective-permute-start | bytes 983048 | tf_op jit(solution)/shard_map/ppermute | solution.py:413
  79.2 13.0 %collective-permute-start.15 = (bf16[128,1280]{1,0:T(8,128)(2,1)S(1)}, bf16[128,1280]{1,0:T(8,128)(2,1)S(1)}, u32[]{:S(2)}, u32[]{:S(2)}) collective-permute-start(bf16[128,1280]{1,0:T(8,128)(2,1)S(1)} %get-tuple-element.57), channel_id=1, source_target_pairs={{0,144},{1,145},{2,146},{3,147},{4,148},{5,149},{6,150},{7,151},{8... | collective-permute-start | bytes 983048 | tf_op jit(solution)/shard_map/ppermute | solution.py:413
  83.8 16.4 %collective-permute-start.24 = (bf16[2,128,1280]{2,1,0:T(8,128)(2,1)S(1)}, bf16[2,128,1280]{2,1,0:T(8,128)(2,1)S(1)}, u32[]{:S(2)}, u32[]{:S(2)}) collective-permute-start(bf16[2,128,1280]{2,1,0:T(8,128)(2,1)S(1)} %get-tuple-element.74), channel_id=1, source_target_pairs={{0,8},{1,9},{2,10},{3,11},{4,12},{5,13},{6,14},{7,15},{8,0},{9,1},... | collective-permute-start | bytes 1966088 | tf_op jit(solution)/shard_map/ppermute | solution.py:413
  84.9 14.1 %collective-permute-start.25 = (bf16[2,64,1280]{2,1,0:T(8,128)(2,1)S(1)}, bf16[2,64,1280]{2,1,0:T(8,128)(2,1)S(1)}, u32[]{:S(2)}, u32[]{:S(2)}) collective-permute-start(bf16[2,64,1280]{2,1,0:T(8,128)(2,1)S(1)} %get-tuple-element.76), channel_id=1, source_target_pairs={{0,32},{1,33},{2,34},{3,35},{4,36},{5,37},{6,38},{7,39},{8,16},{9,... | collective-permute-start | bytes 983048 | tf_op jit(solution)/shard_map/ppermute | solution.py:413
  87.4 18.3 %collective-permute-start.19 = (bf16[2,128,1280]{2,1,0:T(8,128)(2,1)S(1)}, bf16[2,128,1280]{2,1,0:T(8,128)(2,1)S(1)}, u32[]{:S(2)}, u32[]{:S(2)}) collective-permute-start(bf16[2,128,1280]{2,1,0:T(8,128)(2,1)S(1)} %get-tuple-element.64), channel_id=1, source_target_pairs={{0,8},{1,9},{2,10},{3,11},{4,12},{5,13},{6,14},{7,15},{8,0},{9,1},... | collective-permute-start | bytes 1966088 | tf_op jit(solution)/shard_map/ppermute | solution.py:413
  95.7 16.3 %collective-permute-start.16 = (bf16[128,2560]{1,0:T(8,128)(2,1)S(1)}, bf16[128,2560]{1,0:T(8,128)(2,1)S(1)}, u32[]{:S(2)}, u32[]{:S(2)}) collective-permute-start(bf16[128,2560]{1,0:T(8,128)(2,1)S(1)} %get-tuple-element.59), channel_id=1, source_target_pairs={{0,144},{1,145},{2,146},{3,147},{4,148},{5,149},{6,150},{7,151},{8... | collective-permute-start | bytes 1966088 | tf_op jit(solution)/shard_map/ppermute | solution.py:413
  99.0 9.7 %collective-permute-start.23 = (bf16[2,64,1280]{2,1,0:T(8,128)(2,1)S(1)}, bf16[2,64,1280]{2,1,0:T(8,128)(2,1)S(1)}, u32[]{:S(2)}, u32[]{:S(2)}) collective-permute-start(bf16[2,64,1280]{2,1,0:T(8,128)(2,1)S(1)} %get-tuple-element.73), channel_id=1, source_target_pairs={{0,32},{1,33},{2,34},{3,35},{4,36},{5,37},{6,38},{7,39},{8,16},{9,... | collective-permute-start | bytes 983048 | tf_op jit(solution)/shard_map/ppermute | solution.py:413
  100.1 16.2 %collective-permute-start.18 = (bf16[2,64,1280]{2,1,0:T(8,128)(2,1)S(1)}, bf16[2,64,1280]{2,1,0:T(8,128)(2,1)S(1)}, u32[]{:S(2)}, u32[]{:S(2)}) collective-permute-start(bf16[2,64,1280]{2,1,0:T(8,128)(2,1)S(1)} %get-tuple-element.63), channel_id=1, source_target_pairs={{0,32},{1,33},{2,34},{3,35},{4,36},{5,37},{6,38},{7,39},{8,16},{9,... | collective-permute-start | bytes 983048 | tf_op jit(solution)/shard_map/ppermute | solution.py:413
  105.2 10.1 %collective-permute-start.26 = (bf16[2,64,1280]{2,1,0:T(8,128)(2,1)S(1)}, bf16[2,64,1280]{2,1,0:T(8,128)(2,1)S(1)}, u32[]{:S(2)}, u32[]{:S(2)}) collective-permute-start(bf16[2,64,1280]{2,1,0:T(8,128)(2,1)S(1)} %get-tuple-element.77), channel_id=1, source_target_pairs={{0,1},{1,2},{2,3},{3,4},{4,5},{5,6},{6,7},{7,0},{8,9},{9,10},{10,1... | collective-permute-start | bytes 983048 | tf_op jit(solution)/shard_map/ppermute | solution.py:413
  105.7 9.6 %collective-permute-start.27 = (bf16[2,64,1280]{2,1,0:T(8,128)(2,1)S(1)}, bf16[2,64,1280]{2,1,0:T(8,128)(2,1)S(1)}, u32[]{:S(2)}, u32[]{:S(2)}) collective-permute-start(bf16[2,64,1280]{2,1,0:T(8,128)(2,1)S(1)} %get-tuple-element.78), channel_id=1, source_target_pairs={{0,7},{1,0},{2,1},{3,2},{4,3},{5,4},{6,5},{7,6},{8,15},{9,8},{10,9... | collective-permute-start | bytes 983048 | tf_op jit(solution)/shard_map/ppermute | solution.py:413
  108.7 12.5 %collective-permute-start.21 = (bf16[2,64,1280]{2,1,0:T(8,128)(2,1)S(1)}, bf16[2,64,1280]{2,1,0:T(8,128)(2,1)S(1)}, u32[]{:S(2)}, u32[]{:S(2)}) collective-permute-start(bf16[2,64,1280]{2,1,0:T(8,128)(2,1)S(1)} %get-tuple-element.67), channel_id=1, source_target_pairs={{0,1},{1,2},{2,3},{3,4},{4,5},{5,6},{6,7},{7,0},{8,9},{9,10},{10,1... | collective-permute-start | bytes 983048 | tf_op jit(solution)/shard_map/ppermute | solution.py:413
  111.9 9.3 %collective-permute-start.22 = (bf16[2,64,1280]{2,1,0:T(8,128)(2,1)S(1)}, bf16[2,64,1280]{2,1,0:T(8,128)(2,1)S(1)}, u32[]{:S(2)}, u32[]{:S(2)}) collective-permute-start(bf16[2,64,1280]{2,1,0:T(8,128)(2,1)S(1)} %get-tuple-element.68), channel_id=1, source_target_pairs={{0,7},{1,0},{2,1},{3,2},{4,3},{5,4},{6,5},{7,6},{8,15},{9,8},{10,9... | collective-permute-start | bytes 983048 | tf_op jit(solution)/shard_map/ppermute | solution.py:413
  (9 other events, 140.0 us)

commit v4 on v3

--- a/solution.py
+++ b/solution.py
@@ -29,8 +29,10 @@
     for d in range(n_dp):
         for t in range(n_tm):
             for h in range(n_h):
-                e, u, g = fn(d, t, h)
-                pairs.append(((d * n_tm + t) * n_h + h, (e * n_tm + u) * n_h + g % n_h))
+                to = fn(d, t, h)
+                if to is not None:
+                    e, u, g = to
+                    pairs.append(((d * n_tm + t) * n_h + h, (e * n_tm + u) * n_h + g % n_h))
     return pairs
 
 
@@ -238,13 +240,9 @@
     y = lax.axis_index("dp") % 4
     core = lax.axis_index("tm") % 2
     toward = jnp.where(core == 0, 3, 1)
-    shard = {"own": y, "near": (y + toward) % 4, "far": (y + 4 - toward) % 4}.get(which, (y + 2) % 4)
-    at = shard * 320
-    if which == "c0":
-        at = at + core * 160
-    if which == "c1":
-        at = at + (1 - core) * 160
-    return at
+    shard = {"own": y, "near": (y + toward) % 4, "far": (y + 4 - toward) % 4, "c": (y + 2) % 4}
+    name, part = (which + ":").split(":")[:2]
+    return shard[name] * 320 + {"": 0, "same": core * 160, "other": (1 - core) * 160}[part]
 
 
 def put_rows(dst_ref, src_ref, which):
@@ -259,21 +257,21 @@
     lax.fori_loop(0, rows // 32, step, 0)
 
 
-def gather_kernel(own_ref, near_ref, far_ref, w_ref):
+def gather_kernel(own_ref, na_ref, nb_ref, fa_ref, fb_ref, w_ref):
     put_rows(w_ref, own_ref, "own")
-    put_rows(w_ref, near_ref, "near")
-    put_rows(w_ref, far_ref, "far")
-
-
-def gather_rows(own, near, far):
-    return call(
-        gather_kernel, (in_vmem((W_HALF, 2560), BF16),), (own, near, far), moved=10_000_000
-    )[0]
+    put_rows(w_ref, na_ref, "near:same")
+    put_rows(w_ref, nb_ref, "near:other")
+    put_rows(w_ref, fa_ref, "far:other")
+    put_rows(w_ref, fb_ref, "far:same")
+
+
+def gather_rows(*parts):
+    return call(gather_kernel, (in_vmem((W_HALF, 2560), BF16),), parts, moved=10_000_000)[0]
 
 
 def grad_proj_kernel(w_in, c0_ref, c1_ref, mine_ref, theirs_ref, w_ref, o_ref, t_ref):
-    put_rows(w_ref, c0_ref, "c0")
-    put_rows(w_ref, c1_ref, "c1")
+    put_rows(w_ref, c0_ref, "c:same")
+    put_rows(w_ref, c1_ref, "c:other")
 
     def step(n, carry):
         r = pl.ds(pl.multiple_of(n * 256, 256), 256)
@@ -356,39 +354,44 @@
     )
 
 
-def prep_kernel(k_ref, v_ref, zlk_ref, zhk_ref, zlv_ref, zhv_ref, tx_ref, tc_ref, sems):
-    copies = []
-    for src, lo_ref, hi_ref in ((k_ref, zlk_ref, zhk_ref), (v_ref, zlv_ref, zhv_ref)):
-        for f in range(4):
-            rows = pl.ds(f * 16, 16)
-            copies.append((src.at[pl.ds(f * 32 + 16, 16)], hi_ref.at[rows]))
-            copies.append((src.at[pl.ds(f * 32, 16)], lo_ref.at[rows]))
-    for kv, src in ((0, k_ref), (1, v_ref)):
-        copies.append((src.at[pl.ds(side_rows("x"), 64)], tx_ref.at[kv]))
-        copies.append((src.at[pl.ds(side_rows("c"), 64)], tc_ref.at[kv]))
-    copies = [pltpu.make_async_copy(x, y, sems.at[n]) for n, (x, y) in enumerate(copies)]
+def run_copies(pairs, sems):
+    copies = [pltpu.make_async_copy(x, y, sems.at[n]) for n, (x, y) in enumerate(pairs)]
     for cp in copies:
         cp.start()
     for cp in copies:
         cp.wait()
 
 
-def prep(keys, values):
-    return call(
-        prep_kernel, (in_vmem((64, 2560), BF16),) * 4 + (in_vmem((2, 64, 2560), BF16),) * 2,
-        (keys, values), moved=4_000_000, scratch=(pltpu.SemaphoreType.DMA((20,)),), hbm_in=2,
-    )
-
-
-def slice_kernel(near_ref, part_ref):
+def row_halo(src, lo_ref, hi_ref):
+    pairs = []
+    for f in range(4):
+        rows = pl.ds(f * 16, 16)
+        pairs.append((src.at[pl.ds(f * 32 + 16, 16)], hi_ref.at[rows]))
+        pairs.append((src.at[pl.ds(f * 32, 16)], lo_ref.at[rows]))
+    return pairs
+
+
+def prep_k_kernel(w_ref, k_ref, wa_ref, wb_ref, lo_ref, hi_ref, sems):
     core = lax.axis_index("tm") % 2
-
-    def step(i, carry):
-        r = pl.multiple_of(i * 32, 32)
-        part_ref[pl.ds(r, 32), :] = near_ref[pl.ds(pl.multiple_of(core * 160 + r, 32), 32), :]
-        return carry
-
-    lax.fori_loop(0, 5, step, 0)
+    same = pl.ds(pl.multiple_of(core * 160, 160), 160)
+    other = pl.ds(pl.multiple_of((1 - core) * 160, 160), 160)
+    cut = [(w_ref.at[same], wa_ref), (w_ref.at[other], wb_ref)]
+    run_copies(row_halo(k_ref, lo_ref, hi_ref) + cut, sems)
+
+
+def prep_v_kernel(k_ref, v_ref, lo_ref, hi_ref, tx_ref, tc_ref, sems):
+    pairs = row_halo(v_ref, lo_ref, hi_ref)
+    for kv, src in ((0, k_ref), (1, v_ref)):
+        pairs.append((src.at[pl.ds(side_rows("x"), 64)], tx_ref.at[kv]))
+        pairs.append((src.at[pl.ds(side_rows("c"), 64)], tc_ref.at[kv]))
+    run_copies(pairs, sems)
+
+
+def prep(kernel, first, shapes, sources):
+    return call(
+        kernel, tuple(in_vmem(x, BF16) for x in (*first, *shapes)), sources, moved=3_000_000,
+        scratch=(pltpu.SemaphoreType.DMA((12,)),), hbm_in=2,
+    )
 
 
 def add_kernel(part_ref, remote_ref, out_ref):
@@ -418,6 +421,7 @@
     up_z = lambda d, t, h: (d, t, h + 1)
     down_z = lambda d, t, h: (d, t, h - 1)
     other_chip = lambda d, t, h: (d, 3 - t, h) if t in (1, 2) else (d ^ 4, 3 - t, h)
+    middle_chip = lambda d, t, h: (d, 3 - t, h) if t in (1, 2) else None
     other_chip_mid = lambda d, t, h: (d, 3 - t, h) if t in (1, 2) else (d, t, h ^ 1)
     other_chip_late = lambda d, t, h: (d, 3 - t, h) if t in (1, 2) else (d ^ 1, t, h)
 
@@ -425,14 +429,17 @@
     flat = lambda a: a.reshape(tokens, a.shape[-1])
     q, k, v, d_out = flat(queries), flat(keys), flat(values), flat(d_outputs)
 
-    w_near = send(projection, ring_y)
+    half_row = ((64, 2560),) * 2
+    wa_s, wb_s, k_lo_s, k_hi_s = prep(prep_k_kernel, ((160, 2560),) * 2, half_row, (projection, k))
+    v_lo_s, v_hi_s, tx_s, tc_s = prep(prep_v_kernel, half_row, ((2, 64, 2560),) * 2, (k, v))
+    near_a = send(wa_s, ring_y)
+    near_b = send(wb_s, ring_y)
     their_d_out = send(d_out, pair_chip)
-    k_lo_s, k_hi_s, v_lo_s, v_hi_s, tx_s, tc_s = prep(k, v)
     k_lo = send(k_hi_s, up_z)
     k_hi = send(k_lo_s, down_z)
     v_lo = send(v_hi_s, up_z)
     v_hi = send(v_lo_s, down_z)
-    t_x = send(tx_s, other_chip)
+    t_x = send(tx_s, middle_chip)
     t_c = send(tc_s, other_core)
     cxk_s, cck_s = corners(k_lo, k_hi)
     cxk = send(cxk_s, other_chip)
@@ -440,11 +447,11 @@
     cxv_s, ccv_s = corners(v_lo, v_hi)
     cxv = send(cxv_s, other_chip_mid)
     ccv = send(ccv_s, other_core)
-    w_far = send(w_near, other_core)
-    (w_part,) = call(slice_kernel, (in_vmem((160, 2560), BF16),), (w_near,))
-    w_c0 = send(w_part, ring_y)
+    far_a = send(near_a, other_core)
+    far_b = send(near_b, other_core)
+    w_c0 = send(near_a, ring_y)
     w_c1 = send(w_c0, other_core)
-    rows = gather_rows(projection, w_near, w_far)
+    rows = gather_rows(projection, near_a, near_b, far_a, far_b)
 
     operands = (q, k, v, k_lo, k_hi, v_lo, v_hi, t_x, t_c, cxk, cck, cxv, ccv)
     att_remote, p_remote = forward_half("remote", operands)

time: 123 us -> 112 us (0.911)
  starting transfers between devices: 46.4 us -> 36.2 us
  waiting for transfers between devices: 52.8 us -> 50 us
  Pallas kernels: 22.2 us -> 23.7 us
    ppermute x28 -> x30, starting transfers between devices: 46.4 us -> 36.2 us  [send(): return lax.ppermute(x, AXES, make_perm(shape, fn))]
    ppermute x28 -> x30, waiting for transfers between devices: 52.8 us -> 50 us  [send(): return lax.ppermute(x, AXES, make_perm(shape, fn))]
    pallas_call x16, Pallas kernels: 22.2 us -> 23.7 us  [call(): pl.pallas_call(kernel, out_shape=tuple(outs), in_specs=[vm] * len(near) +...]
  transfers between devices with their start and end apart: 28 -> 30, of which waited for: 12 -> 12; matrix products, arithmetic and copies ran while one was open for 0% -> 0% of each run, Pallas kernels for 17% -> 19%
where the time goes in v4:
time: 112 us; the launch traced here: 111 us
  waiting for transfers between devices  50 us (45%)
  starting transfers between devices  36.2 us (32%)
  Pallas kernels  23.7 us (21%)
    ppermute x30, waiting for transfers between devices, send(): return lax.ppermute(x, AXES, make_perm(shape, fn))  50 us
    ppermute x30, starting transfers between devices, send(): return lax.ppermute(x, AXES, make_perm(shape, fn))  36.2 us
    pallas_call x16, Pallas kernels, call(): pl.pallas_call(kernel, out_shape=tuple(outs), in_specs=[vm] * len(near) +...  23.7 us
  transfers between devices with their start and end apart: 30, of which 12 were waited for; matrix products, arithmetic and copies ran while one was open for 0% of the time, Pallas kernels for 19%

profile of v4, /device:TPU:1, one launch (start us, length us, event | category | flops | bytes accessed | tf_op | source)
XLA Modules:
  0.0 111.0 jit_solution(750345256008276520)
XLA Ops:
  0.6 1.9 %shard_map.84 = (bf16[160,2560]{1,0:T(8,128)(2,1)S(1)}, bf16[160,2560]{1,0:T(8,128)(2,1)S(1)}, bf16[64,2560]{1,0:T(8,128)(2,1)S(1)}, bf16[64,2560]{1,0:T(8,128)(2,1)S(1)}) custom-call(bf16[320,2560]{1,0:T(8,128)(2,1)} %own_ref.1, bf16[128,2560]{1,0:T(8,128)(2,1)} %bitcast.8), custom_call_target="tpu_custom_call" | custom-call | bytes 3000000 | tf_op jit(solution)/shard_map/pallas_call | solution.py:53
  2.5 3.6 %collective-permute-start = (bf16[160,2560]{1,0:T(8,128)(2,1)S(1)}, bf16[160,2560]{1,0:T(8,128)(2,1)S(1)}, u32[]{:S(2)}, u32[]{:S(2)}) collective-permute-start(bf16[160,2560]{1,0:T(8,128)(2,1)S(1)} %get-tuple-element.47), channel_id=1, source_target_pairs={{0,32},{1,33},{2,34},{3,35},{4,36},{5,37},{6,38},{7,39},{8,104},{9... | collective-permute-start | bytes 2457608 | tf_op jit(solution)/shard_map/ppermute | solution.py:416
  6.6 8.8 %collective-permute-done.na_ref = bf16[160,2560]{1,0:T(8,128)(2,1)S(1)} collective-permute-done((bf16[160,2560]{1,0:T(8,128)(2,1)S(1)}, bf16[160,2560]{1,0:T(8,128)(2,1)S(1)}, u32[]{:S(2)}, u32[]{:S(2)}) %collective-permute-start) | collective-permute-done | bytes 819232 | tf_op jit(solution)/shard_map/ppermute | solution.py:416
  15.4 3.1 %collective-permute-start.4 = (bf16[160,2560]{1,0:T(8,128)(2,1)S(1)}, bf16[160,2560]{1,0:T(8,128)(2,1)S(1)}, u32[]{:S(2)}, u32[]{:S(2)}) collective-permute-start(bf16[160,2560]{1,0:T(8,128)(2,1)S(1)} %collective-permute-done.na_ref), channel_id=1, source_target_pairs={{0,32},{1,33},{2,34},{3,35},{4,36},{5,37},{6,38},{7,39},{8,104},{9... | collective-permute-start | bytes 2457608 | tf_op jit(solution)/shard_map/ppermute | solution.py:416
  20.2 3.9 %collective-permute-start.8 = (bf16[64,2560]{1,0:T(8,128)(2,1)S(1)}, bf16[64,2560]{1,0:T(8,128)(2,1)S(1)}, u32[]{:S(2)}, u32[]{:S(2)}) collective-permute-start(bf16[64,2560]{1,0:T(8,128)(2,1)S(1)} %get-tuple-element.51), channel_id=1, source_target_pairs={{0,7},{1,0},{2,1},{3,2},{4,3},{5,4},{6,5},{7,6},{8,15},{9,8},{10,9... | collective-permute-start | bytes 983048 | tf_op jit(solution)/shard_map/ppermute | solution.py:416
  24.1 1.8 %shard_map.87 = (bf16[64,2560]{1,0:T(8,128)(2,1)S(1)}, bf16[64,2560]{1,0:T(8,128)(2,1)S(1)}, bf16[2,64,2560]{2,1,0:T(8,128)(2,1)S(1)}, bf16[2,64,2560]{2,1,0:T(8,128)(2,1)S(1)}) custom-call(bf16[128,2560]{1,0:T(8,128)(2,1)} %bitcast.9, bf16[128,2560]{1,0:T(8,128)(2,1)} %bitcast.14), custom_call_target="tpu_custom_call" | custom-call | bytes 3000000 | tf_op jit(solution)/shard_map/pallas_call | solution.py:53
  26.0 6.4 %collective-permute-done.7.lo_ref.rest_0_ = bf16[64,2560]{1,0:T(8,128)(2,1)S(1)} collective-permute-done((bf16[64,2560]{1,0:T(8,128)(2,1)S(1)}, bf16[64,2560]{1,0:T(8,128)(2,1)S(1)}, u32[]{:S(2)}, u32[]{:S(2)}) %collective-permute-start.7) | collective-permute-done | bytes 327712 | tf_op jit(solution)/shard_map/ppermute | solution.py:416
  32.4 2.5 %collective-permute-start.6 = (bf16[128,2560]{1,0:T(8,128)(2,1)S(1)}, bf16[128,2560]{1,0:T(8,128)(2,1)S(1)}, u32[]{:S(2)}, u32[]{:S(2)}) collective-permute-start(bf16[128,2560]{1,0:T(8,128)(2,1)S(1)} %bitcast.23), channel_id=1, source_target_pairs={{0,144},{1,145},{2,146},{3,147},{4,148},{5,149},{6,150},{7,151},{8... | collective-permute-start | bytes 1966088 | tf_op jit(solution)/shard_map/ppermute | solution.py:416
  36.3 2.7 %collective-permute-done.9.lo_ref.rest_2_ = bf16[64,2560]{1,0:T(8,128)(2,1)S(1)} collective-permute-done((bf16[64,2560]{1,0:T(8,128)(2,1)S(1)}, bf16[64,2560]{1,0:T(8,128)(2,1)S(1)}, u32[]{:S(2)}, u32[]{:S(2)}) %collective-permute-start.9) | collective-permute-done | bytes 327712 | tf_op jit(solution)/shard_map/ppermute | solution.py:416
  39.7 4.5 %collective-permute-done.10.hi_ref.rest_3_ = bf16[64,2560]{1,0:T(8,128)(2,1)S(1)} collective-permute-done((bf16[64,2560]{1,0:T(8,128)(2,1)S(1)}, bf16[64,2560]{1,0:T(8,128)(2,1)S(1)}, u32[]{:S(2)}, u32[]{:S(2)}) %collective-permute-start.10) | collective-permute-done | bytes 327712 | tf_op jit(solution)/shard_map/ppermute | solution.py:416
  44.2 2.5 %collective-permute-start.11 = (bf16[2,64,2560]{2,1,0:T(8,128)(2,1)S(1)}, bf16[2,64,2560]{2,1,0:T(8,128)(2,1)S(1)}, u32[]{:S(2)}, u32[]{:S(2)}) collective-permute-start(bf16[2,64,2560]{2,1,0:T(8,128)(2,1)S(1)} %get-tuple-element.54), channel_id=1, source_target_pairs={{8,16},{9,17},{10,18},{11,19},{12,20},{13,21},{14,22},{15,23},{16,... | collective-permute-start | bytes 1966088 | tf_op jit(solution)/shard_map/ppermute | solution.py:416
  46.7 3.5 %collective-permute-done.6.theirs_ref = bf16[128,2560]{1,0:T(8,128)(2,1)S(1)} collective-permute-done((bf16[128,2560]{1,0:T(8,128)(2,1)S(1)}, bf16[128,2560]{1,0:T(8,128)(2,1)S(1)}, u32[]{:S(2)}, u32[]{:S(2)}) %collective-permute-start.6) | collective-permute-done | bytes 655392 | tf_op jit(solution)/shard_map/ppermute | solution.py:416
  50.9 5.5 %collective-permute-done.11.rest_4_ = bf16[2,64,2560]{2,1,0:T(8,128)(2,1)S(1)} collective-permute-done((bf16[2,64,2560]{2,1,0:T(8,128)(2,1)S(1)}, bf16[2,64,2560]{2,1,0:T(8,128)(2,1)S(1)}, u32[]{:S(2)}, u32[]{:S(2)}) %collective-permute-start.11) | collective-permute-done | bytes 655392 | tf_op jit(solution)/shard_map/ppermute | solution.py:416
  58.7 5.0 %shard_map.86 = (bf16[1280,2560]{1,0:T(8,128)(2,1)S(1)}, bf16[128,1280]{1,0:T(8,128)(2,1)S(1)}, bf16[128,1280]{1,0:T(8,128)(2,1)S(1)}) custom-call(bf16[1280,2560]{1,0:T(8,128)(2,1)S(1)} %shard_map.85.w_in, bf16[160,2560]{1,0:T(8,128)(2,1)S(1)} %collective-permute-done.4.c0_ref, ...), custom_call_target="tpu_custom_call", output_to_operand_aliasing={{0}: (0, {})} | custom-call | flops 1677721600 | bytes 9000000 | tf_op jit(solution)/shard_map/pallas_call | solution.py:53
  70.2 2.2 %shard_map.96 = (bf16[128,1280]{1,0:T(8,128)(2,1)S(1)}, f32[2,128,1280]{2,1,0:T(8,128)S(1)}, f32[2,128,1280]{2,1,0:T(8,128)S(1)}, bf16[2,64,1280]{2,1,0:T(8,128)...) custom-call(bf16[128,2560]{1,0:T(8,128)(2,1)S(1)} %bitcast.21, ...), custom_call_target="tpu_custom_call" | custom-call | flops 503316480 | bytes 12000000 | tf_op jit(solution)/shard_map/pallas_call | solution.py:53
  74.0 2.2 %shard_map.94 = (bf16[128,1280]{1,0:T(8,128)(2,1)S(1)}, f32[2,128,1280]{2,1,0:T(8,128)S(1)}, f32[2,128,1280]{2,1,0:T(8,128)S(1)}, bf16[2,64,1280]{2,1,0:T(8,128)...) custom-call(bf16[128,2560]{1,0:T(8,128)(2,1)S(1)} %bitcast.22, ...), custom_call_target="tpu_custom_call" | custom-call | flops 503316480 | bytes 12000000 | tf_op jit(solution)/shard_map/pallas_call | solution.py:53
  76.2 2.4 %collective-permute-start.21 = (bf16[2,128,1280]{2,1,0:T(8,128)(2,1)S(1)}, bf16[2,128,1280]{2,1,0:T(8,128)(2,1)S(1)}, u32[]{:S(2)}, u32[]{:S(2)}) collective-permute-start(bf16[2,128,1280]{2,1,0:T(8,128)(2,1)S(1)} %get-tuple-element.68), channel_id=1, source_target_pairs={{0,8},{1,9},{2,10},{3,11},{4,12},{5,13},{6,14},{7,15},{8,0},{9,1},... | collective-permute-start | bytes 1966088 | tf_op jit(solution)/shard_map/ppermute | solution.py:416
  78.6 2.4 %collective-permute-done.17.theirs_ref = bf16[128,1280]{1,0:T(8,128)(2,1)S(1)} collective-permute-done((bf16[128,1280]{1,0:T(8,128)(2,1)S(1)}, bf16[128,1280]{1,0:T(8,128)(2,1)S(1)}, u32[]{:S(2)}, u32[]{:S(2)}) %collective-permute-start.17) | collective-permute-done | bytes 327712 | tf_op jit(solution)/shard_map/ppermute | solution.py:416
  81.0 3.5 %shard_map.92 = (f32[128,2560]{1,0:T(8,128)S(1)}, bf16[128,2560]{1,0:T(8,128)(2,1)S(1)}) custom-call(bf16[1280,2560]{1,0:T(8,128)(2,1)S(1)} %get-tuple-element.49.w_ref, bf16[128,1280]{1,0:T(8,128)(2,1)S(1)} %get-tuple-element.60.mine_ref, bf16[128,1280]{1,0:T(8,128)(2,1)S(1)} %collective-permute-done.17.theirs_ref), custom_call_target="tpu_custom_call" | custom-call | flops 1677721600 | bytes 9000000 | tf_op jit(solution)/shard_map/pallas_call | solution.py:53
  87.9 4.8 %collective-permute-done.22.fx_ref = bf16[2,64,1280]{2,1,0:T(8,128)(2,1)S(1)} collective-permute-done((bf16[2,64,1280]{2,1,0:T(8,128)(2,1)S(1)}, bf16[2,64,1280]{2,1,0:T(8,128)(2,1)S(1)}, u32[]{:S(2)}, u32[]{:S(2)}) %collective-permute-start.22) | collective-permute-done | bytes 327712 | tf_op jit(solution)/shard_map/ppermute | solution.py:416
  92.8 3.3 %collective-permute-start.29 = (bf16[2,64,1280]{2,1,0:T(8,128)(2,1)S(1)}, bf16[2,64,1280]{2,1,0:T(8,128)(2,1)S(1)}, u32[]{:S(2)}, u32[]{:S(2)}) collective-permute-start(bf16[2,64,1280]{2,1,0:T(8,128)(2,1)S(1)} %get-tuple-element.82), channel_id=1, source_target_pairs={{0,7},{1,0},{2,1},{3,2},{4,3},{5,4},{6,5},{7,6},{8,15},{9,8},{10,9... | collective-permute-start | bytes 983048 | tf_op jit(solution)/shard_map/ppermute | solution.py:416
  96.3 4.4 %collective-permute-done.18.remote_ref = bf16[128,2560]{1,0:T(8,128)(2,1)S(1)} collective-permute-done((bf16[128,2560]{1,0:T(8,128)(2,1)S(1)}, bf16[128,2560]{1,0:T(8,128)(2,1)S(1)}, u32[]{:S(2)}, u32[]{:S(2)}) %collective-permute-start.18) | collective-permute-done | bytes 655392 | tf_op jit(solution)/shard_map/ppermute | solution.py:416
  100.7 2.1 %collective-permute-start.24 = (bf16[2,64,1280]{2,1,0:T(8,128)(2,1)S(1)}, bf16[2,64,1280]{2,1,0:T(8,128)(2,1)S(1)}, u32[]{:S(2)}, u32[]{:S(2)}) collective-permute-start(bf16[2,64,1280]{2,1,0:T(8,128)(2,1)S(1)} %get-tuple-element.72), channel_id=1, source_target_pairs={{0,7},{1,0},{2,1},{3,2},{4,3},{5,4},{6,5},{7,6},{8,15},{9,8},{10,9... | collective-permute-start | bytes 983048 | tf_op jit(solution)/shard_map/ppermute | solution.py:416
  104.8 5.0 %collective-permute-done.23.lo_ref = bf16[2,64,1280]{2,1,0:T(8,128)(2,1)S(1)} collective-permute-done((bf16[2,64,1280]{2,1,0:T(8,128)(2,1)S(1)}, bf16[2,64,1280]{2,1,0:T(8,128)(2,1)S(1)}, u32[]{:S(2)}, u32[]{:S(2)}) %collective-permute-start.23) | collective-permute-done | bytes 327712 | tf_op jit(solution)/shard_map/ppermute | solution.py:416
  (62 shorter events, 21.9 us)
Async XLA Ops:
  2.5 12.9 %collective-permute-start = (bf16[160,2560]{1,0:T(8,128)(2,1)S(1)}, bf16[160,2560]{1,0:T(8,128)(2,1)S(1)}, u32[]{:S(2)}, u32[]{:S(2)}) collective-permute-start(bf16[160,2560]{1,0:T(8,128)(2,1)S(1)} %get-tuple-element.47), channel_id=1, source_target_pairs={{0,32},{1,33},{2,34},{3,35},{4,36},{5,37},{6,38},{7,39},{8,104},{9... | collective-permute-start | bytes 2457608 | tf_op jit(solution)/shard_map/ppermute | solution.py:416
  6.1 32.9 %collective-permute-start.1 = (bf16[160,2560]{1,0:T(8,128)(2,1)S(1)}, bf16[160,2560]{1,0:T(8,128)(2,1)S(1)}, u32[]{:S(2)}, u32[]{:S(2)}) collective-permute-start(bf16[160,2560]{1,0:T(8,128)(2,1)S(1)} %get-tuple-element.48), channel_id=1, source_target_pairs={{0,32},{1,33},{2,34},{3,35},{4,36},{5,37},{6,38},{7,39},{8,104},{9... | collective-permute-start | bytes 2457608 | tf_op jit(solution)/shard_map/ppermute | solution.py:416
  15.4 24.1 %collective-permute-start.4 = (bf16[160,2560]{1,0:T(8,128)(2,1)S(1)}, bf16[160,2560]{1,0:T(8,128)(2,1)S(1)}, u32[]{:S(2)}, u32[]{:S(2)}) collective-permute-start(bf16[160,2560]{1,0:T(8,128)(2,1)S(1)} %collective-permute-done.na_ref), channel_id=1, source_target_pairs={{0,32},{1,33},{2,34},{3,35},{4,36},{5,37},{6,38},{7,39},{8,104},{9... | collective-permute-start | bytes 2457608 | tf_op jit(solution)/shard_map/ppermute | solution.py:416
  18.5 13.8 %collective-permute-start.7 = (bf16[64,2560]{1,0:T(8,128)(2,1)S(1)}, bf16[64,2560]{1,0:T(8,128)(2,1)S(1)}, u32[]{:S(2)}, u32[]{:S(2)}) collective-permute-start(bf16[64,2560]{1,0:T(8,128)(2,1)S(1)} %get-tuple-element.50), channel_id=1, source_target_pairs={{0,1},{1,2},{2,3},{3,4},{4,5},{5,6},{6,7},{7,0},{8,9},{9,10},{10,1... | collective-permute-start | bytes 983048 | tf_op jit(solution)/shard_map/ppermute | solution.py:416
  20.2 14.7 %collective-permute-start.8 = (bf16[64,2560]{1,0:T(8,128)(2,1)S(1)}, bf16[64,2560]{1,0:T(8,128)(2,1)S(1)}, u32[]{:S(2)}, u32[]{:S(2)}) collective-permute-start(bf16[64,2560]{1,0:T(8,128)(2,1)S(1)} %get-tuple-element.51), channel_id=1, source_target_pairs={{0,7},{1,0},{2,1},{3,2},{4,3},{5,4},{6,5},{7,6},{8,15},{9,8},{10,9... | collective-permute-start | bytes 983048 | tf_op jit(solution)/shard_map/ppermute | solution.py:416
  25.9 13.1 %collective-permute-start.9 = (bf16[64,2560]{1,0:T(8,128)(2,1)S(1)}, bf16[64,2560]{1,0:T(8,128)(2,1)S(1)}, u32[]{:S(2)}, u32[]{:S(2)}) collective-permute-start(bf16[64,2560]{1,0:T(8,128)(2,1)S(1)} %get-tuple-element.52), channel_id=1, source_target_pairs={{0,1},{1,2},{2,3},{3,4},{4,5},{5,6},{6,7},{7,0},{8,9},{9,10},{10,1... | collective-permute-start | bytes 983048 | tf_op jit(solution)/shard_map/ppermute | solution.py:416
  32.4 17.8 %collective-permute-start.6 = (bf16[128,2560]{1,0:T(8,128)(2,1)S(1)}, bf16[128,2560]{1,0:T(8,128)(2,1)S(1)}, u32[]{:S(2)}, u32[]{:S(2)}) collective-permute-start(bf16[128,2560]{1,0:T(8,128)(2,1)S(1)} %bitcast.23), channel_id=1, source_target_pairs={{0,144},{1,145},{2,146},{3,147},{4,148},{5,149},{6,150},{7,151},{8... | collective-permute-start | bytes 1966088 | tf_op jit(solution)/shard_map/ppermute | solution.py:416
  39.0 17.7 %collective-permute-start.2 = (bf16[160,2560]{1,0:T(8,128)(2,1)S(1)}, bf16[160,2560]{1,0:T(8,128)(2,1)S(1)}, u32[]{:S(2)}, u32[]{:S(2)}) collective-permute-start(bf16[160,2560]{1,0:T(8,128)(2,1)S(1)} %collective-permute-done.na_ref), channel_id=1, source_target_pairs={{0,8},{1,9},{2,10},{3,11},{4,12},{5,13},{6,14},{7,15},{8,0},{9,1},... | collective-permute-start | bytes 2457608 | tf_op jit(solution)/shard_map/ppermute | solution.py:416
  39.1 17.7 %collective-permute-start.3 = (bf16[160,2560]{1,0:T(8,128)(2,1)S(1)}, bf16[160,2560]{1,0:T(8,128)(2,1)S(1)}, u32[]{:S(2)}, u32[]{:S(2)}) collective-permute-start(bf16[160,2560]{1,0:T(8,128)(2,1)S(1)} %collective-permute-done.1.nb_ref), channel_id=1, source_target_pairs={{0,8},{1,9},{2,10},{3,11},{4,12},{5,13},{6,14},{7,15},{8,0},{9,1},... | collective-permute-start | bytes 2457608 | tf_op jit(solution)/shard_map/ppermute | solution.py:416
  39.6 18.7 %collective-permute-start.5 = (bf16[160,2560]{1,0:T(8,128)(2,1)S(1)}, bf16[160,2560]{1,0:T(8,128)(2,1)S(1)}, u32[]{:S(2)}, u32[]{:S(2)}) collective-permute-start(bf16[160,2560]{1,0:T(8,128)(2,1)S(1)} %collective-permute-done.4.c0_ref), channel_id=1, source_target_pairs={{0,8},{1,9},{2,10},{3,11},{4,12},{5,13},{6,14},{7,15},{8,0},{9,1},... | collective-permute-start | bytes 2457608 | tf_op jit(solution)/shard_map/ppermute | solution.py:416
  44.2 12.2 %collective-permute-start.11 = (bf16[2,64,2560]{2,1,0:T(8,128)(2,1)S(1)}, bf16[2,64,2560]{2,1,0:T(8,128)(2,1)S(1)}, u32[]{:S(2)}, u32[]{:S(2)}) collective-permute-start(bf16[2,64,2560]{2,1,0:T(8,128)(2,1)S(1)} %get-tuple-element.54), channel_id=1, source_target_pairs={{8,16},{9,17},{10,18},{11,19},{12,20},{13,21},{14,22},{15,23},{16,... | collective-permute-start | bytes 1966088 | tf_op jit(solution)/shard_map/ppermute | solution.py:416
  50.2 13.5 %collective-permute-start.12 = (bf16[2,64,2560]{2,1,0:T(8,128)(2,1)S(1)}, bf16[2,64,2560]{2,1,0:T(8,128)(2,1)S(1)}, u32[]{:S(2)}, u32[]{:S(2)}) collective-permute-start(bf16[2,64,2560]{2,1,0:T(8,128)(2,1)S(1)} %get-tuple-element.55), channel_id=1, source_target_pairs={{0,8},{1,9},{2,10},{3,11},{4,12},{5,13},{6,14},{7,15},{8,0},{9,1},... | collective-permute-start | bytes 1966088 | tf_op jit(solution)/shard_map/ppermute | solution.py:416
  56.7 9.7 %collective-permute-start.15 = (bf16[64,2560]{1,0:T(8,128)(2,1)S(1)}, bf16[64,2560]{1,0:T(8,128)(2,1)S(1)}, u32[]{:S(2)}, u32[]{:S(2)}) collective-permute-start(bf16[64,2560]{1,0:T(8,128)(2,1)S(1)} %get-tuple-element.58), channel_id=1, source_target_pairs={{0,1},{1,0},{2,3},{3,2},{4,5},{5,4},{6,7},{7,6},{8,16},{9,17},{10,... | collective-permute-start | bytes 983048 | tf_op jit(solution)/shard_map/ppermute | solution.py:416
  63.7 10.3 %collective-permute-start.19 = (bf16[128,1280]{1,0:T(8,128)(2,1)S(1)}, bf16[128,1280]{1,0:T(8,128)(2,1)S(1)}, u32[]{:S(2)}, u32[]{:S(2)}) collective-permute-start(bf16[128,1280]{1,0:T(8,128)(2,1)S(1)} %get-tuple-element.65), channel_id=1, source_target_pairs={{0,144},{1,145},{2,146},{3,147},{4,148},{5,149},{6,150},{7,151},{8... | collective-permute-start | bytes 983048 | tf_op jit(solution)/shard_map/ppermute | solution.py:416
  68.2 12.8 %collective-permute-start.17 = (bf16[128,1280]{1,0:T(8,128)(2,1)S(1)}, bf16[128,1280]{1,0:T(8,128)(2,1)S(1)}, u32[]{:S(2)}, u32[]{:S(2)}) collective-permute-start(bf16[128,1280]{1,0:T(8,128)(2,1)S(1)} %get-tuple-element.61), channel_id=1, source_target_pairs={{0,144},{1,145},{2,146},{3,147},{4,148},{5,149},{6,150},{7,151},{8... | collective-permute-start | bytes 983048 | tf_op jit(solution)/shard_map/ppermute | solution.py:416
  72.5 15.2 %collective-permute-start.26 = (bf16[2,128,1280]{2,1,0:T(8,128)(2,1)S(1)}, bf16[2,128,1280]{2,1,0:T(8,128)(2,1)S(1)}, u32[]{:S(2)}, u32[]{:S(2)}) collective-permute-start(bf16[2,128,1280]{2,1,0:T(8,128)(2,1)S(1)} %get-tuple-element.78), channel_id=1, source_target_pairs={{0,8},{1,9},{2,10},{3,11},{4,12},{5,13},{6,14},{7,15},{8,0},{9,1},... | collective-permute-start | bytes 1966088 | tf_op jit(solution)/shard_map/ppermute | solution.py:416
  73.6 12.3 %collective-permute-start.27 = (bf16[2,64,1280]{2,1,0:T(8,128)(2,1)S(1)}, bf16[2,64,1280]{2,1,0:T(8,128)(2,1)S(1)}, u32[]{:S(2)}, u32[]{:S(2)}) collective-permute-start(bf16[2,64,1280]{2,1,0:T(8,128)(2,1)S(1)} %get-tuple-element.80), channel_id=1, source_target_pairs={{0,32},{1,33},{2,34},{3,35},{4,36},{5,37},{6,38},{7,39},{8,16},{9,... | collective-permute-start | bytes 983048 | tf_op jit(solution)/shard_map/ppermute | solution.py:416
  76.2 16.6 %collective-permute-start.21 = (bf16[2,128,1280]{2,1,0:T(8,128)(2,1)S(1)}, bf16[2,128,1280]{2,1,0:T(8,128)(2,1)S(1)}, u32[]{:S(2)}, u32[]{:S(2)}) collective-permute-start(bf16[2,128,1280]{2,1,0:T(8,128)(2,1)S(1)} %get-tuple-element.68), channel_id=1, source_target_pairs={{0,8},{1,9},{2,10},{3,11},{4,12},{5,13},{6,14},{7,15},{8,0},{9,1},... | collective-permute-start | bytes 1966088 | tf_op jit(solution)/shard_map/ppermute | solution.py:416
  84.5 16.2 %collective-permute-start.18 = (bf16[128,2560]{1,0:T(8,128)(2,1)S(1)}, bf16[128,2560]{1,0:T(8,128)(2,1)S(1)}, u32[]{:S(2)}, u32[]{:S(2)}) collective-permute-start(bf16[128,2560]{1,0:T(8,128)(2,1)S(1)} %get-tuple-element.63), channel_id=1, source_target_pairs={{0,144},{1,145},{2,146},{3,147},{4,148},{5,149},{6,150},{7,151},{8... | collective-permute-start | bytes 1966088 | tf_op jit(solution)/shard_map/ppermute | solution.py:416
  85.9 10.3 %collective-permute-start.25 = (bf16[2,64,1280]{2,1,0:T(8,128)(2,1)S(1)}, bf16[2,64,1280]{2,1,0:T(8,128)(2,1)S(1)}, u32[]{:S(2)}, u32[]{:S(2)}) collective-permute-start(bf16[2,64,1280]{2,1,0:T(8,128)(2,1)S(1)} %get-tuple-element.77), channel_id=1, source_target_pairs={{0,32},{1,33},{2,34},{3,35},{4,36},{5,37},{6,38},{7,39},{8,16},{9,... | collective-permute-start | bytes 983048 | tf_op jit(solution)/shard_map/ppermute | solution.py:416
  87.7 17.2 %collective-permute-start.20 = (bf16[2,64,1280]{2,1,0:T(8,128)(2,1)S(1)}, bf16[2,64,1280]{2,1,0:T(8,128)(2,1)S(1)}, u32[]{:S(2)}, u32[]{:S(2)}) collective-permute-start(bf16[2,64,1280]{2,1,0:T(8,128)(2,1)S(1)} %get-tuple-element.67), channel_id=1, source_target_pairs={{0,32},{1,33},{2,34},{3,35},{4,36},{5,37},{6,38},{7,39},{8,16},{9,... | collective-permute-start | bytes 983048 | tf_op jit(solution)/shard_map/ppermute | solution.py:416
  92.7 11.1 %collective-permute-start.28 = (bf16[2,64,1280]{2,1,0:T(8,128)(2,1)S(1)}, bf16[2,64,1280]{2,1,0:T(8,128)(2,1)S(1)}, u32[]{:S(2)}, u32[]{:S(2)}) collective-permute-start(bf16[2,64,1280]{2,1,0:T(8,128)(2,1)S(1)} %get-tuple-element.81), channel_id=1, source_target_pairs={{0,1},{1,2},{2,3},{3,4},{4,5},{5,6},{6,7},{7,0},{8,9},{9,10},{10,1... | collective-permute-start | bytes 983048 | tf_op jit(solution)/shard_map/ppermute | solution.py:416
  92.8 11.0 %collective-permute-start.29 = (bf16[2,64,1280]{2,1,0:T(8,128)(2,1)S(1)}, bf16[2,64,1280]{2,1,0:T(8,128)(2,1)S(1)}, u32[]{:S(2)}, u32[]{:S(2)}) collective-permute-start(bf16[2,64,1280]{2,1,0:T(8,128)(2,1)S(1)} %get-tuple-element.82), channel_id=1, source_target_pairs={{0,7},{1,0},{2,1},{3,2},{4,3},{5,4},{6,5},{7,6},{8,15},{9,8},{10,9... | collective-permute-start | bytes 983048 | tf_op jit(solution)/shard_map/ppermute | solution.py:416
  96.3 13.5 %collective-permute-start.23 = (bf16[2,64,1280]{2,1,0:T(8,128)(2,1)S(1)}, bf16[2,64,1280]{2,1,0:T(8,128)(2,1)S(1)}, u32[]{:S(2)}, u32[]{:S(2)}) collective-permute-start(bf16[2,64,1280]{2,1,0:T(8,128)(2,1)S(1)} %get-tuple-element.71), channel_id=1, source_target_pairs={{0,1},{1,2},{2,3},{3,4},{4,5},{5,6},{6,7},{7,0},{8,9},{9,10},{10,1... | collective-permute-start | bytes 983048 | tf_op jit(solution)/shard_map/ppermute | solution.py:416
  (11 other events, 138.9 us)
